TPU v7x, 32 devices: a whole 2x2x4 slice. The times are simulated.
32 devices in a mesh: row: 2 (over core), col: 16 (over z, y, x).
Axes of the slice: x: 2, y: 2, z: 4, core: 2. Of those that a mesh axis runs over, the one named last changes fastest.
Arguments:
- source_bytes: int32 [2, 2048], P('row', 'col'), may hold values from 0 to 383
- decoder_bytes: int32 [2, 2048], P('row', 'col'), may hold values from 0 to 383
- target_bytes: int32 [2, 2048], P('row', 'col'), may hold values from 0 to 383
- target_keep: int32 [2, 2048], P('row', 'col'), may hold values 0 or 1
- source_length: int32 [2], P('row'), may hold values from 1024 to 2048, as said below
- target_length: int32 [2], P('row'), may hold values from 1024 to 2048, as said below
- language: int32 [2], P('row'), may hold values from 0 to 3, as said below
- step_count: int32 [1], replicated, may hold values from 2 to 20
- attn_weights: float32 [3, 4, 1472, 384], P(None, None, 'row', 'col')
- attn_first: float32 [3, 4, 1472, 384], P(None, None, 'row', 'col'), may hold values from -2.3841858e-06 to 2.3841858e-06
- attn_second: float32 [3, 4, 1472, 384], P(None, None, 'row', 'col'), may hold values from 1.2633388e-15 to 2.0213421e-14
- feed_weights: float32 [2, 3, 16, 329728], P(None, None, 'col', 'row'), may hold values from -0.15625 to 0.15625
- feed_first: float32 [2, 3, 16, 329728], P(None, None, 'col', 'row'), may hold values from -2.3841858e-06 to 2.3841858e-06
- feed_second: float32 [2, 3, 16, 329728], P(None, None, 'col', 'row'), may hold values from 1.2633388e-15 to 2.0213421e-14
- table_weights: float32 [2, 1472, 384], P(None, 'row', 'col')
- table_first: float32 [2, 1472, 384], P(None, 'row', 'col'), may hold values from -2.3841858e-06 to 2.3841858e-06
- table_second: float32 [2, 1472, 384], P(None, 'row', 'col'), may hold values from 1.2633388e-15 to 2.0213421e-14
- norm_gain_stack: float32 [7, 1472], replicated, may hold values from 0.5 to 1.5
- gain_first: float32 [7, 1472], replicated, may hold values from -1.335144e-05 to 1.335144e-05
- gain_second: float32 [7, 1472], replicated, may hold values from 3.158347e-14 to 5.053355e-13
Outputs:
- loss: float32 [], replicated
- grad_norm: float32 [], replicated
- first_attn: float32 [3, 4, 1472, 384], P(None, None, 'row', 'col')
- second_attn: float32 [3, 4, 1472, 384], P(None, None, 'row', 'col')
- master_attn: float32 [3, 4, 1472, 384], P(None, None, 'row', 'col')
- first_feed: float32 [2, 3, 16, 329728], P(None, None, 'col', 'row')
- second_feed: float32 [2, 3, 16, 329728], P(None, None, 'col', 'row')
- master_feed: float32 [2, 3, 16, 329728], P(None, None, 'col', 'row')
- first_table: float32 [2, 1472, 384], P(None, 'row', 'col')
- second_table: float32 [2, 1472, 384], P(None, 'row', 'col')
- master_table: float32 [2, 1472, 384], P(None, 'row', 'col')
- first_gain: float32 [7, 1472], replicated
- second_gain: float32 [7, 1472], replicated
- master_gain: float32 [7, 1472], replicated
Inputs may be any that keep to these rules, and one draw needn't show every extreme that they name: `source_length`: one sequence, which one drawn from the seed, fills all 2048 slots; the others hold 1024 or more. `target_length`: one sequence, which one drawn from the seed, fills all 2048 slots; the others hold 1024 or more. `language`: neighbouring sequences belong to different groups; with 4 or more sequences every group occurs.
All inputs are finite; a program needn't handle non-finite values. No bound on the sum of `target_keep` on one device may be relied on, other than what follows from the above.
Results may differ from a plain program's by a relative error of at most 0.012.
The roundings to bfloat16 on the way count: a program that leaves them out, or rounds other values in their place, can miss the bound.
Values may be sent and summed in bfloat16 or wider, within the bound.
No kernel may reach another device: no remote copies, remote signals or barrier semaphores. Data moves between devices by JAX's collectives and lax.ppermute only.
A program may use at most 384 MiB of HBM per device.

v0:
```python
import jax
import jax.numpy as jnp
from jax import lax
from jax.sharding import PartitionSpec as P

D = 1472
HEADS = 6
HEAD_DIM = 64
NLANG = 4
INNER = 384


RMS_EPS = 1e-06
CLIP_NORM = 0.01
BETA_FIRST = 0.9
BETA_SECOND = 0.999
ADAM_EPS = 1e-08
MATRIX_RATE = 0.05
GAIN_RATE = 0.2
DECAY_STEP = 0.005
MASKED = -1000000000.0
PRECISE = lax.Precision.HIGHEST
ROWS_DIMS = (((0,), (0,)), ((), ()))
COLS_DIMS = (((1,), (1,)), ((), ()))


def contract_rows(left, right):
    return lax.dot_general(left, right, ROWS_DIMS, preferred_element_type=jnp.float32)


def contract_columns_helper(left, right):
    return lax.dot_general(left, right, COLS_DIMS, preferred_element_type=jnp.float32)


def matmul(left, right):
    return jnp.dot(left, right, preferred_element_type=jnp.float32)


def split_heads(matrix):
    return matrix.reshape(matrix.shape[0], HEADS, HEAD_DIM)


def rms_forward(stream, gain):
    scale = lax.rsqrt(jnp.mean(stream * stream, axis=-1, keepdims=True) + RMS_EPS)
    return ((stream * scale * gain).astype(jnp.bfloat16), scale)


def root_mean_norm_reverse(stream, gain, scale, grad_out):
    weighted = grad_out * gain
    inner_mean = jnp.mean(weighted * stream, axis=-1, keepdims=True)
    grad_in = scale * weighted - stream * (scale * scale * scale) * inner_mean
    grad_gain = jnp.sum(grad_out * stream * scale, axis=0)
    return (grad_in, grad_gain)


def pack_tiles(full, rows_n, cols_n):
    depth, width, height = full.shape
    split = full.reshape(depth, rows_n, width // rows_n, cols_n, height // cols_n)
    return split.transpose(0, 1, 3, 2, 4).reshape(
        depth, rows_n * cols_n, width // rows_n, height // cols_n
    )


def unpack_tiles(pieces, rows_n, cols_n):
    depth, total, part_w, part_h = pieces.shape
    split = pieces.reshape(depth, rows_n, cols_n, part_w, part_h)
    return split.transpose(0, 1, 3, 2, 4).reshape(depth, rows_n * part_w, cols_n * part_h)


def gather_keys(own_kv):
    return lax.all_gather(own_kv, "col", axis=0, tiled=True)


def gather_tokens(normed):
    return lax.all_gather(normed, "col", axis=0, tiled=True)


def own_keys_values(normed_kv, weight_bundle):
    return jnp.concatenate(
        [matmul(normed_kv, weight_bundle[1]), matmul(normed_kv, weight_bundle[2])], 1
    ).astype(jnp.bfloat16)


def attention_scores(queries, keys, key_limit, causal, query_first):
    scores = jnp.einsum(
        "qhd,khd->hqk", split_heads(queries), split_heads(keys), preferred_element_type=jnp.float32
    ) * HEAD_DIM ** (-0.5)
    key_pos = jnp.arange(keys.shape[0], dtype=jnp.int32)
    query_pos = query_first + jnp.arange(queries.shape[0], dtype=jnp.int32)
    allowed = jnp.broadcast_to(key_pos[None, :] < key_limit, (queries.shape[0], keys.shape[0]))
    if causal:
        allowed = allowed & (key_pos[None, :] <= query_pos[:, None])
    return jnp.where(allowed[None], scores, MASKED)


def attention_probs(queries, kv_all, key_limit, causal, first_pos):
    scores = attention_scores(queries, kv_all[:, : queries.shape[1]], key_limit, causal, first_pos)
    peak = jnp.max(scores, axis=-1, keepdims=True)
    raised = jnp.exp(scores - peak)
    total = jnp.sum(raised, axis=-1, keepdims=True)
    return (raised / total, peak[..., 0] + jnp.log(total[..., 0]))


def attend_forward(normed_q, normed_kv, weight_bundle, key_limit, causal, first_pos):
    width = weight_bundle.shape[2]
    queries = matmul(normed_q, weight_bundle[0]).astype(jnp.bfloat16)
    kv_all = gather_keys(own_keys_values(normed_kv, weight_bundle))
    probs, _ = attention_probs(queries, kv_all, key_limit, causal, first_pos)
    context = jnp.einsum(
        "hqk,khd->qhd",
        probs.astype(jnp.bfloat16),
        split_heads(kv_all[:, width:]),
        preferred_element_type=jnp.float32,
    )
    context = context.reshape(queries.shape[0], width).astype(jnp.bfloat16)
    return (contract_columns_helper(context, weight_bundle[3]), kv_all)


def attention_reverse_pass(
    normed_q, normed_kv, weight_bundle, key_limit, causal, first_pos, grad_branch
):
    width = weight_bundle.shape[2]
    count = normed_q.shape[0]
    queries = matmul(normed_q, weight_bundle[0]).astype(jnp.bfloat16)
    kv_all = gather_keys(own_keys_values(normed_kv, weight_bundle))
    probs, lse = attention_probs(queries, kv_all, key_limit, causal, first_pos)
    probs_b = probs.astype(jnp.bfloat16)
    keys_h = split_heads(kv_all[:, :width])
    values_h = split_heads(kv_all[:, width:])
    context = (
        jnp.einsum("hqk,khd->qhd", probs_b, values_h, preferred_element_type=jnp.float32)
        .reshape(count, width)
        .astype(jnp.bfloat16)
    )
    grad_b = grad_branch.astype(jnp.bfloat16)
    grad_out_w = contract_rows(grad_b, context)
    grad_context_flat = matmul(grad_b, weight_bundle[3]).astype(jnp.bfloat16)
    grad_context = split_heads(grad_context_flat)
    grad_probs = jnp.einsum(
        "qhd,khd->hqk", grad_context, values_h, preferred_element_type=jnp.float32
    )
    inner_sum = jnp.sum(probs * grad_probs, axis=-1)
    grad_scores = (probs * (grad_probs - inner_sum[:, :, None])).astype(jnp.bfloat16)
    grad_queries = jnp.einsum(
        "hqk,khd->qhd", grad_scores, keys_h, preferred_element_type=jnp.float32
    ) * HEAD_DIM ** (-0.5)
    grad_queries = grad_queries.reshape(count, width).astype(jnp.bfloat16)
    query_h = split_heads(queries)
    grad_keys = jnp.einsum(
        "hqk,qhd->khd", grad_scores, query_h, preferred_element_type=jnp.float32
    ) * HEAD_DIM ** (-0.5)
    grad_values = jnp.einsum(
        "hqk,qhd->khd", probs_b, grad_context, preferred_element_type=jnp.float32
    )
    grad_kv = lax.psum_scatter(
        jnp.concatenate(
            [
                grad_keys.reshape(lax.axis_size("col") * count, width),
                grad_values.reshape(lax.axis_size("col") * count, width),
            ],
            1,
        ).astype(jnp.bfloat16),
        "col",
        scatter_dimension=0,
        tiled=True,
    )
    local_key_gradient = grad_kv[:, :width]
    local_value_gradient = grad_kv[:, width:]
    weight_gradient_total = jnp.stack(
        [
            contract_rows(normed_q, grad_queries),
            contract_rows(normed_kv, local_key_gradient),
            contract_rows(normed_kv, local_value_gradient),
            grad_out_w,
        ]
    )
    normed_query_gradient = contract_columns_helper(grad_queries, weight_bundle[0])
    normed_keyvalue_gradient = contract_columns_helper(
        local_key_gradient, weight_bundle[1]
    ) + contract_columns_helper(local_value_gradient, weight_bundle[2])
    return (normed_query_gradient, normed_keyvalue_gradient, weight_gradient_total)


def gated_units(gate, upper):
    return jax.nn.gelu(gate, approximate=True) * upper


def feed_forward(normed, weight_bundle):
    normed_all = gather_tokens(normed)
    hidden = gated_units(
        matmul(normed_all, weight_bundle[0]), matmul(normed_all, weight_bundle[1])
    ).astype(jnp.bfloat16)
    return (
        lax.psum_scatter(
            contract_columns_helper(hidden, weight_bundle[2]).astype(jnp.bfloat16),
            "col",
            scatter_dimension=0,
            tiled=True,
        ).astype(jnp.float32),
        normed_all,
    )


def feed_backward(normed, weight_bundle, grad_branch):
    normed_all = gather_tokens(normed)
    activation, pull = jax.vjp(
        gated_units, matmul(normed_all, weight_bundle[0]), matmul(normed_all, weight_bundle[1])
    )
    hidden = activation.astype(jnp.bfloat16)
    grad_all = lax.all_gather(grad_branch.astype(jnp.bfloat16), "col", axis=0, tiled=True)
    grad_down = contract_rows(grad_all, hidden)
    grad_gate, grad_upper = pull(matmul(grad_all, weight_bundle[2]))
    gate_b = grad_gate.astype(jnp.bfloat16)
    upper_b = grad_upper.astype(jnp.bfloat16)
    grad_normed = lax.psum_scatter(
        (
            contract_columns_helper(gate_b, weight_bundle[0])
            + contract_columns_helper(upper_b, weight_bundle[1])
        ).astype(jnp.bfloat16),
        "col",
        scatter_dimension=0,
        tiled=True,
    ).astype(jnp.float32)
    return (
        grad_normed,
        jnp.stack(
            [contract_rows(normed_all, gate_b), contract_rows(normed_all, upper_b), grad_down]
        ),
    )


def adam(weight_bundle, first, second, grad, clip, count, rate, decay_step):
    clipped = grad * clip
    first_new = BETA_FIRST * first + (1.0 - BETA_FIRST) * clipped
    second_new = BETA_SECOND * second + (1.0 - BETA_SECOND) * clipped * clipped
    fixed_first = first_new / (1.0 - BETA_FIRST**count)
    fixed_second = second_new / (1.0 - BETA_SECOND**count)
    master = (
        weight_bundle
        - rate * (fixed_first / (jnp.sqrt(fixed_second) + ADAM_EPS))
        - decay_step * weight_bundle
    )
    return (first_new, second_new, master)


def local(
    source_bytes,
    decoder_bytes,
    target_bytes,
    target_keep,
    source_length,
    target_length,
    language,
    step_count,
    attn_weights,
    attn_first,
    attn_second,
    feed_weights,
    feed_first,
    feed_second,
    table_weights,
    table_first,
    table_second,
    norm_gain_stack,
    gain_first,
    gain_second,
):
    rows_n = lax.axis_size("row")
    cols_n = lax.axis_size("col")
    local_rows = source_bytes.shape[1]
    first_pos = lax.axis_index("col") * local_rows
    positions = first_pos + jnp.arange(local_rows, dtype=jnp.int32)
    src_limit = source_length[0]
    tgt_limit = target_length[0]
    weight = ((positions < tgt_limit) & (target_keep[0] > 0)).astype(jnp.float32)
    member = (language[0] == jnp.arange(NLANG, dtype=jnp.int32)).astype(jnp.float32)
    counts = lax.psum(member * jnp.sum(weight), ("row", "col"))
    inverse = 1.0 / (NLANG * jnp.maximum(counts, 1.0))
    token_scale = weight * jnp.sum(member * inverse)
    width = attn_weights.shape[3]
    tiles = jnp.concatenate(
        [attn_weights.reshape(12, attn_weights.shape[2], width), table_weights], 0
    ).astype(jnp.bfloat16)
    full = unpack_tiles(
        lax.all_gather(tiles[:, None], ("row", "col"), axis=1, tiled=True), rows_n, cols_n
    )
    model_width = full.shape[1]
    attn_b = full[:12].reshape(3, 4, model_width, full.shape[2])
    table_b = full[12:]
    feed_flat = lax.all_gather(feed_weights.astype(jnp.bfloat16), "row", axis=3, tiled=True)
    feed_b = feed_flat.reshape(2, 3, model_width, feed_flat.shape[3] // model_width)
    vocab_ids = jnp.arange(table_b.shape[2], dtype=jnp.int32)
    src_hot = (source_bytes[0][:, None] == vocab_ids).astype(jnp.bfloat16)
    dec_hot = (decoder_bytes[0][:, None] == vocab_ids).astype(jnp.bfloat16)
    encoder_layer_zero = contract_columns_helper(src_hot, table_b[0])
    decoder_layer_zero = contract_columns_helper(dec_hot, table_b[0])
    normed_zero, _ = rms_forward(encoder_layer_zero, norm_gain_stack[0])
    branch, kept_enc_self = attend_forward(
        normed_zero, normed_zero, attn_b[0], src_limit, False, first_pos
    )
    enc_one = encoder_layer_zero + branch
    normed_one, _ = rms_forward(enc_one, norm_gain_stack[1])
    branch, kept_enc_feed = feed_forward(normed_one, feed_b[0])
    enc_two = enc_one + branch
    memory, memory_scale = rms_forward(enc_two, norm_gain_stack[2])
    normed_three, _ = rms_forward(decoder_layer_zero, norm_gain_stack[3])
    branch, kept_dec_self = attend_forward(
        normed_three, normed_three, attn_b[1], tgt_limit, True, first_pos
    )
    dec_one = decoder_layer_zero + branch
    normed_four, _ = rms_forward(dec_one, norm_gain_stack[4])
    branch, kept_cross = attend_forward(normed_four, memory, attn_b[2], src_limit, False, first_pos)
    dec_two = dec_one + branch
    normed_five, _ = rms_forward(dec_two, norm_gain_stack[5])
    branch, kept_dec_feed = feed_forward(normed_five, feed_b[1])
    dec_three = dec_two + branch
    final, final_scale = rms_forward(dec_three, norm_gain_stack[6])
    logits = matmul(final, table_b[1])
    lse = jax.nn.logsumexp(logits, axis=-1)
    target_hot = (target_bytes[0][:, None] == vocab_ids).astype(jnp.float32)
    picked = jnp.sum(logits * target_hot, axis=-1)
    loss_local = jnp.sum((lse - picked) * weight) * member
    grad_logits = ((jnp.exp(logits - lse[:, None]) - target_hot) * token_scale[:, None]).astype(
        jnp.bfloat16
    )
    head_grad = contract_rows(final, grad_logits)
    grad_final = contract_columns_helper(grad_logits, table_b[1])
    grad_dec, gain_six = root_mean_norm_reverse(
        dec_three, norm_gain_stack[6], final_scale, grad_final
    )
    normed_five, scale_five = rms_forward(dec_two, norm_gain_stack[5])
    grad_normed, feed_dec_grad = feed_backward(normed_five, feed_b[1], grad_dec)
    part, gain_five = root_mean_norm_reverse(dec_two, norm_gain_stack[5], scale_five, grad_normed)
    grad_dec = grad_dec + part
    normed_four, scale_four = rms_forward(dec_one, norm_gain_stack[4])
    normed_query_gradient, grad_memory, cross_grad = attention_reverse_pass(
        normed_four, memory, attn_b[2], src_limit, False, first_pos, grad_dec
    )
    part, gain_four = root_mean_norm_reverse(
        dec_one, norm_gain_stack[4], scale_four, normed_query_gradient
    )
    grad_dec = grad_dec + part
    normed_three, norm_scale_third = rms_forward(decoder_layer_zero, norm_gain_stack[3])
    normed_query_gradient, normed_keyvalue_gradient, decoder_self_gradient = attention_reverse_pass(
        normed_three, normed_three, attn_b[1], tgt_limit, True, first_pos, grad_dec
    )
    part, norm_gain_third = root_mean_norm_reverse(
        decoder_layer_zero,
        norm_gain_stack[3],
        norm_scale_third,
        normed_query_gradient + normed_keyvalue_gradient,
    )
    grad_dec = grad_dec + part
    grad_enc, gain_two = root_mean_norm_reverse(
        enc_two, norm_gain_stack[2], memory_scale, grad_memory
    )
    normed_one, scale_one = rms_forward(enc_one, norm_gain_stack[1])
    grad_normed, feed_enc_grad = feed_backward(normed_one, feed_b[0], grad_enc)
    part, gain_one = root_mean_norm_reverse(enc_one, norm_gain_stack[1], scale_one, grad_normed)
    grad_enc = grad_enc + part
    normed_zero, norm_scale_initial = rms_forward(encoder_layer_zero, norm_gain_stack[0])
    normed_query_gradient, normed_keyvalue_gradient, encoder_self_gradient = attention_reverse_pass(
        normed_zero, normed_zero, attn_b[0], src_limit, False, first_pos, grad_enc
    )
    part, norm_gain_initial = root_mean_norm_reverse(
        encoder_layer_zero,
        norm_gain_stack[0],
        norm_scale_initial,
        normed_query_gradient + normed_keyvalue_gradient,
    )
    grad_enc = grad_enc + part
    embed_grad = lax.dot_general(
        grad_enc,
        src_hot.astype(jnp.float32),
        ROWS_DIMS,
        precision=PRECISE,
        preferred_element_type=jnp.float32,
    )
    embed_grad = embed_grad + lax.dot_general(
        grad_dec,
        dec_hot.astype(jnp.float32),
        ROWS_DIMS,
        precision=PRECISE,
        preferred_element_type=jnp.float32,
    )
    attn_grad = jnp.stack([encoder_self_gradient, decoder_self_gradient, cross_grad]).reshape(
        12, model_width, full.shape[2]
    )
    grad_tiles = pack_tiles(
        jnp.concatenate([attn_grad, jnp.stack([embed_grad, head_grad])], 0), rows_n, cols_n
    )
    reduced = lax.psum_scatter(grad_tiles, ("row", "col"), scatter_dimension=1, tiled=True)[:, 0]
    attn_red = reduced[:12].reshape(attn_weights.shape)
    table_red = reduced[12:]
    feed_local = jnp.stack([feed_enc_grad, feed_dec_grad]).reshape(2, 3, 1, feed_flat.shape[3])
    feed_red = lax.psum_scatter(
        feed_local.astype(jnp.bfloat16), "row", scatter_dimension=3, tiled=True
    ).astype(jnp.float32)
    gain_local = jnp.stack(
        [norm_gain_initial, gain_one, gain_two, norm_gain_third, gain_four, gain_five, gain_six]
    )
    square_local = (
        jnp.sum(attn_red * attn_red) + jnp.sum(table_red * table_red) + jnp.sum(feed_red * feed_red)
    )
    gain_red, square_sum, loss_sums = lax.psum(
        (gain_local, square_local, loss_local), ("row", "col")
    )
    loss = jnp.sum(loss_sums * inverse)
    grad_norm = jnp.sqrt(square_sum + jnp.sum(gain_red * gain_red))
    clip = CLIP_NORM / jnp.maximum(grad_norm, CLIP_NORM)
    count = step_count[0].astype(jnp.float32)
    slot_total = local_rows * cols_n
    attn_rate = jnp.array(
        [MATRIX_RATE, MATRIX_RATE, MATRIX_RATE, (slot_total / (3.0 * INNER)) ** 0.5], jnp.float32
    )[None, :, None, None]
    table_rate = jnp.array([1.0, 1.5 * D ** (-0.5)], jnp.float32)[:, None, None]
    attn_new = adam(
        attn_weights, attn_first, attn_second, attn_red, clip, count, attn_rate, DECAY_STEP
    )
    feed_new = adam(
        feed_weights, feed_first, feed_second, feed_red, clip, count, MATRIX_RATE, DECAY_STEP
    )
    table_new = adam(
        table_weights, table_first, table_second, table_red, clip, count, table_rate, DECAY_STEP
    )
    gain_new = adam(norm_gain_stack, gain_first, gain_second, gain_red, clip, count, GAIN_RATE, 0.0)
    return (
        loss,
        grad_norm,
        attn_new[0],
        attn_new[1],
        attn_new[2],
        feed_new[0],
        feed_new[1],
        feed_new[2],
        table_new[0],
        table_new[1],
        table_new[2],
        gain_new[0],
        gain_new[1],
        gain_new[2],
    )


def solution(mesh):
    in_specs = (
        P("row", "col"),
        P("row", "col"),
        P("row", "col"),
        P("row", "col"),
        P("row"),
        P("row"),
        P("row"),
        P(),
        P(None, None, "row", "col"),
        P(None, None, "row", "col"),
        P(None, None, "row", "col"),
        P(None, None, "col", "row"),
        P(None, None, "col", "row"),
        P(None, None, "col", "row"),
        P(None, "row", "col"),
        P(None, "row", "col"),
        P(None, "row", "col"),
        P(),
        P(),
        P(),
    )
    out_specs = (
        P(),
        P(),
        P(None, None, "row", "col"),
        P(None, None, "row", "col"),
        P(None, None, "row", "col"),
        P(None, None, "col", "row"),
        P(None, None, "col", "row"),
        P(None, None, "col", "row"),
        P(None, "row", "col"),
        P(None, "row", "col"),
        P(None, "row", "col"),
        P(),
        P(),
        P(),
    )
    return jax.shard_map(local, mesh=mesh, in_specs=in_specs, out_specs=out_specs, check_vma=False)
```

profile of v0, /device:TPU:0, one launch (start us, length us, event | category | flops | bytes accessed | tf_op | source)
XLA Modules:
  0.0 2736.9 jit_solution(6010264014936306160)
XLA Ops:
  10.5 117.5 %all-gather.10.cloned.1.call-done = bf16[14,32,736,24]{2,3,1,0:T(8,128)(2,1)} async-done(((bf16[14,1,736,24]{2,3,1,0:T(8,128)(2,1)}), bf16[14,32,736,24]{2,3,1,0:T(8,128)(2,1)}) %all-gather.10.cloned.1.call-update) | async-done | bytes 15826960 | tf_op jit(solution)/shard_map/all_gather | solution.py:285
  128.0 11.2 fusion.145
  164.1 7.6 convert_element_type.259
  186.4 44.1 %all-gather.14.cloned.1.call-done = bf16[2048,768]{1,0:T(8,128)(2,1)} async-done(((bf16[128,768]{1,0:T(8,128)(2,1)}), bf16[2048,768]{1,0:T(8,128)(2,1)}) %all-gather.14.cloned.1.call-update) | async-done | bytes 3145744 | tf_op jit(solution)/shard_map/all_gather | solution.py:71
  239.4 5.0 fusion.150
  244.5 5.6 fusion.47
  252.6 29.6 %slice_reduce_fusion.1 = (bf16[329728]{0:T(1024)(128)(2,1)}, bf16[329728]{0:T(1024)(128)(2,1)}, bf16[329728]{0:T(1024)(128)(2,1)}, bf16[329728]{0:T(1024)(128)(2...) fusion(bf16[2,3,1,329728]{3,2,1,0:T(2,128)(2,1)} %all-gather.18.cloned.1.call-done), kind=kLoop, calls=%fused_computation.118 | loop fusion | bytes 7913472 | tf_op jit(solution)/shard_map/slice | solution.py:191
  286.5 80.4 %all-gather.16.cloned.1.call-done = bf16[2048,1472]{0,1:T(8,128)(2,1)} async-done(((bf16[128,1472]{0,1:T(8,128)(2,1)}), bf16[2048,1472]{0,1:T(8,128)(2,1)}) %all-gather.16.cloned.1.call-update) | async-done | bytes 6029328 | tf_op jit(solution)/shard_map/all_gather | solution.py:75
  379.9 8.6 copy.155
  422.0 110.9 %reduce-scatter.24.cloned.1.call-done = bf16[128,1472]{1,0:T(8,128)(2,1)} async-done(((bf16[2048,1472]{1,0:T(8,128)(2,1)}), bf16[128,1472]{1,0:T(8,128)(2,1)}) %reduce-scatter.24.cloned.1.call-update) | async-done | bytes 376848
  571.3 32.1 %all-gather.12.cloned.1.call-done = bf16[2048,768]{1,0:T(8,128)(2,1)} async-done(((bf16[128,768]{1,0:T(8,128)(2,1)}), bf16[2048,768]{1,0:T(8,128)(2,1)}) %all-gather.12.cloned.1.call-update) | async-done | bytes 3145744 | tf_op jit(solution)/shard_map/all_gather | solution.py:71
  612.8 6.3 fusion.149
  626.1 47.3 %all-gather.20.cloned.1.call-done = bf16[2048,768]{1,0:T(8,128)(2,1)} async-done(((bf16[128,768]{1,0:T(8,128)(2,1)}), bf16[2048,768]{1,0:T(8,128)(2,1)}) %all-gather.20.cloned.1.call-update) | async-done | bytes 3145744 | tf_op jit(solution)/shard_map/all_gather | solution.py:71
  682.4 6.1 fusion.151
  702.0 104.2 %all-gather.22.cloned.1.call-done = bf16[2048,1472]{0,1:T(8,128)(2,1)} async-done(((bf16[128,1472]{0,1:T(8,128)(2,1)}), bf16[2048,1472]{0,1:T(8,128)(2,1)}) %all-gather.22.cloned.1.call-update) | async-done | bytes 6029328 | tf_op jit(solution)/shard_map/all_gather | solution.py:75
  806.2 4.6 fusion.154
  819.5 8.6 copy.157
  836.3 135.8 %reduce-scatter.26.cloned.1.call-done = bf16[128,1472]{1,0:T(8,128)(2,1)} async-done(((bf16[2048,1472]{1,0:T(8,128)(2,1)}), bf16[128,1472]{1,0:T(8,128)(2,1)}) %reduce-scatter.26.cloned.1.call-update) | async-done | bytes 376848
  977.5 40.0 %all-reduce.3 = (f32[4]{0:T(128)S(1)}, f32[4]{0:T(128)S(1)}) all-reduce(f32[4]{0:T(128)S(1)} %get-tuple-element.136, f32[4]{0:T(128)S(1)} %get-tuple-element.137), channel_id=1, replica_groups=mesh['row'=2,'col'=16] {'row','col'}, use_global_device_ids=true, to_apply=%region_21.22 | all-reduce | flops 8 | bytes 64 | tf_op jit(solution)/shard_map/psum | solution.py:277
  1023.7 111.6 %all-gather.24.cloned.1.call-done = bf16[2048,1472]{0,1:T(8,128)(2,1)} async-done(((bf16[128,1472]{0,1:T(8,128)(2,1)}), bf16[2048,1472]{0,1:T(8,128)(2,1)}) %all-gather.24.cloned.1.call-update) | async-done | bytes 6029328 | tf_op jit(solution)/shard_map/all_gather | solution.py:210
  1135.4 6.8 multiply_convert_fusion.7
  1148.3 8.6 copy.159
  1156.9 144.4 %reduce-scatter.28.cloned.1.call-done = bf16[128,1472]{1,0:T(8,128)(2,1)} async-done(((bf16[2048,1472]{1,0:T(8,128)(2,1)}), bf16[128,1472]{1,0:T(8,128)(2,1)}) %reduce-scatter.28.cloned.1.call-update) | async-done | bytes 376848
  1324.2 129.8 %reduce-scatter.30.cloned.1.call-done = bf16[128,768]{1,0:T(8,128)(2,1)} async-done(((bf16[2048,768]{1,0:T(8,128)(2,1)}), bf16[128,768]{1,0:T(8,128)(2,1)}) %reduce-scatter.30.cloned.1.call-update) | async-done | bytes 196624
  1466.1 4.9 multiply_reduce_fusion
  1481.8 89.7 %all-gather.26.cloned.1.call-done = bf16[2048,1472]{0,1:T(8,128)(2,1)} async-done(((bf16[128,1472]{0,1:T(8,128)(2,1)}), bf16[2048,1472]{0,1:T(8,128)(2,1)}) %all-gather.26.cloned.1.call-update) | async-done | bytes 6029328 | tf_op jit(solution)/shard_map/all_gather | solution.py:210
  1571.5 6.6 multiply_convert_fusion.6
  1584.2 8.6 copy.163
  1595.8 4.8 concatenate.76
  1600.7 5.8 convolution_convert_fusion.5
  1610.5 5.8 convolution_convert_fusion.7
  1617.7 5.8 convolution_convert_fusion.6
  1647.8 58.0 %reduce-scatter.36.cloned.1.call-done = bf16[128,768]{1,0:T(8,128)(2,1)} async-done(((bf16[2048,768]{1,0:T(8,128)(2,1)}), bf16[128,768]{1,0:T(8,128)(2,1)}) %reduce-scatter.36.cloned.1.call-update) | async-done | bytes 196624
  1711.6 6.2 maximum_bitcast_fusion.3
  1728.7 4.8 convolution_convert_fusion.10
  1733.8 4.9 convolution_convert_fusion.9
  1744.3 112.2 %reduce-scatter.32.cloned.1.call-done = bf16[128,1472]{1,0:T(8,128)(2,1)} async-done(((bf16[2048,1472]{1,0:T(8,128)(2,1)}), bf16[128,1472]{1,0:T(8,128)(2,1)}) %reduce-scatter.32.cloned.1.call-update) | async-done | bytes 376848
  1876.1 19.7 maximum_maximum_fusion
  1903.5 102.5 %reduce-scatter.34.cloned.1.call-done = bf16[128,768]{1,0:T(8,128)(2,1)} async-done(((bf16[2048,768]{1,0:T(8,128)(2,1)}), bf16[128,768]{1,0:T(8,128)(2,1)}) %reduce-scatter.34.cloned.1.call-update) | async-done | bytes 196624
  2025.7 14.4 pad_maximum_fusion
  2040.2 27.8 %copy.144 = f32[3,4,1472,384]{2,3,1,0:T(8,128)} copy(f32[3,4,1472,384]{3,2,1,0:T(8,128)} %pad_maximum_fusion) | data formatting | bytes 54263808 | tf_op jit(solution)/shard_map/stack | solution.py:386
  2068.0 37.7 %concatenate.74 = f32[12,2,736,16,24]{2,1,4,3,0:T(2,128)} reshape(f32[3,4,1472,384]{2,3,1,0:T(8,128)} %copy.144) | data formatting | bytes 54263808 | tf_op jit(solution)/shard_map/concatenate | solution.py:390
  2105.7 21.6 maximum_bitcast_fusion
  2127.3 25.1 copy.147
  2154.7 10.1 multiply_reduce_fusion.3
  2164.9 480.3 %all-reduce.7.cloned.1.call-done = f32[14,32,736,24]{2,3,1,0:T(8,128)} async-done(((f32[14,32,736,24]{2,3,1,0:T(8,128)}), f32[14,32,736,24]{2,3,1,0:T(8,128)}) %all-reduce.7.cloned.1.call-update) | async-done | bytes 31653904
  2650.7 40.3 %all-reduce.2 = (f32[]{:T(128)}, f32[7,1472]{1,0:T(8,128)S(1)}) all-reduce(f32[]{:T(128)S(6)} %add.294, f32[7,1472]{1,0:T(8,128)S(1)} %stack.147), channel_id=1, replica_groups=mesh['row'=2,'col'=16] {'row','col'}, use_global_device_ids=true, to_apply=%region_44.45 | all-reduce | flops 10305 | bytes 82440 | tf_op jit(solution)/shard_map/psum | solution.py:405
  2698.5 28.4 %multiply_subtract_fusion = (f32[2,3,1,164864]{3,2,1,0:T(1,128)}, f32[2,3,1,164864]{3,2,1,0:T(1,128)}, f32[2,3,1,164864]{3,2,1,0:T(1,128)}) fusion(f32[2,3,1,164864]{3,2,1,0:T(1,128)S(1)} %copy-done.11, f32[]{:T(128)} %bitcast.73, f32[]{:T(128)} %bitcast.72, f32[]{:T(128)S(6)} %div.162, bf16[2,3,1,329728]{3,2,1,0:T(2,128)(2,1)} %all-reduce.9.cloned.1.call-done, ...), kind=kLoop, calls=%fused_computation.31 | loop fusion | flops 16816128 | bytes 25718800 | tf_op jit(solution)/shard_map/sub | solution.py:239
  (587 shorter events, 379.5 us)
Async XLA Ops:
  7.2 120.8 %all-gather.10.cloned.1.call-start = ((), (), s32[]{:S(2)}) async-start(), calls=%async_computation.7 | async-start | bytes 17031168 | tf_op jit(solution)/shard_map/all_gather | solution.py:285
  10.2 220.3 %all-gather.14.cloned.1.call-start = ((), (), s32[]{:S(2)}) async-start(), calls=%async_computation.9 | async-start | bytes 3342336 | tf_op jit(solution)/shard_map/all_gather | solution.py:71
  10.4 151.1 %copy-start.110 = (f32[1472]{0:T(1024)}, f32[1472]{0:T(1024)S(1)}, u32[]{:S(2)}) copy-start(f32[1472]{0:T(1024)S(1)} %get-tuple-element.40) | copy-start | bytes 17668
  10.4 240.9 %copy-start.112 = (f32[1472]{0:T(1024)}, f32[1472]{0:T(1024)S(1)}, u32[]{:S(2)}) copy-start(f32[1472]{0:T(1024)S(1)} %get-tuple-element.39) | copy-start | bytes 17668
  10.4 395.6 %copy-start.107 = (f32[1472]{0:T(1024)}, f32[1472]{0:T(1024)S(1)}, u32[]{:S(2)}) copy-start(f32[1472]{0:T(1024)S(1)} %get-tuple-element.41) | copy-start | bytes 17668
  10.5 1448.4 %copy-start.101 = (f32[1472]{0:T(1024)}, f32[1472]{0:T(1024)S(1)}, u32[]{:S(2)}) copy-start(f32[1472]{0:T(1024)S(1)} %get-tuple-element.38) | copy-start | bytes 17668
  164.1 88.6 %all-gather.18.cloned.1.call-start = ((), (), s32[]{:S(2)}) async-start(), calls=%async_computation.11 | async-start | bytes 11870208 | tf_op jit(solution)/shard_map/all_gather | solution.py:290
  171.7 195.2 %all-gather.16.cloned.1.call-start = ((), (), s32[]{:S(2)}) async-start(), calls=%async_computation.10 | async-start | bytes 6406144 | tf_op jit(solution)/shard_map/all_gather | solution.py:75
  252.4 280.5 %reduce-scatter.24.cloned.1.call-start = ((), (), s32[]{:S(2)}) async-start(), calls=%async_computation.16 | async-start | bytes 6684672
  283.0 91.6 %copy-start.57 = (bf16[1472,224]{1,0:T(8,128)(2,1)}, bf16[1472,224]{1,0:T(8,128)(2,1)S(1)}, u32[]{:S(2)}) copy-start(bf16[1472,224]{1,0:T(8,128)(2,1)S(1)} %squeeze.60) | copy-start | bytes 1978372
  388.5 214.8 %all-gather.12.cloned.1.call-start = ((), (), s32[]{:S(2)}) async-start(), calls=%async_computation.8 | async-start | bytes 3342336 | tf_op jit(solution)/shard_map/all_gather | solution.py:71
  405.4 218.3 %copy-start.2 = (f32[128,1472]{0,1:T(8,128)}, f32[128,1472]{0,1:T(8,128)S(1)}, u32[]{:S(2)}) copy-start(f32[128,1472]{0,1:T(8,128)S(1)} %get-tuple-element.104) | copy-start | bytes 2260996
  406.4 163.0 %copy-start.9 = (bf16[128,1472]{0,1:T(8,128)(2,1)}, bf16[128,1472]{0,1:T(8,128)(2,1)S(1)}, u32[]{:S(2)}) copy-start(bf16[128,1472]{0,1:T(8,128)(2,1)S(1)} %multiply_convert_fusion.16) | copy-start | bytes 1130500
  408.1 265.2 %all-gather.20.cloned.1.call-start = ((), (), s32[]{:S(2)}) async-start(), calls=%async_computation.12 | async-start | bytes 3342336 | tf_op jit(solution)/shard_map/all_gather | solution.py:71
  534.8 924.0 %copy-start.121 = (f32[128]{0:T(128)}, f32[128]{0:T(128)S(1)}, u32[]{:S(2)}) copy-start(f32[128]{0:T(128)S(1)} %get-tuple-element.98) | copy-start | bytes 1540
  538.2 268.0 %all-gather.22.cloned.1.call-start = ((), (), s32[]{:S(2)}) async-start(), calls=%async_computation.13 | async-start | bytes 6406144 | tf_op jit(solution)/shard_map/all_gather | solution.py:75
  695.4 276.8 %reduce-scatter.26.cloned.1.call-start = ((), (), s32[]{:S(2)}) async-start(), calls=%async_computation.17 | async-start | bytes 6684672
  699.2 115.2 %copy-start.59 = (bf16[1472,224]{1,0:T(8,128)(2,1)}, bf16[1472,224]{1,0:T(8,128)(2,1)S(1)}, u32[]{:S(2)}) copy-start(bf16[1472,224]{1,0:T(8,128)(2,1)S(1)} %squeeze.67) | copy-start | bytes 1978372
  828.1 307.3 %all-gather.24.cloned.1.call-start = ((), (), s32[]{:S(2)}) async-start(), calls=%async_computation.14 | async-start | bytes 6406144 | tf_op jit(solution)/shard_map/all_gather | solution.py:210
  1021.7 120.5 %copy-start.144 = (f32[128]{0:T(128)}, f32[128]{0:T(128)S(1)}, u32[]{:S(2)}) copy-start(f32[128]{0:T(128)S(1)} %broadcast_multiply_fusion.6) | copy-start | bytes 1540
  1023.7 277.6 %reduce-scatter.28.cloned.1.call-start = ((), (), s32[]{:S(2)}) async-start(), calls=%async_computation.18 | async-start | bytes 6684672
  1156.9 297.2 %reduce-scatter.30.cloned.1.call-start = ((), (), s32[]{:S(2)}) async-start(), calls=%async_computation.19 | async-start | bytes 3342336
  1324.2 247.3 %all-gather.26.cloned.1.call-start = ((), (), s32[]{:S(2)}) async-start(), calls=%async_computation.15 | async-start | bytes 6406144 | tf_op jit(solution)/shard_map/all_gather | solution.py:210
  1459.9 245.9 %reduce-scatter.36.cloned.1.call-start = ((), (), s32[]{:S(2)}) async-start(), calls=%async_computation.22 | async-start | bytes 3342336
  1465.5 174.0 %copy-start.12 = (f32[128,1472]{0,1:T(8,128)}, f32[128,1472]{0,1:T(8,128)S(1)}, u32[]{:S(2)}) copy-start(f32[128,1472]{0,1:T(8,128)S(1)} %subtract_add_fusion) | copy-start | bytes 2260996
  1481.6 375.0 %reduce-scatter.32.cloned.1.call-start = ((), (), s32[]{:S(2)}) async-start(), calls=%async_computation.20 | async-start | bytes 6684672
  1592.8 413.2 %reduce-scatter.34.cloned.1.call-start = ((), (), s32[]{:S(2)}) async-start(), calls=%async_computation.21 | async-start | bytes 3342336
  1739.0 118.8 %copy-start.113 = (f32[1472]{0:T(1024)S(1)}, f32[1472]{0:T(1024)}, u32[]{:S(2)}) copy-start(f32[1472]{0:T(1024)} %copy-done.112) | copy-start | bytes 17668
  1739.0 118.8 %copy-start.130 = (f32[128]{0:T(128)S(1)}, f32[128]{0:T(128)}, u32[]{:S(2)}) copy-start(f32[128]{0:T(128)} %copy-done.129) | copy-start | bytes 1540
  1741.6 116.7 %copy-start.50 = (f32[128,1472]{0,1:T(8,128)S(1)}, f32[128,1472]{0,1:T(8,128)}, u32[]{:S(2)}) copy-start(f32[128,1472]{0,1:T(8,128)} %copy-done.49) | copy-start | bytes 2260996
  1741.6 116.7 %copy-start.102 = (f32[1472]{0:T(1024)S(1)}, f32[1472]{0:T(1024)}, u32[]{:S(2)}) copy-start(f32[1472]{0:T(1024)} %copy-done.101) | copy-start | bytes 17668
  1741.6 116.7 %copy-start.122 = (f32[128]{0:T(128)S(1)}, f32[128]{0:T(128)}, u32[]{:S(2)}) copy-start(f32[128]{0:T(128)} %copy-done.121) | copy-start | bytes 1540
  1741.7 116.7 %copy-start.138 = (f32[128]{0:T(128)S(1)}, f32[128]{0:T(128)}, u32[]{:S(2)}) copy-start(f32[128]{0:T(128)} %get-tuple-element.97) | copy-start | bytes 1540
  1741.7 116.7 %copy-start.142 = (f32[128]{0:T(128)S(1)}, f32[128]{0:T(128)}, u32[]{:S(2)}) copy-start(f32[128]{0:T(128)} %copy-done.141) | copy-start | bytes 1540
  1741.7 116.7 %copy-start.148 = (f32[128]{0:T(128)S(1)}, f32[128]{0:T(128)}, u32[]{:S(2)}) copy-start(f32[128]{0:T(128)} %get-tuple-element.95) | copy-start | bytes 1540
  1876.0 278.6 %all-reduce.9.cloned.1.call-start = ((), (), s32[]{:S(2)}) async-start(), calls=%async_computation.24 | async-start | bytes 15826944
  1895.8 749.4 %all-reduce.7.cloned.1.call-start = ((), (), s32[]{:S(2)}) async-start(), calls=%async_computation.23 | async-start | bytes 66060288
  1901.1 105.0 %copy-start.26 = (bf16[1472,384]{0,1:T(8,128)(2,1)S(1)}, bf16[1472,384]{0,1:T(8,128)(2,1)}, u32[]{:S(2)}) copy-start(bf16[1472,384]{0,1:T(8,128)(2,1)} %squeeze.53) | copy-start | bytes 3391492
  1901.7 105.8 %copy-start.6 = (f32[128,1472]{0,1:T(8,128)S(1)}, f32[128,1472]{0,1:T(8,128)}, u32[]{:S(2)}) copy-start(f32[128,1472]{0,1:T(8,128)} %copy-done.5) | copy-start | bytes 2260996
  1901.7 105.8 %copy-start.111 = (f32[1472]{0:T(1024)S(1)}, f32[1472]{0:T(1024)}, u32[]{:S(2)}) copy-start(f32[1472]{0:T(1024)} %copy-done.110) | copy-start | bytes 17668
  1901.7 105.8 %copy-start.125 = (f32[128]{0:T(128)S(1)}, f32[128]{0:T(128)}, u32[]{:S(2)}) copy-start(f32[128]{0:T(128)} %copy-done.124) | copy-start | bytes 1540
  2154.6 538.4 %copy-start.104 = (f32[7,1472]{1,0:T(8,128)S(1)}, f32[7,1472]{1,0:T(8,128)}, u32[]{:S(2)}) copy-start(f32[7,1472]{1,0:T(8,128)} %param.39) | copy-start | bytes 123652
  2154.6 538.4 %copy-start.114 = (f32[7,1472]{1,0:T(8,128)S(1)}, f32[7,1472]{1,0:T(8,128)}, u32[]{:S(2)}) copy-start(f32[7,1472]{1,0:T(8,128)} %param.41) | copy-start | bytes 123652
  2154.6 538.4 %copy-start.115 = (f32[7,1472]{1,0:T(8,128)S(1)}, f32[7,1472]{1,0:T(8,128)}, u32[]{:S(2)}) copy-start(f32[7,1472]{1,0:T(8,128)} %param.40) | copy-start | bytes 123652
  2154.7 540.4 %copy-start.85 = (f32[3,4,736,24]{2,3,1,0:T(8,128)S(1)}, f32[3,4,736,24]{2,3,1,0:T(8,128)}, u32[]{:S(2)}) copy-start(f32[3,4,736,24]{2,3,1,0:T(8,128)} %param.32) | copy-start | bytes 2543620
  2154.7 540.4 %copy-start.86 = (f32[3,4,736,24]{2,3,1,0:T(8,128)S(1)}, f32[3,4,736,24]{2,3,1,0:T(8,128)}, u32[]{:S(2)}) copy-start(f32[3,4,736,24]{2,3,1,0:T(8,128)} %param.31) | copy-start | bytes 2543620
  2164.8 530.3 %copy-start.61 = (f32[3,4,736,24]{2,3,1,0:T(8,128)S(1)}, f32[3,4,736,24]{2,3,1,0:T(8,128)}, u32[]{:S(2)}) copy-start(f32[3,4,736,24]{2,3,1,0:T(8,128)} %param.30) | copy-start | bytes 2543620
  2164.8 530.3 %copy-start.152 = (f32[4]{0:T(128)S(1)}, f32[4]{0:T(128)}, u32[]{:S(2)}) copy-start(f32[4]{0:T(128)} %constant.110.clone) | copy-start | bytes 52
  (139 other events, 1186.8 us)
Sparse Core Ops, SparseCore 0:
  11.5 116.3 all-gather.9
  164.2 66.2 all-gather.13
  232.6 17.6 all-gather.17
  253.5 113.3 all-gather.15
  388.6 144.1 reduce-scatter.23
  536.0 67.2 all-gather.11
  606.7 66.6 all-gather.19
  695.5 110.6 all-gather.21
  828.2 143.8 reduce-scatter.25
  1023.8 111.5 all-gather.23
  1157.0 144.2 reduce-scatter.27
  1324.3 129.6 reduce-scatter.29
  1460.0 111.3 all-gather.25
  1576.9 128.9 reduce-scatter.35
  1710.9 145.5 reduce-scatter.31
  1876.1 129.8 reduce-scatter.33
  2008.4 37.2 all-reduce.8
  2152.6 492.6 all-reduce.6
where the time goes:
time: 2750 us; the launch traced here: 2740 us
  waiting for transfers between devices  1900 us (69%)
  local copies, waits for them, and re-layouts  375 us (14%)
  matrix products  201 us (7%)
  other arithmetic  154 us (6%)
  blocking collectives  80.3 us (3%)
    unnamed x27, waiting for transfers between devices  1270 us
    all_gather x2, waiting for transfers between devices, feed_backward(): lax.all_gather(grad_branch.astype(jnp.bfloat16), 'col', axis=0, tiled=True)  201 us
    all_gather x2, waiting for transfers between devices, gather_tokens(): return lax.all_gather(normed, 'col', axis=0, tiled=True)  185 us
    all_gather x3, waiting for transfers between devices, gather_keys(): return lax.all_gather(own_kv, 'col', axis=0, tiled=True)  124 us
    all_gather x1, waiting for transfers between devices, local(): lax.all_gather(tiles[:, None], ('row', 'col'), axis=1, tiled=True)  117 us
    unnamed x350, local copies, waits for them, and re-layouts  72.1 us
  transfers between devices with their start and end apart: 18, of which 16 were waited for; matrix products, arithmetic and copies ran while one was open for 18% of the time, Pallas kernels for 0%

commit v1 on v0

v1 whole, which is shorter than its diff:
```python
import functools

import jax
import jax.numpy as jnp
import numpy as np
from jax import lax
from jax.experimental import pallas as pl
from jax.experimental.pallas import tpu as pltpu
from jax.sharding import Mesh, PartitionSpec as P

D = 1472
HEADS = 6
HEAD_DIM = 64
NLANG = 4
INNER = 384
FF = 3584
LANES = 128
HALF = 768
WIDE = 2 * HALF

RMS_EPS = 1e-06
CLIP_NORM = 0.01
BETA_FIRST = 0.9
BETA_SECOND = 0.999
ADAM_EPS = 1e-08
MATRIX_RATE = 0.05
GAIN_RATE = 0.2
DECAY_STEP = 0.005
MASKED = -1000000000.0
PERIOD = 896
VMEM_LIMIT = 44 * 1024 * 1024
BF = jnp.bfloat16
F32 = jnp.float32


def dot_nn(a, b):
    return lax.dot_general(a, b, (((1,), (0,)), ((), ())), preferred_element_type=F32)


def dot_nt(a, b):
    return lax.dot_general(a, b, (((1,), (1,)), ((), ())), preferred_element_type=F32)


def dot_tn(a, b):
    return lax.dot_general(a, b, (((0,), (0,)), ((), ())), preferred_element_type=F32)


def flat_pieces(hid):
    found = []
    for t in range(PERIOD // LANES):
        at = LANES * t
        while at < LANES * (t + 1):
            j = at // hid
            end = min(LANES * (t + 1), (j + 1) * hid)
            found.append((t, at - LANES * t, j, at - j * hid, end - at))
            at = end
    return found


def unflatten_kernel(hid, groups, flat_ref, spread_ref, out_ref, acc_ref):
    chunks = PERIOD // LANES
    acc_ref[...] = jnp.zeros_like(acc_ref)
    for t in range(chunks):
        rows = flat_ref[0, pl.ds(t, groups, stride=chunks), :].astype(BF)
        for piece_t, lane, j, first, length in flat_pieces(hid):
            if piece_t == t:
                placed = dot_tn(rows, spread_ref[j])
                acc_ref[first : first + length, :] += placed[lane : lane + length, :]
    out_ref[0] = acc_ref[...].astype(BF)


def unflatten(flat, spread, hid, groups):
    count, flat_rows, _ = flat.shape
    lanes = spread.shape[2]
    return pl.pallas_call(
        functools.partial(unflatten_kernel, hid, groups),
        out_shape=jax.ShapeDtypeStruct((count, hid, lanes), BF),
        grid=(count,),
        in_specs=[
            pl.BlockSpec((1, flat_rows, LANES), lambda i: (i, 0, 0)),
            pl.BlockSpec(spread.shape, lambda i: (0, 0, 0)),
        ],
        out_specs=pl.BlockSpec((1, hid, lanes), lambda i: (i, 0, 0)),
        scratch_shapes=[pltpu.VMEM((hid, lanes), F32)],
        compiler_params=pltpu.CompilerParams(vmem_limit_bytes=VMEM_LIMIT),
        name="unflatten",
    )(flat, spread)


def flatten_kernel(hid, groups, grad_ref, spread_ref, out_ref):
    chunks = PERIOD // LANES
    high = grad_ref[0].astype(BF)
    low = (grad_ref[0] - high.astype(F32)).astype(BF)
    for t in range(chunks):
        total = jnp.zeros((groups, LANES), F32)
        for piece_t, lane, j, first, length in flat_pieces(hid):
            if piece_t == t:
                for part in (high, low):
                    rows = part[first : first + length, :]
                    parts = []
                    if lane > 0:
                        parts.append(jnp.zeros((lane, rows.shape[1]), BF))
                    parts.append(rows)
                    if lane + length < LANES:
                        parts.append(jnp.zeros((LANES - lane - length, rows.shape[1]), BF))
                    rows = jnp.concatenate(parts, 0) if len(parts) > 1 else rows
                    total = total + dot_nt(spread_ref[j], rows)
        out_ref[0, pl.ds(t, groups, stride=chunks), :] = total


def flatten(grads, spread, hid, groups):
    count, _, lanes = grads.shape
    flat_rows = groups * PERIOD // LANES
    return pl.pallas_call(
        functools.partial(flatten_kernel, hid, groups),
        out_shape=jax.ShapeDtypeStruct((count, flat_rows, LANES), F32),
        grid=(count,),
        in_specs=[
            pl.BlockSpec((1, hid, lanes), lambda i: (i, 0, 0)),
            pl.BlockSpec(spread.shape, lambda i: (0, 0, 0)),
        ],
        out_specs=pl.BlockSpec((1, flat_rows, LANES), lambda i: (i, 0, 0)),
        compiler_params=pltpu.CompilerParams(vmem_limit_bytes=VMEM_LIMIT),
        name="flatten",
    )(grads, spread)


def head_lanes(shape, h):
    lane = lax.broadcasted_iota(jnp.int32, shape, 1)
    return (lane < HEAD_DIM) if h == 0 else (lane >= HEAD_DIM)


def attend_kernel(causal, where_ref, q_ref, kv0_ref, kv1_ref, kv2_ref, out_ref, pos_ref):
    count = q_ref.shape[0]
    length = kv0_ref.shape[0]
    blocks = length // count
    limit = where_ref[3 * blocks]
    first = where_ref[3 * blocks + 1]
    for p, kv_ref in enumerate((kv0_ref, kv1_ref, kv2_ref)):
        for b in range(blocks):
            pos_ref[:, b * count : (b + 1) * count] = (
                lax.broadcasted_iota(jnp.int32, (8, count), 1) + where_ref[p * blocks + b]
            )
        pos = pos_ref[0:1, :]
        allowed = pos < limit
        if causal:
            query = first + lax.broadcasted_iota(jnp.int32, (count, length), 0)
            allowed = allowed & (pos <= query)
        queries = q_ref[:, p * LANES : (p + 1) * LANES]
        context = []
        for h in range(2):
            own = jnp.where(head_lanes(queries.shape, h), queries, jnp.zeros_like(queries))
            scores = dot_nt(own, kv_ref[:, :LANES]) * HEAD_DIM ** (-0.5)
            scores = jnp.where(allowed, scores, MASKED)
            raised = jnp.exp(scores - jnp.max(scores, axis=1, keepdims=True))
            probs = raised * (1.0 / jnp.sum(raised, axis=1, keepdims=True))
            context.append(dot_nn(probs.astype(BF), kv_ref[:, LANES:]))
        out_ref[:, p * LANES : (p + 1) * LANES] = jnp.where(
            head_lanes(context[0].shape, 0), context[0], context[1]
        ).astype(BF)


def attend(where, queries, kv, causal):
    count = queries.shape[0]
    length = kv[0].shape[0]
    vmem = pl.BlockSpec(memory_space=pltpu.VMEM)
    return pl.pallas_call(
        functools.partial(attend_kernel, causal),
        out_shape=jax.ShapeDtypeStruct((count, INNER), BF),
        in_specs=[pl.BlockSpec(memory_space=pltpu.SMEM)] + [vmem] * 4,
        out_specs=vmem,
        scratch_shapes=[pltpu.VMEM((8, length), jnp.int32)],
        compiler_params=pltpu.CompilerParams(vmem_limit_bytes=VMEM_LIMIT),
        cost_estimate=pl.CostEstimate(
            flops=4 * count * length * INNER * 2,
            transcendentals=HEADS * count * length,
            bytes_accessed=4 * length * INNER,
        ),
        name="attend",
    )(where, queries, *kv)


def attend_back_kernel(
    causal, where_ref, q_ref, g_ref, kv0_ref, kv1_ref, kv2_ref, dq_ref, d0_ref, d1_ref, d2_ref, pos_ref
):
    count = q_ref.shape[0]
    length = kv0_ref.shape[0]
    blocks = length // count
    limit = where_ref[3 * blocks]
    first = where_ref[3 * blocks + 1]
    scale = HEAD_DIM ** (-0.5)
    for p, (kv_ref, d_ref) in enumerate(((kv0_ref, d0_ref), (kv1_ref, d1_ref), (kv2_ref, d2_ref))):
        for b in range(blocks):
            pos_ref[b * count : (b + 1) * count, :] = (
                lax.broadcasted_iota(jnp.int32, (count, count), 0) + where_ref[p * blocks + b]
            )
        pos = pos_ref[...]
        allowed = pos < limit
        if causal:
            query = first + lax.broadcasted_iota(jnp.int32, (length, count), 1)
            allowed = allowed & (pos <= query)
        queries = q_ref[:, p * LANES : (p + 1) * LANES]
        grads = g_ref[:, p * LANES : (p + 1) * LANES]
        d_query, d_key, d_value = [], None, None
        for h in range(2):
            own_q = jnp.where(head_lanes(queries.shape, h), queries, jnp.zeros_like(queries))
            own_g = jnp.where(head_lanes(grads.shape, h), grads, jnp.zeros_like(grads))
            scores = dot_nt(kv_ref[:, :LANES], own_q) * scale
            scores = jnp.where(allowed, scores, MASKED)
            raised = jnp.exp(scores - jnp.max(scores, axis=0, keepdims=True))
            probs = raised * (1.0 / jnp.sum(raised, axis=0, keepdims=True))
            d_probs = dot_nt(kv_ref[:, LANES:], own_g)
            inner = jnp.sum(probs * d_probs, axis=0, keepdims=True)
            d_scores = (probs * (d_probs - inner)).astype(BF)
            d_query.append(dot_tn(d_scores, kv_ref[:, :LANES]) * scale)
            key_part = dot_nn(d_scores, own_q) * scale
            value_part = dot_nn(probs.astype(BF), own_g)
            d_key = key_part if h == 0 else d_key + key_part
            d_value = value_part if h == 0 else d_value + value_part
        dq_ref[:, p * LANES : (p + 1) * LANES] = jnp.where(
            head_lanes(d_query[0].shape, 0), d_query[0], d_query[1]
        ).astype(BF)
        d_ref[:, :LANES] = d_key.astype(BF)
        d_ref[:, LANES:] = d_value.astype(BF)


def attend_back(where, queries, grads, kv, causal):
    count = queries.shape[0]
    length = kv[0].shape[0]
    vmem = pl.BlockSpec(memory_space=pltpu.VMEM)
    part = jax.ShapeDtypeStruct((length, 2 * LANES), BF)
    out = pl.pallas_call(
        functools.partial(attend_back_kernel, causal),
        out_shape=(jax.ShapeDtypeStruct((count, INNER), BF), part, part, part),
        in_specs=[pl.BlockSpec(memory_space=pltpu.SMEM)] + [vmem] * 5,
        out_specs=(vmem,) * 4,
        scratch_shapes=[pltpu.VMEM((length, count), jnp.int32)],
        compiler_params=pltpu.CompilerParams(vmem_limit_bytes=VMEM_LIMIT),
        cost_estimate=pl.CostEstimate(
            flops=10 * count * length * INNER * 2,
            transcendentals=HEADS * count * length,
            bytes_accessed=8 * length * INNER,
        ),
        name="attend_back",
    )(where, queries, grads, *kv)
    return out[0], list(out[1:])


def rms_scale(stream):
    return lax.rsqrt(jnp.sum(stream * stream, axis=-1, keepdims=True) * (1.0 / D) + RMS_EPS)


def rms_reverse(stream, gain, scale, grad_out):
    weighted = grad_out * gain
    inner_mean = jnp.sum(weighted * stream, axis=-1, keepdims=True) * (1.0 / D)
    grad_in = scale * weighted - stream * (scale * scale * scale) * inner_mean
    grad_gain = jnp.sum(grad_out * stream * scale, axis=0)
    return (grad_in, grad_gain)


def gated_units(gate, upper):
    return jax.nn.gelu(gate, approximate=True) * upper


def adam(weight, first, second, grad, clip, count, rate, decay_step):
    clipped = grad * clip
    first_new = BETA_FIRST * first + (1.0 - BETA_FIRST) * clipped
    second_new = BETA_SECOND * second + (1.0 - BETA_SECOND) * clipped * clipped
    fixed_first = first_new / (1.0 - BETA_FIRST**count)
    fixed_second = second_new / (1.0 - BETA_SECOND**count)
    master = (
        weight - rate * (fixed_first / (jnp.sqrt(fixed_second) + ADAM_EPS)) - decay_step * weight
    )
    return (first_new, second_new, master)


class Links:
    def __init__(self, groups):
        self.groups = groups
        self.z_bits = [f"z{i}" for i in range(groups.bit_length() - 1)]
        self.near = self.z_bits[:-1] if len(self.z_bits) > 1 else []

    def swap(self, value, bit):
        if bit[0] == "z":
            step = 1 << int(bit[1:])
            return lax.ppermute(value, "z", [(i, i ^ step) for i in range(self.groups)])
        return lax.ppermute(value, bit, [(0, 1), (1, 0)])

    def swap_by_core(self, value, bits):
        pairs = []
        for c in range(2):
            for y in range(2):
                for x in range(2):
                    to = (y, x ^ 1) if bits[c] == "x" else (y ^ 1, x)
                    pairs.append((c * 4 + y * 2 + x, c * 4 + to[0] * 2 + to[1]))
        return lax.ppermute(value, ("c", "y", "x"), pairs)

    def ring(self, value, step):
        n = self.groups
        return lax.ppermute(value, "z", [(i, (i + step) % n) for i in range(n)])

    def plane_gather(self, own):
        first = self.swap_by_core(own, "xy")
        pair = jnp.concatenate([own, first], 0)
        second = self.swap_by_core(pair, "yx")
        mine = jnp.concatenate([pair, second], 0)
        return jnp.concatenate([mine, self.swap(mine, "c")], 0)

    def plane_scatter(self, parts):
        rows = parts.shape[0] // 8
        total = parts[: 4 * rows] + self.swap(parts[4 * rows :].astype(BF), "c").astype(F32)
        far = self.swap_by_core(total[2 * rows :].astype(BF), "yx").astype(F32)
        total = total[: 2 * rows] + far
        near = self.swap_by_core(total[rows:].astype(BF), "xy").astype(F32)
        return total[:rows] + near

    def orders(self):
        dims = ["x", "y"] + self.near
        return [[dims[(i + p) % len(dims)] for i in range(len(dims))] for p in range(3)]

    def sequence_gather(self, parts):
        out = []
        for part, order in zip(parts, self.orders()):
            for bit in order + ["c"]:
                part = jnp.concatenate([part, self.swap(part, bit)], 0)
            out.append(part)
        return out

    def sequence_scatter(self, parts):
        out = []
        for part, order in zip(parts, self.orders()):
            for bit in ["c"] + order[::-1]:
                rows = part.shape[0] // 2
                part = part[:rows].astype(F32) + self.swap(part[rows:].astype(BF), bit).astype(F32)
            out.append(part)
        return out

    def owner_scatter(self, grads, width):
        dims = self.z_bits[::-1] + ["y", "x"]
        count = grads.shape[0]
        far = [b for b in self.z_bits if b not in self.near]
        out = []
        for p, order in enumerate(self.orders()):
            part = grads[:, :, p * 256 : (p + 1) * 256]
            part = part.reshape([count] + [2] * len(dims) + [width, 256])
            left = list(dims)
            for bit in order + far:
                axis = 1 + left.index(bit)
                left.remove(bit)
                send = lax.index_in_dim(part, 1, axis, keepdims=False).astype(BF)
                keep = lax.index_in_dim(part, 0, axis, keepdims=False).astype(F32)
                part = keep + self.swap(send, bit).astype(F32)
            out.append(part)
        return jnp.concatenate(out, -1)

    def total(self, value, rows_high):
        for bit in ["c", "x", "y"] + self.z_bits:
            value = value + self.swap(value, bit)
        return lax.psum(value, "rh") if rows_high > 1 else value


def step(
    shape,
    source_bytes,
    decoder_bytes,
    target_bytes,
    target_keep,
    source_length,
    target_length,
    language,
    step_count,
    attn_weights,
    attn_first,
    attn_second,
    feed_weights,
    feed_first,
    feed_second,
    table_weights,
    table_first,
    table_second,
    norm_gain_stack,
    gain_first,
    gain_second,
):
    rows_high, groups = shape
    rows_n, cols_n = 2 * rows_high, 4 * groups
    links = Links(groups)
    core, zc, yc, xc = (lax.axis_index(a) for a in ("c", "z", "y", "x"))
    on_first = core == 0
    tokens = source_bytes.shape[1]
    chunk = attn_weights.shape[2]
    width = attn_weights.shape[3]
    everywhere = ("rh", "c", "z", "y", "x")

    def own_half(value):
        return jnp.where(on_first, value[..., :HALF], value[..., HALF:])

    def other_half(value):
        return jnp.where(on_first, value[..., HALF:], value[..., :HALF])

    def in_order(own, other, axis):
        return jnp.concatenate(
            [jnp.where(on_first, own, other), jnp.where(on_first, other, own)], axis
        )

    def widen(value):
        pad = [(0, 0)] * (value.ndim - 1) + [(0, HALF - value.shape[-1])]
        return jnp.pad(value, pad)

    def spread_features(value):
        split = value.reshape(value.shape[0], rows_high, 2, chunk).transpose(0, 2, 1, 3)
        return widen(split.reshape(value.shape[0], 2, D // 2)).reshape(value.shape[0], WIDE)

    def join_features(value):
        split = value.reshape(value.shape[0], 2, HALF)[:, :, : D // 2]
        split = split.reshape(value.shape[0], 2, rows_high, chunk).transpose(0, 2, 1, 3)
        return split.reshape(value.shape[0], D)

    half = groups // 2
    packed = jnp.concatenate(
        [source_bytes, decoder_bytes, target_bytes, target_keep]
        + [
            jnp.broadcast_to(v[:, None], (1, tokens))
            for v in (source_length, target_length, language, language)
        ],
        0,
    )
    pairs = []
    for c in range(2):
        for k in range(cols_n):
            block = (((k // 4) % half) * 4 + k % 4) * 2 + c
            pairs.append(((k // 4 // half) * cols_n + block, c * cols_n + k))
    packed = lax.ppermute(packed, ("c", "z", "y", "x"), pairs)
    block = (((zc % half) * 2 + yc) * 2 + xc) * 2 + core
    first_pos = block * tokens
    src_limit, tgt_limit, tongue = packed[4, 0], packed[5, 0], packed[6, 0]
    positions = first_pos + jnp.arange(tokens, dtype=jnp.int32)
    weight = ((positions < tgt_limit) & (packed[3] > 0)).astype(F32)
    member = (tongue == jnp.arange(LANES, dtype=jnp.int32)).astype(F32)
    counts = links.total(jnp.broadcast_to((member * jnp.sum(weight))[None], (8, LANES)), rows_high)
    inverse = 1.0 / (NLANG * jnp.maximum(counts[0], 1.0))
    token_scale = weight * jnp.sum(member * inverse)

    bit_value = {"c": 1, "x": 2, "y": 4}
    for i, bit in enumerate(links.near):
        bit_value[bit] = 8 << i
    masks = []
    for order in links.orders():
        mask = [0]
        for bit in order + ["c"]:
            mask = mask + [m ^ bit_value[bit] for m in mask]
        masks.append(mask)
    firsts = (jnp.array(np.array(masks).reshape(-1), jnp.int32) ^ block) * tokens

    def places(limit):
        return jnp.concatenate([firsts, jnp.stack([limit, first_pos]).astype(jnp.int32)])

    src_places, tgt_places = places(src_limit), places(tgt_limit)

    attn_t = attn_weights.transpose(0, 1, 3, 2)
    table_t = table_weights.transpose(0, 2, 1)

    def gather_tiles(tiles):
        tiles = tiles.astype(BF)
        if rows_high == 1:
            tiles = widen(tiles)
        full = lax.all_gather(tiles[:, None], everywhere, axis=1, tiled=True)
        if rows_high == 1:
            return full.reshape(tiles.shape[0], 2, INNER, HALF)
        full = full.reshape(tiles.shape[0], rows_high, 2, INNER, chunk).transpose(0, 2, 3, 1, 4)
        return widen(full.reshape(tiles.shape[0], 2, INNER, D // 2))

    early = gather_tiles(jnp.concatenate([attn_t[0], table_t[:1]], 0))
    late = gather_tiles(jnp.concatenate([attn_t[1], attn_t[2], table_t[1:]], 0))
    weights = [early[:4], late[:4], late[4:8]]
    embed_w, head_w = early[4], late[8]

    def project(value, matrix):
        return dot_nt(value[:, :HALF], matrix[0]) + dot_nt(value[:, HALF:], matrix[1])

    def unproject(value, matrix):
        return jnp.concatenate([dot_nn(value, matrix[0]), dot_nn(value, matrix[1])], 1)

    hid = FF // cols_n
    hid_half = hid // 2
    period_rows = PERIOD // hid
    period_groups = chunk // period_rows
    lanes_own = HALF if rows_high == 1 else chunk
    shape3 = (period_rows, period_groups, lanes_own)
    spread = (
        lax.broadcasted_iota(jnp.int32, shape3, 2)
        == lax.broadcasted_iota(jnp.int32, shape3, 1) * period_rows
        + lax.broadcasted_iota(jnp.int32, shape3, 0)
    ).astype(BF)
    flat_shape = (6, chunk * hid // LANES, LANES)
    feed_t = unflatten(feed_weights.reshape(flat_shape), spread, hid, period_groups)
    if rows_high > 1:
        feed_t = lax.all_gather(feed_t[None], "rh", axis=0, tiled=True)
        feed_t = widen(feed_t.transpose(1, 2, 0, 3).reshape(6, hid, D // 2))

    def ring_gather(mine):
        keep = jnp.where(on_first, mine[:, :hid_half], mine[:, hid_half:])
        send = jnp.where(on_first, mine[:, hid_half:], mine[:, :hid_half])
        value = in_order(keep, links.swap(send, "c"), 2)
        held = [value]
        for _ in range(groups - 1):
            held.append(links.ring(held[-1], 1))
        return [jnp.concatenate([h[m] for h in held], 0) for m in range(3)]

    def ring_scatter(grads):
        grads = [g.reshape(groups, hid_half, WIDE) for g in grads]

        def at(s):
            return jnp.stack([g[s] for g in grads])

        value = at(groups - 1)
        for s in range(groups - 2, -1, -1):
            value = at(s).astype(F32) + links.ring(value.astype(BF), -1).astype(F32)
        keep, send = own_half(value), other_half(value)
        full = in_order(keep, links.swap(send.astype(BF), "c").astype(F32), 1)
        if rows_high > 1:
            full = full[:, :, : D // 2].reshape(3, hid, rows_high, chunk)
            full = lax.psum_scatter(full, "rh", scatter_dimension=2, tiled=True)
            full = full.reshape(3, hid, chunk)
        return full

    feed_b = [ring_gather(feed_t[:3]), ring_gather(feed_t[3:])]
    gains = spread_features(norm_gain_stack)

    def norm(stream, index):
        scale = rms_scale(stream)
        return (stream * scale * gains[index]).astype(BF), scale

    def key_value_parts(normed, matrices):
        keys = project(normed, matrices[1]).astype(BF)
        values = project(normed, matrices[2]).astype(BF)
        return [
            jnp.concatenate(
                [keys[:, p * LANES : (p + 1) * LANES], values[:, p * LANES : (p + 1) * LANES]], 1
            )
            for p in range(3)
        ]

    def attention(normed_q, normed_kv, matrices, where, causal):
        queries = project(normed_q, matrices[0]).astype(BF)
        kv = links.sequence_gather(key_value_parts(normed_kv, matrices))
        context = attend(where, queries, kv, causal)
        return unproject(context, matrices[3]), (queries, kv, context)

    def feed(normed, matrices):
        everyone = links.plane_gather(normed)
        gate = dot_nt(everyone, matrices[0])
        upper = dot_nt(everyone, matrices[1])
        hidden = gated_units(gate, upper).astype(BF)
        return links.plane_scatter(dot_nn(hidden, matrices[2])), (everyone, gate, upper, hidden)

    vocab_ids = jnp.arange(INNER, dtype=jnp.int32)
    src_hot = (packed[0][:, None] == vocab_ids).astype(BF)
    dec_hot = (packed[1][:, None] == vocab_ids).astype(BF)
    enc_zero = unproject(src_hot, embed_w)
    dec_zero = unproject(dec_hot, embed_w)
    n_zero, s_zero = norm(enc_zero, 0)
    branch, kept_enc = attention(n_zero, n_zero, weights[0], src_places, False)
    enc_one = enc_zero + branch
    n_one, s_one = norm(enc_one, 1)
    branch, kept_enc_feed = feed(n_one, feed_b[0])
    enc_two = enc_one + branch
    memory, s_two = norm(enc_two, 2)
    n_three, s_three = norm(dec_zero, 3)
    branch, kept_dec = attention(n_three, n_three, weights[1], tgt_places, True)
    dec_one = dec_zero + branch
    n_four, s_four = norm(dec_one, 4)
    branch, kept_cross = attention(n_four, memory, weights[2], src_places, False)
    dec_two = dec_one + branch
    n_five, s_five = norm(dec_two, 5)
    branch, kept_dec_feed = feed(n_five, feed_b[1])
    dec_three = dec_two + branch
    final, s_six = norm(dec_three, 6)

    logits = project(final, head_w)
    lse = jax.nn.logsumexp(logits, axis=-1)
    target_hot = (packed[2][:, None] == vocab_ids).astype(F32)
    picked = jnp.sum(logits * target_hot, axis=-1)
    loss_local = jnp.sum((lse - picked) * token_scale)
    grad_logits = ((jnp.exp(logits - lse[:, None]) - target_hot) * token_scale[:, None]).astype(BF)

    own_index = zc * 4 + yc * 2 + xc
    columns = jnp.arange(INNER, dtype=jnp.int32)
    moved = ((columns // width) ^ own_index) * width + columns % width
    shuffle = (columns[:, None] == moved[None, :]).astype(BF)

    def relative(value):
        return dot_nn(value, shuffle).astype(BF)

    def weight_grads(pairs):
        out = []
        for cols, feats in pairs:
            count = cols.shape[1] // INNER
            send = dot_tn(cols, other_half(feats)).astype(BF).reshape(count, INNER, HALF)
            keep = dot_tn(cols, own_half(feats)).reshape(count, INNER, HALF)
            out.append(keep + links.swap(send, "c").astype(F32))
        return jnp.concatenate(out, 0)

    def feed_back(kept, matrices, grad):
        everyone, gate, upper, hidden = kept
        grad_all = links.plane_gather(grad.astype(BF))
        _, pull = jax.vjp(gated_units, gate, upper)
        grad_gate, grad_upper = pull(dot_nt(grad_all, matrices[2]))
        gate_b, upper_b = grad_gate.astype(BF), grad_upper.astype(BF)
        grad_normed = links.plane_scatter(
            dot_nn(gate_b, matrices[0]) + dot_nn(upper_b, matrices[1])
        )
        grads = [
            dot_tn(gate_b, everyone).astype(BF),
            dot_tn(upper_b, everyone).astype(BF),
            dot_tn(hidden, grad_all).astype(BF),
        ]
        return grad_normed, grads

    def attention_back(kept, normed_q, normed_kv, matrices, where, causal, grad):
        queries, kv, context = kept
        grad_b = grad.astype(BF)
        grad_context = project(grad_b, matrices[3]).astype(BF)
        d_query, d_parts = attend_back(where, queries, grad_context, kv, causal)
        d_parts = [p.astype(BF) for p in links.sequence_scatter(d_parts)]
        d_key = jnp.concatenate([p[:, :LANES] for p in d_parts], 1)
        d_value = jnp.concatenate([p[:, LANES:] for p in d_parts], 1)
        d_normed_q = unproject(d_query, matrices[0])
        d_normed_kv = unproject(d_key, matrices[1]) + unproject(d_value, matrices[2])
        cols = [relative(v) for v in (d_query, d_key, d_value, context)]
        if normed_q is normed_kv:
            grads = weight_grads(
                [(jnp.concatenate(cols[:3], 1), normed_q), (cols[3], grad_b)]
            )
        else:
            grads = weight_grads(
                [(cols[0], normed_q), (jnp.concatenate(cols[1:3], 1), normed_kv), (cols[3], grad_b)]
            )
        return d_normed_q, d_normed_kv, grads

    head_grad = weight_grads([(relative(grad_logits), final)])
    grad_final = unproject(grad_logits, head_w)
    grad_dec, gain_six = rms_reverse(dec_three, gains[6], s_six, grad_final)
    grad_normed, feed_dec_grad = feed_back(kept_dec_feed, feed_b[1], grad_dec)
    part, gain_five = rms_reverse(dec_two, gains[5], s_five, grad_normed)
    grad_dec = grad_dec + part
    d_q, grad_memory, cross_grad = attention_back(
        kept_cross, n_four, memory, weights[2], src_places, False, grad_dec
    )
    part, gain_four = rms_reverse(dec_one, gains[4], s_four, d_q)
    grad_dec = grad_dec + part
    d_q, d_kv, dec_grad = attention_back(
        kept_dec, n_three, n_three, weights[1], tgt_places, True, grad_dec
    )
    part, gain_three = rms_reverse(dec_zero, gains[3], s_three, d_q + d_kv)
    grad_dec = grad_dec + part
    grad_enc, gain_two = rms_reverse(enc_two, gains[2], s_two, grad_memory)
    grad_normed, feed_enc_grad = feed_back(kept_enc_feed, feed_b[0], grad_enc)
    part, gain_one = rms_reverse(enc_one, gains[1], s_one, grad_normed)
    grad_enc = grad_enc + part
    d_q, d_kv, enc_grad = attention_back(
        kept_enc, n_zero, n_zero, weights[0], src_places, False, grad_enc
    )
    part, gain_zero = rms_reverse(enc_zero, gains[0], s_zero, d_q + d_kv)
    grad_enc = grad_enc + part
    hot = jnp.concatenate([relative(src_hot), relative(dec_hot)], 0)
    streams = jnp.concatenate([grad_enc, grad_dec], 0)
    stream_high = streams.astype(BF)
    stream_low = (streams - stream_high.astype(F32)).astype(BF)
    embed_grad = weight_grads(
        [(jnp.concatenate([hot, hot], 0), jnp.concatenate([stream_high, stream_low], 0))]
    )

    late_red = links.owner_scatter(jnp.concatenate([dec_grad, cross_grad, head_grad], 0), width)
    early_red = links.owner_scatter(jnp.concatenate([enc_grad, embed_grad], 0), width)

    def own_chunk(value):
        value = value[:, :, : D // 2]
        if rows_high > 1:
            value = value.reshape(value.shape[0], width, rows_high, chunk)
            value = lax.psum_scatter(value, "rh", scatter_dimension=2, tiled=True)
            value = value.reshape(value.shape[0], width, chunk)
        return value

    late_red, early_red = own_chunk(late_red), own_chunk(early_red)
    attn_red = jnp.stack([early_red[:4], late_red[:4], late_red[4:8]])
    table_red = jnp.stack([early_red[4], late_red[8]])
    feed_red = [
        flatten(ring_scatter(g), spread, hid, period_groups) for g in (feed_enc_grad, feed_dec_grad)
    ]
    feed_red = jnp.stack(feed_red)
    square_local = (
        jnp.sum(attn_red * attn_red) + jnp.sum(table_red * table_red) + jnp.sum(feed_red * feed_red)
    )
    lane = jnp.arange(WIDE)
    extra = jnp.where(lane == 0, square_local, 0.0) + jnp.where(lane == 1, loss_local, 0.0)
    gain_local = jnp.stack(
        [gain_zero, gain_one, gain_two, gain_three, gain_four, gain_five, gain_six, extra]
    )
    everything = links.total(gain_local, rows_high)
    loss = everything[7, 1]
    gain_red = join_features(everything[:7])
    grad_norm = jnp.sqrt(everything[7, 0] + jnp.sum(gain_red * gain_red))
    clip = CLIP_NORM / jnp.maximum(grad_norm, CLIP_NORM)
    count = step_count[0].astype(F32)
    slot_total = tokens * cols_n
    attn_rate = jnp.array(
        [MATRIX_RATE, MATRIX_RATE, MATRIX_RATE, (slot_total / (3.0 * INNER)) ** 0.5], F32
    )[None, :, None, None]
    table_rate = jnp.array([1.0, 1.5 * D ** (-0.5)], F32)[:, None, None]

    def attn_turn(value):
        return value.transpose(0, 1, 3, 2)

    def table_turn(value):
        return value.transpose(0, 2, 1)

    attn_new = adam(
        attn_t, attn_turn(attn_first), attn_turn(attn_second), attn_red, clip, count, attn_rate, DECAY_STEP
    )
    feed_shape = (2, 3) + flat_shape[1:]
    feed_new = adam(
        feed_weights.reshape(feed_shape),
        feed_first.reshape(feed_shape),
        feed_second.reshape(feed_shape),
        feed_red,
        clip,
        count,
        MATRIX_RATE,
        DECAY_STEP,
    )
    table_new = adam(
        table_t, table_turn(table_first), table_turn(table_second), table_red, clip, count, table_rate, DECAY_STEP
    )
    gain_new = adam(norm_gain_stack, gain_first, gain_second, gain_red, clip, count, GAIN_RATE, 0.0)
    return (
        (loss, grad_norm)
        + tuple(attn_turn(v) for v in attn_new)
        + tuple(v.reshape(feed_weights.shape) for v in feed_new)
        + tuple(table_turn(v) for v in table_new)
        + tuple(gain_new)
    )


def solution(mesh):
    rows_high = mesh.shape["row"] // 2
    groups = mesh.shape["col"] // 4
    split = Mesh(mesh.devices.reshape(rows_high, 2, groups, 2, 2), ("rh", "c", "z", "y", "x"))
    row, col = ("rh", "c"), ("z", "y", "x")
    attn = P(None, None, row, col)
    feed = P(None, None, col, row)
    table = P(None, row, col)
    ids = P(row, col)
    in_specs = (ids,) * 4 + (P(row),) * 3 + (P(),) + (attn,) * 3 + (feed,) * 3 + (table,) * 3 + (P(),) * 3
    out_specs = (P(), P()) + (attn,) * 3 + (feed,) * 3 + (table,) * 3 + (P(),) * 3
    return jax.shard_map(
        functools.partial(step, (rows_high, groups)),
        mesh=split,
        in_specs=in_specs,
        out_specs=out_specs,
        check_vma=False,
    )
```

time: 2750 us -> 948 us (0.34)
  waiting for transfers between devices: 1900 us -> 452 us
  local copies, waits for them, and re-layouts: 375 us -> 80.2 us
  starting transfers between devices: 1.52 us -> 150 us
  matrix products: 201 us -> 87.7 us
  blocking collectives: 80.3 us -> 0 us
  other arithmetic: 154 us -> 80.7 us
  Pallas kernels: 0 us -> 60.2 us
    unnamed x27 -> x2, waiting for transfers between devices: 1270 us -> 0.03 us
    all_gather x9 -> x2, waiting for transfers between devices: 627 us -> 51 us  [gather_tiles(): full = lax.all_gather(tiles[:, None], everywhere, axis=1, tiled=True)]
    ppermute x0 -> x156, waiting for transfers between devices: none -> 401 us  [the longest x12 170 us: ring(): return lax.ppermute(value, 'z', [(i, (i + step) % n) for i in range(n)])]
    ppermute x0 -> x156, starting transfers between devices: none -> 149 us  [the longest x93 74.7 us: swap(): return lax.ppermute(value, bit, [(0, 1), (1, 0)])]
    dot_general x76 -> x107, matrix products: 183 us -> 87.7 us  [the longest x24 31.9 us: dot_tn(): lax.dot_general(a, b, (((0,), (0,)), ((), ())), preferred_element_type=F32)]
    slice x26 -> x75, local copies, waits for them, and re-layouts: 112 us -> 25.1 us  [the longest x2 7.65 us: owner_scatter(): part = grads[:, :, p * 256:(p + 1) * 256]]
    psum x2 -> x0, blocking collectives: 80.3 us -> none  [the longest x1 40.3 us: local(): lax.psum((gain_local, square_local, loss_local), ('row', 'col'))]
    squeeze x20 -> x7, local copies, waits for them, and re-layouts: 64.7 us -> 3.56 us  [the longest x6 3.53 us: ring_gather(): return [jnp.concatenate([h[m] for h in held], 0) for m in range(3)]]
  transfers between devices with their start and end apart: 18 -> 158, of which waited for: 16 -> 74; matrix products, arithmetic and copies ran while one was open for 18% -> 17% of each run, Pallas kernels for 0% -> 6%
where the time goes in v1:
time: 948 us; the launch traced here: 938 us
  waiting for transfers between devices  452 us (48%)
  starting transfers between devices  150 us (16%)
  matrix products  87.7 us (9%)
  other arithmetic  80.7 us (9%)
  local copies, waits for them, and re-layouts  80.2 us (8%)
  Pallas kernels  60.2 us (6%)
  between operations  27.8 us (3%)
    ppermute x12, waiting for transfers between devices, ring(): return lax.ppermute(value, 'z', [(i, (i + step) % n) for i in range(n)])  170 us
    ppermute x34, waiting for transfers between devices, swap(): return lax.ppermute(value, 'z', [(i, i ^ step) for i in range(self.groups)])  96.2 us
    ppermute x93, starting transfers between devices, swap(): return lax.ppermute(value, bit, [(0, 1), (1, 0)])  74.7 us
    ppermute x93, waiting for transfers between devices, swap(): return lax.ppermute(value, bit, [(0, 1), (1, 0)])  72 us
    ppermute x16, waiting for transfers between devices, swap_by_core(): return lax.ppermute(value, ('c', 'y', 'x'), pairs)  63 us
    all_gather x2, waiting for transfers between devices, gather_tiles(): full = lax.all_gather(tiles[:, None], everywhere, axis=1, tiled=True)  51 us
    unnamed x588, local copies, waits for them, and re-layouts  35.4 us
    dot_general x24, matrix products, dot_tn(): lax.dot_general(a, b, (((0,), (0,)), ((), ())), preferred_element_type=F32)  31.9 us
  transfers between devices with their start and end apart: 158, of which 74 were waited for; matrix products, arithmetic and copies ran while one was open for 17% of the time, Pallas kernels for 6%

profile of v1, /device:TPU:0, one launch (start us, length us, event | category | flops | bytes accessed | tf_op | source)
XLA Modules:
  0.0 938.3 jit_solution(1679645274603851033)
XLA Ops:
  13.9 4.4 unflatten.1
  23.7 4.9 collective-permute-start.16
  36.2 51.0 %all-gather.5.cloned.1.call-done = bf16[5,768,768]{2,1,0:T(8,128)(2,1)} async-done(((bf16[5,24,768]{2,1,0:T(8,128)(2,1)}), bf16[5,768,768]{2,1,0:T(8,128)(2,1)}) %all-gather.5.cloned.1.call-update) | async-done | bytes 5898256 | tf_op jit(solution)/shard_map/all_gather | solution.py:467
  112.2 4.2 collective-permute-done.3
  120.0 4.8 attend.3
  128.3 6.6 collective-permute-done.13
  136.6 31.1 %collective-permute-done.18 = bf16[3,112,1536]{2,1,0:T(8,128)(2,1)S(1)} collective-permute-done((bf16[3,112,1536]{2,1,0:T(8,128)(2,1)}, bf16[3,112,1536]{2,1,0:T(8,128)(2,1)S(1)}, u32[]{:S(2)}, u32[]{:S(2)}) %collective-permute-start.18) | collective-permute-done | bytes 1032224 | tf_op jit(solution)/shard_map/ppermute | solution.py:300
  167.6 5.1 collective-permute-start.19
  174.9 36.0 %collective-permute-done.19 = bf16[3,112,1536]{2,1,0:T(8,128)(2,1)S(1)} collective-permute-done((bf16[3,112,1536]{2,1,0:T(8,128)(2,1)S(1)}, bf16[3,112,1536]{2,1,0:T(8,128)(2,1)S(1)}, u32[]{:S(2)}, u32[]{:S(2)}) %collective-permute-start.19) | collective-permute-done | bytes 1032224 | tf_op jit(solution)/shard_map/ppermute | solution.py:300
  233.4 6.9 collective-permute-done.21
  242.1 6.3 collective-permute-done.22
  250.4 5.9 fusion.347
  292.5 5.2 attend.4
  300.2 5.0 attend.5
  309.3 5.6 collective-permute-done.47
  315.8 19.0 %collective-permute-done.52 = bf16[3,112,1536]{2,1,0:T(8,128)(2,1)S(1)} collective-permute-done((bf16[3,112,1536]{2,1,0:T(8,128)(2,1)}, bf16[3,112,1536]{2,1,0:T(8,128)(2,1)S(1)}, u32[]{:S(2)}, u32[]{:S(2)}) %collective-permute-start.52) | collective-permute-done | bytes 1032224 | tf_op jit(solution)/shard_map/ppermute | solution.py:300
  336.9 23.7 %collective-permute-done.53 = bf16[3,112,1536]{2,1,0:T(8,128)(2,1)S(1)} collective-permute-done((bf16[3,112,1536]{2,1,0:T(8,128)(2,1)S(1)}, bf16[3,112,1536]{2,1,0:T(8,128)(2,1)S(1)}, u32[]{:S(2)}, u32[]{:S(2)}) %collective-permute-start.53) | collective-permute-done | bytes 1032224 | tf_op jit(solution)/shard_map/ppermute | solution.py:300
  377.2 6.5 collective-permute-done.55
  387.9 6.1 collective-permute-done.58
  402.5 4.1 collective-permute-done.61
  416.8 10.1 %collective-permute-done.62 = bf16[128,1536]{1,0:T(8,128)(2,1)S(1)} collective-permute-done((bf16[128,1536]{1,0:T(8,128)(2,1)S(1)}, bf16[128,1536]{1,0:T(8,128)(2,1)S(1)}, u32[]{:S(2)}, u32[]{:S(2)}) %collective-permute-start.62) | collective-permute-done | bytes 393248 | tf_op jit(solution)/shard_map/ppermute | solution.py:296
  428.1 11.0 %collective-permute-done.63 = bf16[256,1536]{1,0:T(8,128)(2,1)S(1)} collective-permute-done((bf16[256,1536]{1,0:T(8,128)(2,1)S(1)}, bf16[256,1536]{1,0:T(8,128)(2,1)S(1)}, u32[]{:S(2)}, u32[]{:S(2)}) %collective-permute-start.63) | collective-permute-done | bytes 786464 | tf_op jit(solution)/shard_map/ppermute | solution.py:296
  445.0 6.2 fusion.18
  467.6 22.7 %collective-permute-done.147 = bf16[3,112,1536]{2,1,0:T(8,128)(2,1)S(1)} collective-permute-done((bf16[3,112,1536]{2,1,0:T(8,128)(2,1)S(1)}, bf16[3,112,1536]{2,1,0:T(8,128)(2,1)S(1)}, u32[]{:S(2)}, u32[]{:S(2)}) %collective-permute-start.147) | collective-permute-done | bytes 1032224 | tf_op jit(solution)/shard_map/ppermute | solution.py:300
  497.3 17.2 %collective-permute-done.148 = bf16[3,112,1536]{2,1,0:T(8,128)(2,1)S(1)} collective-permute-done((bf16[3,112,1536]{2,1,0:T(8,128)(2,1)S(1)}, bf16[3,112,1536]{2,1,0:T(8,128)(2,1)S(1)}, u32[]{:S(2)}, u32[]{:S(2)}) %collective-permute-start.148) | collective-permute-done | bytes 1032224 | tf_op jit(solution)/shard_map/ppermute | solution.py:300
  514.8 4.7 collective-permute-start.149
  521.9 10.1 %attend_back.3 = (bf16[128,384]{1,0:T(8,128)(2,1)S(1)}, bf16[2048,256]{1,0:T(8,128)(2,1)S(1)}, bf16[2048,256]{1,0:T(8,128)(2,1)S(1)}, bf16[2048,256]{1,0:T(8,128)(2,1)S(1)}) custom-call(s32[50]{0:T(128)S(1)} %get-tuple-element.292.where_ref, bf16[128,384]{1,0:T(8,128)(2,1)S(1)} %copy-done.19, bf16[128,384]{1,0:T(8,128)(2,1)S(1)} %fusion.38.g_ref, ...), custom_call_target="tpu_custom_call" | custom-call | flops 2013265920 | bytes 6291456 | tf_op jit(solution)/shard_map/attend_back/pallas_call | solution.py:232
  536.0 10.4 %attend_back.5 = (bf16[128,384]{1,0:T(8,128)(2,1)S(1)}, bf16[2048,256]{1,0:T(8,128)(2,1)S(1)}, bf16[2048,256]{1,0:T(8,128)(2,1)S(1)}, bf16[2048,256]{1,0:T(8,128)(2,1)S(1)}) custom-call(s32[50]{0:T(128)S(1)} %get-tuple-element.291.where_ref, bf16[128,384]{1,0:T(8,128)(2,1)S(1)} %fusion.32.q_ref, bf16[128,384]{1,0:T(8,128)(2,1)S(1)} %fusion.40.g_ref, ...), custom_call_target="tpu_custom_call" | custom-call | flops 2013265920 | bytes 6291456 | tf_op jit(solution)/shard_map/attend_back/pallas_call | solution.py:232
  559.5 5.9 collective-permute-done.77
  567.5 5.2 collective-permute-done.69
  575.2 4.2 collective-permute-done.103
  584.5 5.1 flatten.3
  642.9 7.0 fusion.346
  657.7 14.7 %collective-permute-done.139 = bf16[9,2,2,2,24,256]{5,4,0,1,2,3:T(8,128)(2,1)S(1)} collective-permute-done((bf16[9,2,2,2,24,256]{5,4,0,1,2,3:T(8,128)(2,1)S(1)}, bf16[9,2,2,2,24,256]{5,4,0,1,2,3:T(8,128)(2,1)S(1)}, u32[]{:S(2)}, u32[]{:S(2)}) %collective-permute-start.139) | collective-permute-done | bytes 884768 | tf_op jit(solution)/shard_map/ppermute | solution.py:286
  709.9 22.1 %collective-permute-done.133 = bf16[9,2,24,256]{3,2,0,1:T(8,128)(2,1)S(1)} collective-permute-done((bf16[9,2,24,256]{3,2,0,1:T(8,128)(2,1)S(1)}, bf16[9,2,24,256]{3,2,0,1:T(8,128)(2,1)S(1)}, u32[]{:S(2)}, u32[]{:S(2)}) %collective-permute-start.133) | collective-permute-done | bytes 221216 | tf_op jit(solution)/shard_map/ppermute | solution.py:286
  740.0 6.6 collective-permute-done.84
  747.8 13.9 %collective-permute-done.144 = bf16[3,112,1536]{2,1,0:T(8,128)(2,1)S(1)} collective-permute-done((bf16[3,112,1536]{2,1,0:T(8,128)(2,1)S(1)}, bf16[3,112,1536]{2,1,0:T(8,128)(2,1)S(1)}, u32[]{:S(2)}, u32[]{:S(2)}) %collective-permute-start.144) | collective-permute-done | bytes 1032224 | tf_op jit(solution)/shard_map/ppermute | solution.py:300
  762.0 5.2 collective-permute-start.145
  770.2 10.0 %attend_back.4 = (bf16[128,384]{1,0:T(8,128)(2,1)S(1)}, bf16[2048,256]{1,0:T(8,128)(2,1)S(1)}, bf16[2048,256]{1,0:T(8,128)(2,1)S(1)}, bf16[2048,256]{1,0:T(8,128)(2,1)S(1)}) custom-call(s32[50]{0:T(128)S(1)} %get-tuple-element.292.where_ref, bf16[128,384]{1,0:T(8,128)(2,1)S(1)} %copy-done.17, bf16[128,384]{1,0:T(8,128)(2,1)S(1)} %fusion.39.g_ref, ...), custom_call_target="tpu_custom_call" | custom-call | flops 2013265920 | bytes 6291456 | tf_op jit(solution)/shard_map/attend_back/pallas_call | solution.py:232
  782.8 6.2 collective-permute-done.145
  792.8 5.7 collective-permute-done.95
  816.4 5.3 flatten.2
  830.3 9.8 %collective-permute-done.121 = bf16[5,2,2,2,24,256]{5,4,0,1,2,3:T(8,128)(2,1)S(1)} collective-permute-done((bf16[5,2,2,2,24,256]{5,4,0,1,2,3:T(8,128)(2,1)S(1)}, bf16[5,2,2,2,24,256]{5,4,0,1,2,3:T(8,128)(2,1)S(1)}, u32[]{:S(2)}, u32[]{:S(2)}) %collective-permute-start.121) | collective-permute-done | bytes 491552 | tf_op jit(solution)/shard_map/ppermute | solution.py:286
  887.4 4.2 stack.108
  895.1 12.9 %fusion = (f32[2,3,1,164864]{3,1,2,0:T(4,128)S(1)}, f32[2,3,1,164864]{3,1,2,0:T(4,128)S(1)}, f32[2,3,1,164864]{3,1,2,0:T(4,128)S(1)}) fusion(f32[2,3,1,164864]{3,2,1,0:T(1,128)} %param.34, f32[]{:T(128)} %bitcast.181, f32[]{:T(128)} %bitcast.180, f32[]{:T(128)S(6)} %div.76, f32[1,3,1,164864]{3,1,2,0:T(4,128)S(1)} %copy-done.42, ...), kind=kLoop, calls=%fused_computation.4 | loop fusion | flops 16816128 | bytes 27697164 | tf_op jit(solution)/shard_map/sub | solution.py:272
  908.1 5.7 copy.57
  913.8 5.7 copy.58
  919.5 5.7 copy.59
  (1336 shorter events, 414.5 us)
Async XLA Ops:
  7.2 80.0 %all-gather.5.cloned.1.call-start = ((), (), s32[]{:S(2)}) async-start(), calls=%async_computation | async-start | bytes 6082560 | tf_op jit(solution)/shard_map/all_gather | solution.py:467
  10.1 240.3 %all-gather.7.cloned.1.call-start = ((), (), s32[]{:S(2)}) async-start(), calls=%async_computation.1 | async-start | bytes 10948608 | tf_op jit(solution)/shard_map/all_gather | solution.py:467
  34.7 93.2 %collective-permute-start.17 = (bf16[3,112,1536]{2,1,0:T(8,128)(2,1)}, bf16[3,112,1536]{2,1,0:T(8,128)(2,1)}, u32[]{:S(2)}, u32[]{:S(2)}) collective-permute-start(bf16[3,112,1536]{2,1,0:T(8,128)(2,1)} %pad_maximum_fusion.12), channel_id=1, source_target_pairs={{0,4},{4,8},{8,12},{12,0},{1,5},{5,9},{9,13},{13,1},{2,6},{6,10},{... | collective-permute-start | bytes 3096584 | tf_op jit(solution)/shard_map/ppermute | solution.py:300
  127.9 39.7 %collective-permute-start.18 = (bf16[3,112,1536]{2,1,0:T(8,128)(2,1)}, bf16[3,112,1536]{2,1,0:T(8,128)(2,1)S(1)}, u32[]{:S(2)}, u32[]{:S(2)}) collective-permute-start(bf16[3,112,1536]{2,1,0:T(8,128)(2,1)} %collective-permute-done.17), channel_id=1, source_target_pairs={{0,4},{4,8},{8,12},{12,0},{1,5},{5,9},{9,13},{13,1},{2,6},{6,10},{... | collective-permute-start | bytes 3096584 | tf_op jit(solution)/shard_map/ppermute | solution.py:300
  135.0 37.8 %collective-permute-start.14 = (bf16[256,1536]{1,0:T(8,128)(2,1)S(1)}, bf16[256,1536]{1,0:T(8,128)(2,1)S(1)}, u32[]{:S(2)}, u32[]{:S(2)}) collective-permute-start(bf16[256,1536]{1,0:T(8,128)(2,1)S(1)} %pad_maximum_fusion.25), channel_id=1, source_target_pairs={{0,2},{1,3},{2,0},{3,1},{16,17},{17,16},{18,19},{19,18},{4,6},{5,7... | collective-permute-start | bytes 2359304 | tf_op jit(solution)/shard_map/ppermute | solution.py:296
  167.6 43.2 %collective-permute-start.19 = (bf16[3,112,1536]{2,1,0:T(8,128)(2,1)S(1)}, bf16[3,112,1536]{2,1,0:T(8,128)(2,1)S(1)}, u32[]{:S(2)}, u32[]{:S(2)}) collective-permute-start(bf16[3,112,1536]{2,1,0:T(8,128)(2,1)S(1)} %collective-permute-done.18), channel_id=1, source_target_pairs={{0,4},{4,8},{8,12},{12,0},{1,5},{5,9},{9,13},{13,1},{2,6},{6,10},{... | collective-permute-start | bytes 3096584 | tf_op jit(solution)/shard_map/ppermute | solution.py:300
  172.9 38.1 %collective-permute-start.15 = (bf16[512,1536]{1,0:T(8,128)(2,1)S(1)}, bf16[512,1536]{1,0:T(8,128)(2,1)S(1)}, u32[]{:S(2)}, u32[]{:S(2)}) collective-permute-start(bf16[512,1536]{1,0:T(8,128)(2,1)S(1)} %pad_maximum_fusion.7), channel_id=1, source_target_pairs={{0,16},{16,0},{1,17},{17,1},{2,18},{18,2},{3,19},{19,3},{4,20},{20... | collective-permute-start | bytes 4718600 | tf_op jit(solution)/shard_map/ppermute | solution.py:287
  228.2 12.1 %collective-permute-start.21 = (bf16[256,1536]{1,0:T(8,128)(2,1)S(1)}, bf16[256,1536]{1,0:T(8,128)(2,1)S(1)}, u32[]{:S(2)}, u32[]{:S(2)}) collective-permute-start(bf16[256,1536]{1,0:T(8,128)(2,1)S(1)} %slice.2539), channel_id=1, source_target_pairs={{0,2},{1,3},{2,0},{3,1},{16,17},{17,16},{18,19},{19,18},{4,6},{5,7... | collective-permute-start | bytes 2359304 | tf_op jit(solution)/shard_map/ppermute | solution.py:296
  230.6 77.3 %collective-permute-start.51 = (bf16[3,112,1536]{2,1,0:T(8,128)(2,1)}, bf16[3,112,1536]{2,1,0:T(8,128)(2,1)}, u32[]{:S(2)}, u32[]{:S(2)}) collective-permute-start(bf16[3,112,1536]{2,1,0:T(8,128)(2,1)} %pad_maximum_fusion.13), channel_id=1, source_target_pairs={{0,4},{4,8},{8,12},{12,0},{1,5},{5,9},{9,13},{13,1},{2,6},{6,10},{... | collective-permute-start | bytes 3096584 | tf_op jit(solution)/shard_map/ppermute | solution.py:300
  307.9 26.9 %collective-permute-start.52 = (bf16[3,112,1536]{2,1,0:T(8,128)(2,1)}, bf16[3,112,1536]{2,1,0:T(8,128)(2,1)S(1)}, u32[]{:S(2)}, u32[]{:S(2)}) collective-permute-start(bf16[3,112,1536]{2,1,0:T(8,128)(2,1)} %collective-permute-done.51), channel_id=1, source_target_pairs={{0,4},{4,8},{8,12},{12,0},{1,5},{5,9},{9,13},{13,1},{2,6},{6,10},{... | collective-permute-start | bytes 3096584 | tf_op jit(solution)/shard_map/ppermute | solution.py:300
  314.9 19.9 %collective-permute-start.48 = (bf16[256,1536]{1,0:T(8,128)(2,1)S(1)}, bf16[256,1536]{1,0:T(8,128)(2,1)S(1)}, u32[]{:S(2)}, u32[]{:S(2)}) collective-permute-start(bf16[256,1536]{1,0:T(8,128)(2,1)S(1)} %pad_maximum_fusion.27), channel_id=1, source_target_pairs={{0,2},{1,3},{2,0},{3,1},{16,17},{17,16},{18,19},{19,18},{4,6},{5,7... | collective-permute-start | bytes 2359304 | tf_op jit(solution)/shard_map/ppermute | solution.py:296
  334.8 25.8 %collective-permute-start.53 = (bf16[3,112,1536]{2,1,0:T(8,128)(2,1)S(1)}, bf16[3,112,1536]{2,1,0:T(8,128)(2,1)S(1)}, u32[]{:S(2)}, u32[]{:S(2)}) collective-permute-start(bf16[3,112,1536]{2,1,0:T(8,128)(2,1)S(1)} %collective-permute-done.52), channel_id=1, source_target_pairs={{0,4},{4,8},{8,12},{12,0},{1,5},{5,9},{9,13},{13,1},{2,6},{6,10},{... | collective-permute-start | bytes 3096584 | tf_op jit(solution)/shard_map/ppermute | solution.py:300
  334.9 25.8 %collective-permute-start.49 = (bf16[512,1536]{1,0:T(8,128)(2,1)S(1)}, bf16[512,1536]{1,0:T(8,128)(2,1)S(1)}, u32[]{:S(2)}, u32[]{:S(2)}) collective-permute-start(bf16[512,1536]{1,0:T(8,128)(2,1)S(1)} %pad_maximum_fusion.8), channel_id=1, source_target_pairs={{0,16},{16,0},{1,17},{17,1},{2,18},{18,2},{3,19},{19,3},{4,20},{20... | collective-permute-start | bytes 4718600 | tf_op jit(solution)/shard_map/ppermute | solution.py:287
  385.9 22.7 %collective-permute-start.56 = (bf16[128,1536]{1,0:T(8,128)(2,1)}, bf16[128,1536]{1,0:T(8,128)(2,1)}, u32[]{:S(2)}, u32[]{:S(2)}) collective-permute-start(bf16[128,1536]{1,0:T(8,128)(2,1)} %slice.2542), channel_id=1, source_target_pairs={{0,1},{1,0},{2,3},{3,2},{16,18},{17,19},{18,16},{19,17},{4,5},{5,4... | collective-permute-start | bytes 1179656 | tf_op jit(solution)/shard_map/ppermute | solution.py:296
  414.9 12.1 %collective-permute-start.62 = (bf16[128,1536]{1,0:T(8,128)(2,1)S(1)}, bf16[128,1536]{1,0:T(8,128)(2,1)S(1)}, u32[]{:S(2)}, u32[]{:S(2)}) collective-permute-start(bf16[128,1536]{1,0:T(8,128)(2,1)S(1)} %fusion.336), channel_id=1, source_target_pairs={{0,1},{1,0},{2,3},{3,2},{16,18},{17,19},{18,16},{19,17},{4,5},{5,4... | collective-permute-start | bytes 1179656 | tf_op jit(solution)/shard_map/ppermute | solution.py:296
  465.3 24.9 %collective-permute-start.147 = (bf16[3,112,1536]{2,1,0:T(8,128)(2,1)S(1)}, bf16[3,112,1536]{2,1,0:T(8,128)(2,1)S(1)}, u32[]{:S(2)}, u32[]{:S(2)}) collective-permute-start(bf16[3,112,1536]{2,1,0:T(8,128)(2,1)S(1)} %pad_maximum_fusion.21), channel_id=1, source_target_pairs={{0,12},{4,0},{8,4},{12,8},{1,13},{5,1},{9,5},{13,9},{2,14},{6,2},{... | collective-permute-start | bytes 3096584 | tf_op jit(solution)/shard_map/ppermute | solution.py:300
  466.6 28.4 %collective-permute-start.66 = (bf16[256,1536]{1,0:T(8,128)(2,1)S(1)}, bf16[256,1536]{1,0:T(8,128)(2,1)S(1)}, u32[]{:S(2)}, u32[]{:S(2)}) collective-permute-start(bf16[256,1536]{1,0:T(8,128)(2,1)S(1)} %slice.2537), channel_id=1, source_target_pairs={{0,2},{1,3},{2,0},{3,1},{16,17},{17,16},{18,19},{19,18},{4,6},{5,7... | collective-permute-start | bytes 2359304 | tf_op jit(solution)/shard_map/ppermute | solution.py:296
  490.5 24.1 %collective-permute-start.148 = (bf16[3,112,1536]{2,1,0:T(8,128)(2,1)S(1)}, bf16[3,112,1536]{2,1,0:T(8,128)(2,1)S(1)}, u32[]{:S(2)}, u32[]{:S(2)}) collective-permute-start(bf16[3,112,1536]{2,1,0:T(8,128)(2,1)S(1)} %add_convert_fusion.1), channel_id=1, source_target_pairs={{0,12},{4,0},{8,4},{12,8},{1,13},{5,1},{9,5},{13,9},{2,14},{6,2},{... | collective-permute-start | bytes 3096584 | tf_op jit(solution)/shard_map/ppermute | solution.py:300
  495.0 145.4 %collective-permute-start.130 = (bf16[1,384,768]{2,1,0:T(8,128)(2,1)}, bf16[1,384,768]{2,1,0:T(8,128)(2,1)}, u32[]{:S(2)}, u32[]{:S(2)}) collective-permute-start(bf16[1,384,768]{2,1,0:T(8,128)(2,1)} %fusion.28), channel_id=1, source_target_pairs={{0,16},{16,0},{1,17},{17,1},{2,18},{18,2},{3,19},{19,3},{4,20},{20... | collective-permute-start | bytes 1769480 | tf_op jit(solution)/shard_map/ppermute | solution.py:287
  495.3 24.2 %collective-permute-start.67 = (bf16[128,1536]{1,0:T(8,128)(2,1)S(1)}, bf16[128,1536]{1,0:T(8,128)(2,1)S(1)}, u32[]{:S(2)}, u32[]{:S(2)}) collective-permute-start(bf16[128,1536]{1,0:T(8,128)(2,1)S(1)} %slice.2541), channel_id=1, source_target_pairs={{0,1},{1,0},{2,3},{3,2},{16,18},{17,19},{18,16},{19,17},{4,5},{5,4... | collective-permute-start | bytes 1179656 | tf_op jit(solution)/shard_map/ppermute | solution.py:296
  514.8 37.9 %collective-permute-start.149 = (bf16[3,112,1536]{2,1,0:T(8,128)(2,1)S(1)}, bf16[3,112,1536]{2,1,0:T(8,128)(2,1)S(1)}, u32[]{:S(2)}, u32[]{:S(2)}) collective-permute-start(bf16[3,112,1536]{2,1,0:T(8,128)(2,1)S(1)} %add_convert_fusion), channel_id=1, source_target_pairs={{0,12},{4,0},{8,4},{12,8},{1,13},{5,1},{9,5},{13,9},{2,14},{6,2},{... | collective-permute-start | bytes 3096584 | tf_op jit(solution)/shard_map/ppermute | solution.py:300
  532.9 20.8 %collective-permute-start.76 = (bf16[1024,256]{1,0:T(8,128)(2,1)S(1)}, bf16[1024,256]{1,0:T(8,128)(2,1)}, u32[]{:S(2)}, u32[]{:S(2)}) collective-permute-start(bf16[1024,256]{1,0:T(8,128)(2,1)S(1)} %slice.1455), channel_id=1, source_target_pairs={{0,16},{16,0},{1,17},{17,1},{2,18},{18,2},{3,19},{19,3},{4,20},{20... | collective-permute-start | bytes 1572872 | tf_op jit(solution)/shard_map/ppermute | solution.py:287
  533.0 22.0 %collective-permute-start.72 = (bf16[1024,256]{1,0:T(8,128)(2,1)S(1)}, bf16[1024,256]{1,0:T(8,128)(2,1)S(1)}, u32[]{:S(2)}, u32[]{:S(2)}) collective-permute-start(bf16[1024,256]{1,0:T(8,128)(2,1)S(1)} %slice.1446), channel_id=1, source_target_pairs={{0,16},{16,0},{1,17},{17,1},{2,18},{18,2},{3,19},{19,3},{4,20},{20... | collective-permute-start | bytes 1572872 | tf_op jit(solution)/shard_map/ppermute | solution.py:287
  533.6 22.1 %collective-permute-start.68 = (bf16[1024,256]{1,0:T(8,128)(2,1)S(1)}, bf16[1024,256]{1,0:T(8,128)(2,1)S(1)}, u32[]{:S(2)}, u32[]{:S(2)}) collective-permute-start(bf16[1024,256]{1,0:T(8,128)(2,1)S(1)} %slice.1437), channel_id=1, source_target_pairs={{0,16},{16,0},{1,17},{17,1},{2,18},{18,2},{3,19},{19,3},{4,20},{20... | collective-permute-start | bytes 1572872 | tf_op jit(solution)/shard_map/ppermute | solution.py:287
  555.7 75.7 %collective-permute-start.126 = (bf16[1,384,768]{2,1,0:T(8,128)(2,1)}, bf16[1,384,768]{2,1,0:T(8,128)(2,1)}, u32[]{:S(2)}, u32[]{:S(2)}) collective-permute-start(bf16[1,384,768]{2,1,0:T(8,128)(2,1)} %fusion.25), channel_id=1, source_target_pairs={{0,16},{16,0},{1,17},{17,1},{2,18},{18,2},{3,19},{19,3},{4,20},{20... | collective-permute-start | bytes 1769480 | tf_op jit(solution)/shard_map/ppermute | solution.py:287
  556.4 25.5 %collective-permute-start.150 = (bf16[3,112,768]{2,1,0:T(8,128)(2,1)S(1)}, bf16[3,112,768]{2,1,0:T(8,128)(2,1)S(1)}, u32[]{:S(2)}, u32[]{:S(2)}) collective-permute-start(bf16[3,112,768]{2,1,0:T(8,128)(2,1)S(1)} %select_convert_fusion), channel_id=1, source_target_pairs={{0,16},{16,0},{1,17},{17,1},{2,18},{18,2},{3,19},{19,3},{4,20},{20... | collective-permute-start | bytes 1548296 | tf_op jit(solution)/shard_map/ppermute | solution.py:287
  579.4 55.5 %collective-permute-start.127 = (bf16[1,384,768]{2,1,0:T(8,128)(2,1)}, bf16[1,384,768]{2,1,0:T(8,128)(2,1)}, u32[]{:S(2)}, u32[]{:S(2)}) collective-permute-start(bf16[1,384,768]{2,1,0:T(8,128)(2,1)} %fusion.26), channel_id=1, source_target_pairs={{0,16},{16,0},{1,17},{17,1},{2,18},{18,2},{3,19},{19,3},{4,20},{20... | collective-permute-start | bytes 1769480 | tf_op jit(solution)/shard_map/ppermute | solution.py:287
  631.4 22.0 %collective-permute-start.81 = (bf16[256,1536]{1,0:T(8,128)(2,1)}, bf16[256,1536]{1,0:T(8,128)(2,1)}, u32[]{:S(2)}, u32[]{:S(2)}) collective-permute-start(bf16[256,1536]{1,0:T(8,128)(2,1)} %pad_maximum_fusion.30), channel_id=1, source_target_pairs={{0,2},{1,3},{2,0},{3,1},{16,17},{17,16},{18,19},{19,18},{4,6},{5,7... | collective-permute-start | bytes 2359304 | tf_op jit(solution)/shard_map/ppermute | solution.py:296
  651.6 20.8 %collective-permute-start.139 = (bf16[9,2,2,2,24,256]{5,4,0,1,2,3:T(8,128)(2,1)S(1)}, bf16[9,2,2,2,24,256]{5,4,0,1,2,3:T(8,128)(2,1)S(1)}, u32[]{:S(2)}, u32[]{:S(2)}) collective-permute-start(bf16[9,2,2,2,24,256]{5,4,0,1,2,3:T(8,128)(2,1)S(1)} %fusion.47), channel_id=1, source_target_pairs={{0,4},{4,0},{8,12},{12,8},{1,5},{5,1},{9,13},{13,9},{2,6},{6,2},{1... | collective-permute-start | bytes 2654216 | tf_op jit(solution)/shard_map/ppermute | solution.py:286
  654.7 25.7 %collective-permute-start.82 = (bf16[512,1536]{1,0:T(8,128)(2,1)S(1)}, bf16[512,1536]{1,0:T(8,128)(2,1)S(1)}, u32[]{:S(2)}, u32[]{:S(2)}) collective-permute-start(bf16[512,1536]{1,0:T(8,128)(2,1)S(1)} %pad_maximum_fusion.10), channel_id=1, source_target_pairs={{0,16},{16,0},{1,17},{17,1},{2,18},{18,2},{3,19},{19,3},{4,20},{20... | collective-permute-start | bytes 4718600 | tf_op jit(solution)/shard_map/ppermute | solution.py:287
  654.9 22.1 %collective-permute-start.135 = (bf16[9,2,2,2,24,256]{5,4,0,1,3,2:T(8,128)(2,1)S(1)}, bf16[9,2,2,2,24,256]{5,4,0,1,3,2:T(8,128)(2,1)S(1)}, u32[]{:S(2)}, u32[]{:S(2)}) collective-permute-start(bf16[9,2,2,2,24,256]{5,4,0,1,3,2:T(8,128)(2,1)S(1)} %fusion.46), channel_id=1, source_target_pairs={{0,2},{2,0},{1,3},{3,1},{4,6},{6,4},{5,7},{7,5},{8,10},{10,8},{9,1... | collective-permute-start | bytes 2654216 | tf_op jit(solution)/shard_map/ppermute | solution.py:287
  656.2 22.9 %collective-permute-start.131 = (bf16[9,2,2,2,24,256]{5,4,0,1,2,3:T(8,128)(2,1)S(1)}, bf16[9,2,2,2,24,256]{5,4,0,1,2,3:T(8,128)(2,1)S(1)}, u32[]{:S(2)}, u32[]{:S(2)}) collective-permute-start(bf16[9,2,2,2,24,256]{5,4,0,1,2,3:T(8,128)(2,1)S(1)} %fusion.45), channel_id=1, source_target_pairs={{0,1},{1,0},{2,3},{3,2},{4,5},{5,4},{6,7},{7,6},{8,9},{9,8},{10,11... | collective-permute-start | bytes 2654216 | tf_op jit(solution)/shard_map/ppermute | solution.py:287
  672.7 26.8 %collective-permute-start.140 = (bf16[9,2,2,24,256]{4,3,0,1,2:T(8,128)(2,1)S(1)}, bf16[9,2,2,24,256]{4,3,0,1,2:T(8,128)(2,1)S(1)}, u32[]{:S(2)}, u32[]{:S(2)}) collective-permute-start(bf16[9,2,2,24,256]{4,3,0,1,2:T(8,128)(2,1)S(1)} %fusion.75), channel_id=1, source_target_pairs={{0,1},{1,0},{2,3},{3,2},{4,5},{5,4},{6,7},{7,6},{8,9},{9,8},{10,11... | collective-permute-start | bytes 1327112 | tf_op jit(solution)/shard_map/ppermute | solution.py:287
  677.3 23.6 %collective-permute-start.136 = (bf16[9,2,2,24,256]{4,3,0,1,2:T(8,128)(2,1)S(1)}, bf16[9,2,2,24,256]{4,3,0,1,2:T(8,128)(2,1)S(1)}, u32[]{:S(2)}, u32[]{:S(2)}) collective-permute-start(bf16[9,2,2,24,256]{4,3,0,1,2:T(8,128)(2,1)S(1)} %fusion.74), channel_id=1, source_target_pairs={{0,4},{4,0},{8,12},{12,8},{1,5},{5,1},{9,13},{13,9},{2,6},{6,2},{1... | collective-permute-start | bytes 1327112 | tf_op jit(solution)/shard_map/ppermute | solution.py:286
  679.4 22.7 %collective-permute-start.132 = (bf16[9,2,2,24,256]{4,3,0,1,2:T(8,128)(2,1)S(1)}, bf16[9,2,2,24,256]{4,3,0,1,2:T(8,128)(2,1)S(1)}, u32[]{:S(2)}, u32[]{:S(2)}) collective-permute-start(bf16[9,2,2,24,256]{4,3,0,1,2:T(8,128)(2,1)S(1)} %fusion.73), channel_id=1, source_target_pairs={{0,2},{2,0},{1,3},{3,1},{4,6},{6,4},{5,7},{7,5},{8,10},{10,8},{9,1... | collective-permute-start | bytes 1327112 | tf_op jit(solution)/shard_map/ppermute | solution.py:287
  688.6 45.3 %collective-permute-start.83 = (bf16[512,1536]{1,0:T(8,128)(2,1)S(1)}, bf16[512,1536]{1,0:T(8,128)(2,1)S(1)}, u32[]{:S(2)}, u32[]{:S(2)}) collective-permute-start(bf16[512,1536]{1,0:T(8,128)(2,1)S(1)} %slice.2532), channel_id=1, source_target_pairs={{0,16},{16,0},{1,17},{17,1},{2,18},{18,2},{3,19},{19,3},{4,20},{20... | collective-permute-start | bytes 4718600 | tf_op jit(solution)/shard_map/ppermute | solution.py:287
  699.3 36.2 %collective-permute-start.143 = (bf16[3,112,1536]{2,1,0:T(8,128)(2,1)S(1)}, bf16[3,112,1536]{2,1,0:T(8,128)(2,1)S(1)}, u32[]{:S(2)}, u32[]{:S(2)}) collective-permute-start(bf16[3,112,1536]{2,1,0:T(8,128)(2,1)S(1)} %pad_maximum_fusion.20), channel_id=1, source_target_pairs={{0,12},{4,0},{8,4},{12,8},{1,13},{5,1},{9,5},{13,9},{2,14},{6,2},{... | collective-permute-start | bytes 3096584 | tf_op jit(solution)/shard_map/ppermute | solution.py:300
  702.3 29.8 %collective-permute-start.133 = (bf16[9,2,24,256]{3,2,0,1:T(8,128)(2,1)S(1)}, bf16[9,2,24,256]{3,2,0,1:T(8,128)(2,1)S(1)}, u32[]{:S(2)}, u32[]{:S(2)}) collective-permute-start(bf16[9,2,24,256]{3,2,0,1:T(8,128)(2,1)S(1)} %fusion.124), channel_id=1, source_target_pairs={{0,4},{4,0},{8,12},{12,8},{1,5},{5,1},{9,13},{13,9},{2,6},{6,2},{1... | collective-permute-start | bytes 663560 | tf_op jit(solution)/shard_map/ppermute | solution.py:286
  706.5 26.9 %collective-permute-start.142 = (bf16[9,24,256]{2,1,0:T(8,128)(2,1)S(1)}, bf16[9,24,256]{2,1,0:T(8,128)(2,1)S(1)}, u32[]{:S(2)}, u32[]{:S(2)}) collective-permute-start(bf16[9,24,256]{2,1,0:T(8,128)(2,1)S(1)} %fusion.246), channel_id=1, source_target_pairs={{0,8},{4,12},{8,0},{12,4},{1,9},{5,13},{9,1},{13,5},{2,10},{6,14},... | collective-permute-start | bytes 331784 | tf_op jit(solution)/shard_map/ppermute | solution.py:286
  709.2 24.7 %collective-permute-start.138 = (bf16[9,24,256]{2,1,0:T(8,128)(2,1)S(1)}, bf16[9,24,256]{2,1,0:T(8,128)(2,1)S(1)}, u32[]{:S(2)}, u32[]{:S(2)}) collective-permute-start(bf16[9,24,256]{2,1,0:T(8,128)(2,1)S(1)} %fusion.245), channel_id=1, source_target_pairs={{0,8},{4,12},{8,0},{12,4},{1,9},{5,13},{9,1},{13,5},{2,10},{6,14},... | collective-permute-start | bytes 331784 | tf_op jit(solution)/shard_map/ppermute | solution.py:286
  734.5 12.1 %collective-permute-start.84 = (bf16[256,1536]{1,0:T(8,128)(2,1)S(1)}, bf16[256,1536]{1,0:T(8,128)(2,1)S(1)}, u32[]{:S(2)}, u32[]{:S(2)}) collective-permute-start(bf16[256,1536]{1,0:T(8,128)(2,1)S(1)} %slice.2536), channel_id=1, source_target_pairs={{0,2},{1,3},{2,0},{3,1},{16,17},{17,16},{18,19},{19,18},{4,6},{5,7... | collective-permute-start | bytes 2359304 | tf_op jit(solution)/shard_map/ppermute | solution.py:296
  735.8 26.0 %collective-permute-start.144 = (bf16[3,112,1536]{2,1,0:T(8,128)(2,1)S(1)}, bf16[3,112,1536]{2,1,0:T(8,128)(2,1)S(1)}, u32[]{:S(2)}, u32[]{:S(2)}) collective-permute-start(bf16[3,112,1536]{2,1,0:T(8,128)(2,1)S(1)} %add_convert_fusion.3), channel_id=1, source_target_pairs={{0,12},{4,0},{8,4},{12,8},{1,13},{5,1},{9,5},{13,9},{2,14},{6,2},{... | collective-permute-start | bytes 3096584 | tf_op jit(solution)/shard_map/ppermute | solution.py:300
  746.9 20.4 %collective-permute-start.85 = (bf16[128,1536]{1,0:T(8,128)(2,1)S(1)}, bf16[128,1536]{1,0:T(8,128)(2,1)S(1)}, u32[]{:S(2)}, u32[]{:S(2)}) collective-permute-start(bf16[128,1536]{1,0:T(8,128)(2,1)S(1)} %slice.2540), channel_id=1, source_target_pairs={{0,1},{1,0},{2,3},{3,2},{16,18},{17,19},{18,16},{19,17},{4,5},{5,4... | collective-permute-start | bytes 1179656 | tf_op jit(solution)/shard_map/ppermute | solution.py:296
  762.0 27.0 %collective-permute-start.145 = (bf16[3,112,1536]{2,1,0:T(8,128)(2,1)S(1)}, bf16[3,112,1536]{2,1,0:T(8,128)(2,1)S(1)}, u32[]{:S(2)}, u32[]{:S(2)}) collective-permute-start(bf16[3,112,1536]{2,1,0:T(8,128)(2,1)S(1)} %add_convert_fusion.2), channel_id=1, source_target_pairs={{0,12},{4,0},{8,4},{12,8},{1,13},{5,1},{9,5},{13,9},{2,14},{6,2},{... | collective-permute-start | bytes 3096584 | tf_op jit(solution)/shard_map/ppermute | solution.py:300
  789.5 12.1 %collective-permute-start.146 = (bf16[3,112,768]{2,1,0:T(8,128)(2,1)S(1)}, bf16[3,112,768]{2,1,0:T(8,128)(2,1)S(1)}, u32[]{:S(2)}, u32[]{:S(2)}) collective-permute-start(bf16[3,112,768]{2,1,0:T(8,128)(2,1)S(1)} %select_convert_fusion.1), channel_id=1, source_target_pairs={{0,16},{16,0},{1,17},{17,1},{2,18},{18,2},{3,19},{19,3},{4,20},{20... | collective-permute-start | bytes 1548296 | tf_op jit(solution)/shard_map/ppermute | solution.py:287
  827.0 13.2 %collective-permute-start.121 = (bf16[5,2,2,2,24,256]{5,4,0,1,2,3:T(8,128)(2,1)S(1)}, bf16[5,2,2,2,24,256]{5,4,0,1,2,3:T(8,128)(2,1)S(1)}, u32[]{:S(2)}, u32[]{:S(2)}) collective-permute-start(bf16[5,2,2,2,24,256]{5,4,0,1,2,3:T(8,128)(2,1)S(1)} %fusion.69), channel_id=1, source_target_pairs={{0,4},{4,0},{8,12},{12,8},{1,5},{5,1},{9,13},{13,9},{2,6},{6,2},{1... | collective-permute-start | bytes 1474568 | tf_op jit(solution)/shard_map/ppermute | solution.py:286
  828.0 13.1 %collective-permute-start.117 = (bf16[5,2,2,2,24,256]{5,4,0,1,3,2:T(8,128)(2,1)S(1)}, bf16[5,2,2,2,24,256]{5,4,0,1,3,2:T(8,128)(2,1)S(1)}, u32[]{:S(2)}, u32[]{:S(2)}) collective-permute-start(bf16[5,2,2,2,24,256]{5,4,0,1,3,2:T(8,128)(2,1)S(1)} %fusion.68), channel_id=1, source_target_pairs={{0,2},{2,0},{1,3},{3,1},{4,6},{6,4},{5,7},{7,5},{8,10},{10,8},{9,1... | collective-permute-start | bytes 1474568 | tf_op jit(solution)/shard_map/ppermute | solution.py:287
  829.3 13.5 %collective-permute-start.113 = (bf16[5,2,2,2,24,256]{5,4,3,2,1,0:T(8,128)(2,1)S(1)}, bf16[5,2,2,2,24,256]{5,4,3,2,1,0:T(8,128)(2,1)S(1)}, u32[]{:S(2)}, u32[]{:S(2)}) collective-permute-start(bf16[5,2,2,2,24,256]{5,4,3,2,1,0:T(8,128)(2,1)S(1)} %fusion.67), channel_id=1, source_target_pairs={{0,1},{1,0},{2,3},{3,2},{4,5},{5,4},{6,7},{7,6},{8,9},{9,8},{10,11... | collective-permute-start | bytes 1474568 | tf_op jit(solution)/shard_map/ppermute | solution.py:287
  (389 other events, 4697.7 us)
Sparse Core Ops, SparseCore 0:
  11.5 75.5 all-gather.4
  90.1 115.5 all-gather.6

commit v2 on v1

v2 whole, which is shorter than its diff:
```python
import functools

import jax
import jax.numpy as jnp
import numpy as np
from jax import lax
from jax.experimental import pallas as pl
from jax.experimental.pallas import tpu as pltpu
from jax.sharding import Mesh, PartitionSpec as P

D = 1472
HEADS = 6
HEAD_DIM = 64
NLANG = 4
INNER = 384
FF = 3584
LANES = 128
HALF = 768
WIDE = 2 * HALF

RMS_EPS = 1e-06
CLIP_NORM = 0.01
BETA_FIRST = 0.9
BETA_SECOND = 0.999
ADAM_EPS = 1e-08
MATRIX_RATE = 0.05
GAIN_RATE = 0.2
DECAY_STEP = 0.005
MASKED = -1000000000.0
PERIOD = 896
MIB = 1024 * 1024
BF = jnp.bfloat16
F32 = jnp.float32


def dot_nn(a, b):
    return lax.dot_general(a, b, (((1,), (0,)), ((), ())), preferred_element_type=F32)


def dot_nt(a, b):
    return lax.dot_general(a, b, (((1,), (1,)), ((), ())), preferred_element_type=F32)


def dot_tn(a, b):
    return lax.dot_general(a, b, (((0,), (0,)), ((), ())), preferred_element_type=F32)


def flat_pieces(hid):
    found = []
    for t in range(PERIOD // LANES):
        at = LANES * t
        while at < LANES * (t + 1):
            j = at // hid
            end = min(LANES * (t + 1), (j + 1) * hid)
            found.append((t, at - LANES * t, j, at - j * hid, end - at))
            at = end
    return found


def unflatten_kernel(hid, groups, flat_ref, spread_ref, out_ref, acc_ref):
    chunks = PERIOD // LANES
    acc_ref[...] = jnp.zeros_like(acc_ref)
    for t in range(chunks):
        rows = flat_ref[0, pl.ds(t, groups, stride=chunks), :].astype(BF)
        for piece_t, lane, j, first, length in flat_pieces(hid):
            if piece_t == t:
                placed = dot_tn(rows, spread_ref[j])
                acc_ref[first : first + length, :] += placed[lane : lane + length, :]
    out_ref[0] = acc_ref[...].astype(BF)


def unflatten(flat, spread, hid, groups):
    count, flat_rows, _ = flat.shape
    lanes = spread.shape[2]
    return pl.pallas_call(
        functools.partial(unflatten_kernel, hid, groups),
        out_shape=jax.ShapeDtypeStruct((count, hid, lanes), BF),
        grid=(count,),
        in_specs=[
            pl.BlockSpec((1, flat_rows, LANES), lambda i: (i, 0, 0)),
            pl.BlockSpec(spread.shape, lambda i: (0, 0, 0)),
        ],
        out_specs=pl.BlockSpec((1, hid, lanes), lambda i: (i, 0, 0)),
        scratch_shapes=[pltpu.VMEM((hid, lanes), F32)],
        compiler_params=pltpu.CompilerParams(vmem_limit_bytes=10 * MIB),
        name="unflatten",
    )(flat, spread)


def flatten_kernel(hid, groups, grad_ref, spread_ref, out_ref):
    chunks = PERIOD // LANES
    high = grad_ref[0].astype(BF)
    low = (grad_ref[0] - high.astype(F32)).astype(BF)
    for t in range(chunks):
        total = jnp.zeros((groups, LANES), F32)
        for piece_t, lane, j, first, length in flat_pieces(hid):
            if piece_t == t:
                for part in (high, low):
                    rows = part[first : first + length, :]
                    parts = []
                    if lane > 0:
                        parts.append(jnp.zeros((lane, rows.shape[1]), BF))
                    parts.append(rows)
                    if lane + length < LANES:
                        parts.append(jnp.zeros((LANES - lane - length, rows.shape[1]), BF))
                    rows = jnp.concatenate(parts, 0) if len(parts) > 1 else rows
                    total = total + dot_nt(spread_ref[j], rows)
        out_ref[0, pl.ds(t, groups, stride=chunks), :] = total


def flatten(grads, spread, hid, groups):
    count, _, lanes = grads.shape
    flat_rows = groups * PERIOD // LANES
    return pl.pallas_call(
        functools.partial(flatten_kernel, hid, groups),
        out_shape=jax.ShapeDtypeStruct((count, flat_rows, LANES), F32),
        grid=(count,),
        in_specs=[
            pl.BlockSpec((1, hid, lanes), lambda i: (i, 0, 0)),
            pl.BlockSpec(spread.shape, lambda i: (0, 0, 0)),
        ],
        out_specs=pl.BlockSpec((1, flat_rows, LANES), lambda i: (i, 0, 0)),
        compiler_params=pltpu.CompilerParams(vmem_limit_bytes=10 * MIB),
        name="flatten",
    )(grads, spread)


def finish_kernel(
    slot_rate, scal_ref, all_ref, enc_ref, dec_ref, early_ref, own_ref, cross_ref, gain_ref,
    fw_ref, fm_ref, fv_ref, aw_ref, am_ref, av_ref, tw_ref, tm_ref, tv_ref, gw_ref, gm_ref, gv_ref,
    fm_out, fv_out, fw_out, am_out, av_out, aw_out, tm_out, tv_out, tw_out, gm_out, gv_out, gw_out,
):
    at = pl.program_id(0)
    gains = all_ref[0:7, :]
    square = jnp.sum(jnp.sum(gains * gains, axis=1, keepdims=True), axis=0, keepdims=True)
    norm = jnp.sqrt(all_ref[7:8, 0:1] + square)
    clip = CLIP_NORM / jnp.maximum(norm, CLIP_NORM)
    scales = (clip, scal_ref[0], scal_ref[1])

    def feed(grad_ref):
        fm_out[0], fv_out[0], fw_out[0] = adam_rule(
            fw_ref[0], fm_ref[0], fv_ref[0], grad_ref[0], *scales, MATRIX_RATE, DECAY_STEP
        )

    @pl.when(at < 3)
    def _():
        feed(enc_ref)

    @pl.when(at >= 3)
    def _():
        feed(dec_ref)

    chunk = aw_ref.shape[2]
    grads = [ref.at[i] for ref in (early_ref, own_ref, cross_ref) for i in range(4)]
    for i, grad in enumerate(grads):

        @pl.when(at == i // 2)
        def _(i=i, grad=grad):
            rate = slot_rate if i % 4 == 3 else MATRIX_RATE
            k = i % 2
            am_out[k], av_out[k], aw_out[k] = adam_rule(
                aw_ref[k], am_ref[k], av_ref[k], grad[:, :chunk], *scales, rate, DECAY_STEP
            )

    @pl.when(at == 5)
    def _():
        for i, (grad, rate) in enumerate(((early_ref.at[4], 1.0), (cross_ref.at[4], 1.5 * D ** (-0.5)))):
            tm_out[i], tv_out[i], tw_out[i] = adam_rule(
                tw_ref[i], tm_ref[i], tv_ref[i], grad[:, :chunk], *scales, rate, DECAY_STEP
            )
        gm_out[...], gv_out[...], gw_out[...] = adam_rule(
            gw_ref[...], gm_ref[...], gv_ref[...], gain_ref[...], *scales, GAIN_RATE, 0.0
        )


def finish(slot_rate, scalars, everything, feed_grads, rest_grads, feed, attn, table, gain):
    block = (1,) + feed[0].shape[1:]
    flat = pl.BlockSpec(block, lambda i: (i, 0, 0))

    def whole(value):
        return pl.BlockSpec(value.shape, lambda i: (0,) * value.ndim)

    def like(value):
        return jax.ShapeDtypeStruct(value.shape, F32)

    rest = table + gain
    pair = pl.BlockSpec((2,) + attn[0].shape[1:], lambda i: (i, 0, 0))
    return pl.pallas_call(
        functools.partial(finish_kernel, slot_rate),
        out_shape=[like(v) for v in feed + attn + rest],
        grid=(6,),
        in_specs=[pl.BlockSpec(memory_space=pltpu.SMEM), whole(everything)]
        + [
            pl.BlockSpec(block, lambda i: (jnp.minimum(i, 2), 0, 0)),
            pl.BlockSpec(block, lambda i: (jnp.maximum(i - 3, 0), 0, 0)),
        ]
        + [whole(v) for v in rest_grads]
        + [flat] * 3
        + [pair] * 3
        + [whole(v) for v in rest],
        out_specs=[flat] * 3 + [pair] * 3 + [whole(v) for v in rest],
        compiler_params=pltpu.CompilerParams(vmem_limit_bytes=56 * MIB),
        name="finish",
    )(scalars, everything, *feed_grads, *rest_grads, *feed, *attn, *rest)


def head_lanes(shape, h):
    lane = lax.broadcasted_iota(jnp.int32, shape, 1)
    return (lane < HEAD_DIM) if h == 0 else (lane >= HEAD_DIM)


def attend_kernel(causal, where_ref, q_ref, kv_ref, out_ref, pos_ref):
    count = q_ref.shape[0]
    length = kv_ref.shape[0]
    blocks = length // count
    limit = where_ref[blocks]
    first = where_ref[blocks + 1]
    for b in range(blocks):
        pos_ref[:, b * count : (b + 1) * count] = (
            lax.broadcasted_iota(jnp.int32, (8, count), 1) + where_ref[b]
        )
    pos = pos_ref[0:1, :]
    last = jnp.full((count, 1), limit - 1, jnp.int32)
    if causal:
        last = jnp.minimum(last, first + lax.broadcasted_iota(jnp.int32, (count, 1), 0))
    allowed = pos <= last
    for p in range(3):
        lanes = slice(p * LANES, (p + 1) * LANES)
        values = slice(INNER + p * LANES, INNER + (p + 1) * LANES)
        queries = q_ref[:, lanes] * HEAD_DIM ** (-0.5)
        context = []
        for h in range(2):
            own = jnp.where(head_lanes(queries.shape, h), queries, jnp.zeros_like(queries))
            scores = dot_nt(own, kv_ref[:, lanes])
            scores = jnp.where(allowed, scores, MASKED)
            raised = jnp.exp(scores - jnp.max(scores, axis=1, keepdims=True))
            probs = raised * (1.0 / jnp.sum(raised, axis=1, keepdims=True))
            context.append(dot_nn(probs.astype(BF), kv_ref[:, values]))
        out_ref[:, lanes] = jnp.where(
            head_lanes(context[0].shape, 0), context[0], context[1]
        ).astype(BF)


def attend(where, queries, kv, causal):
    count = queries.shape[0]
    length = kv.shape[0]
    vmem = pl.BlockSpec(memory_space=pltpu.VMEM)
    return pl.pallas_call(
        functools.partial(attend_kernel, causal),
        out_shape=jax.ShapeDtypeStruct((count, INNER), BF),
        in_specs=[pl.BlockSpec(memory_space=pltpu.SMEM)] + [vmem] * 2,
        out_specs=vmem,
        scratch_shapes=[pltpu.VMEM((8, length), jnp.int32)],
        compiler_params=pltpu.CompilerParams(vmem_limit_bytes=8 * MIB + 4096 * length),
        cost_estimate=pl.CostEstimate(
            flops=4 * count * length * INNER * 2,
            transcendentals=HEADS * count * length,
            bytes_accessed=4 * length * INNER,
        ),
        name="attend",
    )(where, queries, kv)


def attend_back_kernel(causal, where_ref, q_ref, g_ref, kv_ref, dq_ref, dkv_ref, pos_ref):
    count = q_ref.shape[0]
    length = kv_ref.shape[0]
    blocks = length // count
    limit = where_ref[blocks]
    first = where_ref[blocks + 1]
    scale = HEAD_DIM ** (-0.5)
    last = jnp.full((1, count), limit - 1, jnp.int32)
    if causal:
        last = jnp.minimum(last, first + lax.broadcasted_iota(jnp.int32, (1, count), 1))
    for b in range(blocks):
        pos_ref[b * count : (b + 1) * count, :] = (
            lax.broadcasted_iota(jnp.int32, (count, count), 0) + where_ref[b]
        )
    for p in range(3):
        lanes = slice(p * LANES, (p + 1) * LANES)
        values = slice(INNER + p * LANES, INNER + (p + 1) * LANES)
        allowed = pos_ref[...] <= last
        queries = q_ref[:, lanes] * scale
        grads = g_ref[:, lanes]
        d_query, d_key, d_value = [], None, None
        for h in range(2):
            own_q = jnp.where(head_lanes(queries.shape, h), queries, jnp.zeros_like(queries))
            own_g = jnp.where(head_lanes(grads.shape, h), grads, jnp.zeros_like(grads))
            scores = dot_nt(kv_ref[:, lanes], own_q)
            scores = jnp.where(allowed, scores, MASKED)
            raised = jnp.exp(scores - jnp.max(scores, axis=0, keepdims=True))
            probs = raised * (1.0 / jnp.sum(raised, axis=0, keepdims=True))
            d_probs = dot_nt(kv_ref[:, values], own_g)
            inner = jnp.sum(probs * d_probs, axis=0, keepdims=True)
            d_scores = (probs * (d_probs - inner)).astype(BF)
            d_query.append(dot_tn(d_scores, kv_ref[:, lanes]) * scale)
            key_part = dot_nn(d_scores, own_q)
            value_part = dot_nn(probs.astype(BF), own_g)
            d_key = key_part if h == 0 else d_key + key_part
            d_value = value_part if h == 0 else d_value + value_part
        dq_ref[:, lanes] = jnp.where(
            head_lanes(d_query[0].shape, 0), d_query[0], d_query[1]
        ).astype(BF)
        dkv_ref[:, lanes] = d_key.astype(BF)
        dkv_ref[:, values] = d_value.astype(BF)


def attend_back(where, queries, grads, kv, causal):
    count = queries.shape[0]
    length = kv.shape[0]
    vmem = pl.BlockSpec(memory_space=pltpu.VMEM)
    return pl.pallas_call(
        functools.partial(attend_back_kernel, causal),
        out_shape=(
            jax.ShapeDtypeStruct((count, INNER), BF),
            jax.ShapeDtypeStruct((length, 2 * INNER), BF),
        ),
        in_specs=[pl.BlockSpec(memory_space=pltpu.SMEM)] + [vmem] * 3,
        out_specs=(vmem,) * 2,
        scratch_shapes=[pltpu.VMEM((length, count), jnp.int32)],
        compiler_params=pltpu.CompilerParams(vmem_limit_bytes=8 * MIB + 8192 * length),
        cost_estimate=pl.CostEstimate(
            flops=10 * count * length * INNER * 2,
            transcendentals=HEADS * count * length,
            bytes_accessed=8 * length * INNER,
        ),
        name="attend_back",
    )(where, queries, grads, kv)


def rms_scale(stream):
    return lax.rsqrt(jnp.sum(stream * stream, axis=-1, keepdims=True) * (1.0 / D) + RMS_EPS)


def rms_reverse(stream, gain, scale, grad_out):
    weighted = grad_out * gain
    inner_mean = jnp.sum(weighted * stream, axis=-1, keepdims=True) * (1.0 / D)
    grad_in = scale * weighted - stream * (scale * scale * scale) * inner_mean
    grad_gain = jnp.sum(grad_out * stream * scale, axis=0)
    return (grad_in, grad_gain)


def gated_units(gate, upper):
    return jax.nn.gelu(gate, approximate=True) * upper


def adam_rule(weight, first, second, grad, clip, first_scale, second_scale, rate, decay_step):
    clipped = grad * clip
    first_new = BETA_FIRST * first + (1.0 - BETA_FIRST) * clipped
    second_new = BETA_SECOND * second + (1.0 - BETA_SECOND) * clipped * clipped
    ratio = first_new * first_scale / (jnp.sqrt(second_new * second_scale) + ADAM_EPS)
    return (first_new, second_new, weight - rate * ratio - decay_step * weight)


def anchor(value, *events):
    return lax.optimization_barrier((value,) + events)[0] if events else value


class Links:
    def __init__(self, groups):
        self.groups = groups
        self.z_bits = [f"z{i}" for i in range(groups.bit_length() - 1)]
        self.near = self.z_bits[:-1] if len(self.z_bits) > 1 else []
        self.cargo = []

    def load(self, *trips):
        self.cargo += [(trip, next(trip)) for trip in trips]

    def ship(self):
        trip, (value, step) = self.cargo.pop(0)
        return trip, self.ring(value, step)

    def land(self, trip, came):
        try:
            self.cargo.insert(min(1, len(self.cargo)), (trip, trip.send(came)))
        except StopIteration:
            pass

    def ride(self, value, count=1):
        sent = [self.ship() for _ in range(min(count, len(self.cargo)))]
        if sent:
            came = lax.optimization_barrier((value,) + tuple(c for _, c in sent))
            value = came[0]
            for (trip, _), c in zip(sent, came[1:]):
                self.land(trip, c)
        return value

    def unload(self):
        while self.cargo:
            self.land(*self.ship())

    def swap(self, value, bit):
        if bit[0] == "z":
            step = 1 << int(bit[1:])
            return lax.ppermute(value, "z", [(i, i ^ step) for i in range(self.groups)])
        return lax.ppermute(value, bit, [(0, 1), (1, 0)])

    def swap_by_core(self, value, bits):
        chips = 4 * self.groups
        masks = {"x": 1, "y": 2}
        for i, bit in enumerate(self.z_bits):
            masks[bit] = 4 << i
        pairs = [(c * chips + k, c * chips + (k ^ masks[bits[c]])) for c in range(2) for k in range(chips)]
        return lax.ppermute(value, ("c", "z", "y", "x"), pairs)

    def ring(self, value, step):
        n = self.groups
        return lax.ppermute(value, "z", [(i, (i + step) % n) for i in range(n)])

    def plane_gather(self, own, rides=(0, 0)):
        first = self.ride(self.swap_by_core(own, "xy"), rides[0])
        pair = jnp.concatenate([own, first], 0)
        second = self.ride(self.swap_by_core(pair, "yx"), rides[1])
        mine = jnp.concatenate([pair, second], 0)
        return jnp.concatenate([mine, self.swap(mine, "c")], 0)

    def plane_scatter(self, part_of, rides=(0, 0)):
        total = self.swap(part_of(4, 8).astype(BF), "c").astype(F32) + part_of(0, 4)
        rows = total.shape[0] // 4
        far = self.ride(self.swap_by_core(total[2 * rows :].astype(BF), "yx"), rides[0]).astype(F32)
        near = (total[rows : 2 * rows] + far[rows:]).astype(BF)
        near = self.ride(self.swap_by_core(near, "xy"), rides[1]).astype(F32)
        return total[:rows] + far[:rows] + near

    def orders(self):
        return [self.near + ["x", "y"], self.near + ["y", "x"]]

    def sequence_gather(self, part, rides=0):
        for bits in zip(*self.orders()):
            came = self.swap_by_core(part, bits)
            if bits[0][0] != "z":
                came = self.ride(came, rides)
            part = jnp.concatenate([part, came], 0)
        return jnp.concatenate([part, self.swap(part, "c")], 0)

    def sequence_scatter(self, part, rides=0):
        rows = part.shape[0] // 2
        part = part[:rows].astype(F32) + self.swap(part[rows:], "c").astype(F32)
        for bits in list(zip(*self.orders()))[::-1]:
            rows = part.shape[0] // 2
            came = self.swap_by_core(part[rows:].astype(BF), bits)
            if bits[0][0] != "z":
                came = self.ride(came, rides)
            part = part[:rows] + came.astype(F32)
        return part

    def owner_orders(self):
        return [["x", "y"] + self.z_bits, ["y", "x"] + self.z_bits]

    def owner_scatter(self, keep, send, rides=0):
        part = keep.astype(F32) + self.swap(send, "c").astype(F32)
        stages = [part]
        for bits in zip(*self.owner_orders()):
            rows = part.shape[1] // 2
            came = self.swap_by_core(part[:, rows:].astype(BF), bits)
            if bits[0][0] != "z":
                came = self.ride(came, rides)
            part = part[:, :rows] + came.astype(F32)
            stages.append(part)
        return stages

    def total(self, value, rows_high):
        for bit in ["c", "x", "y"] + self.z_bits:
            value = value + self.swap(value, bit)
        return lax.psum(value, "rh") if rows_high > 1 else value


def step(
    shape,
    source_bytes,
    decoder_bytes,
    target_bytes,
    target_keep,
    source_length,
    target_length,
    language,
    step_count,
    attn_weights,
    attn_first,
    attn_second,
    feed_weights,
    feed_first,
    feed_second,
    table_weights,
    table_first,
    table_second,
    norm_gain_stack,
    gain_first,
    gain_second,
):
    rows_high, groups = shape
    rows_n, cols_n = 2 * rows_high, 4 * groups
    links = Links(groups)
    core, zc, yc, xc = (lax.axis_index(a) for a in ("c", "z", "y", "x"))
    on_first = core == 0
    tokens = source_bytes.shape[1]
    chunk = attn_weights.shape[2]
    width = attn_weights.shape[3]
    everywhere = ("rh", "c", "z", "y", "x")

    def own_half(value):
        return jnp.where(on_first, value[..., :HALF], value[..., HALF:])

    def other_half(value):
        return jnp.where(on_first, value[..., HALF:], value[..., :HALF])

    def in_order(own, other, axis):
        return jnp.concatenate(
            [jnp.where(on_first, own, other), jnp.where(on_first, other, own)], axis
        )

    def widen(value):
        pad = [(0, 0)] * (value.ndim - 1) + [(0, HALF - value.shape[-1])]
        return jnp.pad(value, pad)

    def spread_features(value):
        split = value.reshape(value.shape[0], rows_high, 2, chunk).transpose(0, 2, 1, 3)
        return widen(split.reshape(value.shape[0], 2, D // 2)).reshape(value.shape[0], WIDE)

    def join_features(value):
        if rows_high == 1:
            return jnp.concatenate([value[:, : D // 2], value[:, HALF : HALF + D // 2]], 1)
        split = value.reshape(value.shape[0], 2, HALF)[:, :, : D // 2]
        split = split.reshape(value.shape[0], 2, rows_high, chunk).transpose(0, 2, 1, 3)
        return split.reshape(value.shape[0], D)

    half = groups // 2
    packed = jnp.concatenate(
        [source_bytes, decoder_bytes, target_bytes, target_keep]
        + [
            jnp.broadcast_to(v[:, None], (1, tokens))
            for v in (source_length, target_length, language, language)
        ],
        0,
    )
    pairs = []
    for c in range(2):
        for k in range(cols_n):
            block = (((k // 4) % half) * 4 + k % 4) * 2 + c
            pairs.append(((k // 4 // half) * cols_n + block, c * cols_n + k))
    packed = lax.ppermute(packed, ("c", "z", "y", "x"), pairs)
    block = (((zc % half) * 2 + yc) * 2 + xc) * 2 + core
    first_pos = block * tokens
    src_limit, tgt_limit, tongue = packed[4, 0], packed[5, 0], packed[6, 0]
    positions = first_pos + jnp.arange(tokens, dtype=jnp.int32)
    weight = ((positions < tgt_limit) & (packed[3] > 0)).astype(F32)
    member = (tongue == jnp.arange(LANES, dtype=jnp.int32)).astype(F32)
    bit_value = {"c": 1, "x": 2, "y": 4}
    for i, bit in enumerate(links.near):
        bit_value[bit] = 8 << i
    masks = []
    for order in links.orders():
        mask = [0]
        for bit in order:
            mask = mask + [m ^ bit_value[bit] for m in mask]
        masks.append(mask)
    masks = np.array([masks[c] + [m ^ 1 for m in masks[1 - c]] for c in range(2)], np.int32)
    firsts = (jnp.where(on_first, masks[0], masks[1]) ^ block) * tokens

    def places(limit):
        return jnp.concatenate([firsts, jnp.stack([limit, first_pos]).astype(jnp.int32)])

    src_places, tgt_places = places(src_limit), places(tgt_limit)

    attn_t = attn_weights.transpose(0, 1, 3, 2)
    table_t = table_weights.transpose(0, 2, 1)

    def gather_tiles(tiles):
        tiles = tiles.astype(BF)
        if rows_high == 1 and tiles.shape[2] < HALF:
            tiles = widen(tiles)
        full = lax.all_gather(tiles[:, None], everywhere, axis=1, tiled=True)
        if rows_high == 1:
            return full.reshape(tiles.shape[0], 2, INNER, HALF)
        full = full.reshape(tiles.shape[0], rows_high, 2, INNER, chunk).transpose(0, 2, 3, 1, 4)
        return widen(full.reshape(tiles.shape[0], 2, INNER, D // 2))

    early_tiles = jnp.concatenate([attn_t[0], table_t[:1]], 0)
    own_counts = (member * jnp.sum(weight))[: HALF - D // 2]
    if rows_high == 1:
        lane_row = jnp.pad(own_counts, (D // 2, 0))[None, None]
        place = lax.broadcasted_iota(jnp.int32, (5, width, 1), 0) + lax.broadcasted_iota(jnp.int32, (5, width, 1), 1)
        early = gather_tiles(widen(early_tiles) + jnp.where(place == 0, lane_row, 0.0))
        counts = jnp.sum(early[0, :, ::width, D // 2 :].astype(F32), axis=(0, 1))
    else:
        early = gather_tiles(early_tiles)
        counts = lax.psum(own_counts, everywhere)
    inverse = 1.0 / (NLANG * jnp.maximum(counts, 1.0))
    token_scale = weight * jnp.sum(member[: HALF - D // 2] * inverse)

    def project(value, matrix):
        return dot_nt(value[:, :HALF], matrix[0]) + dot_nt(value[:, HALF:], matrix[1])

    def unproject(value, matrix):
        return jnp.concatenate([dot_nn(value, matrix[0]), dot_nn(value, matrix[1])], 1)

    hid = FF // cols_n
    hid_half = hid // 2
    period_rows = PERIOD // hid
    period_groups = chunk // period_rows
    lanes_own = HALF if rows_high == 1 else chunk
    shape3 = (period_rows, period_groups, lanes_own)
    spread = (
        lax.broadcasted_iota(jnp.int32, shape3, 2)
        == lax.broadcasted_iota(jnp.int32, shape3, 1) * period_rows
        + lax.broadcasted_iota(jnp.int32, shape3, 0)
    ).astype(BF)
    flat_shape = (6, chunk * hid // LANES, LANES)
    feed_t = unflatten(feed_weights.reshape(flat_shape), spread, hid, period_groups)
    if rows_high > 1:
        feed_t = lax.all_gather(feed_t[None], "rh", axis=0, tiled=True)
        feed_t = widen(feed_t.transpose(1, 2, 0, 3).reshape(6, hid, D // 2))

    def halves_joined(mine):
        keep = jnp.where(on_first, mine[:, :hid_half], mine[:, hid_half:])
        send = jnp.where(on_first, mine[:, hid_half:], mine[:, :hid_half])
        return in_order(keep, links.swap(send, "c"), 2)

    def gather_trip(own, out):
        held = [own]
        for _ in range(groups - 1):
            held.append((yield held[-1], 1))
        out.append(jnp.concatenate(held, 0))

    def scatter_trip(grads, out):
        grads = grads.reshape(groups, hid_half, WIDE)
        value = grads[groups - 1]
        for s in range(groups - 2, -1, -1):
            came = yield value.astype(BF), -1
            value = grads[s].astype(F32) + came.astype(F32)
        out.append(value)

    def collect(outs):
        links.unload()
        return [o[0] for o in outs]

    def to_rows(value):
        keep, send = own_half(value).astype(F32), other_half(value).astype(BF)
        full = in_order(keep, links.swap(send, "c").astype(F32), 1)
        if rows_high > 1:
            full = full[:, :, : D // 2].reshape(3, hid, rows_high, chunk)
            full = lax.psum_scatter(full, "rh", scatter_dimension=2, tiled=True)
            full = full.reshape(3, hid, chunk)
        return full

    late = gather_tiles(jnp.concatenate([attn_t[1], attn_t[2], table_t[1:]], 0))
    weights = [early[:4], late[:4], late[4:8]]
    head_w = late[8]
    own_enc, own_dec = halves_joined(feed_t[:3]), halves_joined(feed_t[3:])
    feed_enc, feed_dec = [[], [], []], [[], [], []]
    links.load(*(gather_trip(own_enc[m], feed_enc[m]) for m in range(3)))
    gains = spread_features(norm_gain_stack)

    def norm(stream, index):
        scale = rms_scale(stream)
        return (stream * scale * gains[index]).astype(BF), scale

    def attention(normed_q, normed_kv, matrices, where, causal, rides):
        queries = project(normed_q, matrices[0]).astype(BF)
        kv = jnp.concatenate([project(normed_kv, matrices[1]), project(normed_kv, matrices[2])], 1)
        kv = links.sequence_gather(kv.astype(BF), rides)
        context = attend(where, queries, kv, causal)
        return unproject(context, matrices[3]), (queries, kv, context)

    def eighths(left, right):
        rows = left[0].shape[0] // 8

        def part_of(first, last):
            at = slice(first * rows, last * rows)
            terms = [dot_nn(a[at], b) for a, b in zip(left, right)]
            return functools.reduce(jnp.add, terms)

        return part_of

    def feed(normed, outs, after=()):
        everyone = links.plane_gather(normed, (1, 1))
        matrices = collect(outs)
        links.load(*after)
        gate = dot_nt(everyone, matrices[0])
        upper = dot_nt(everyone, matrices[1])
        hidden = gated_units(gate, upper).astype(BF)
        out = links.plane_scatter(eighths([hidden], [matrices[2]]), (1, 1))
        return out, (everyone, gate, upper, hidden), matrices

    vocab_ids = jnp.arange(INNER, dtype=jnp.int32)
    src_hot = (packed[0][:, None] == vocab_ids).astype(BF)
    dec_hot = (packed[1][:, None] == vocab_ids).astype(BF)
    embed_w = early[4]
    enc_zero = unproject(src_hot, embed_w)
    dec_zero = unproject(dec_hot, embed_w)
    n_zero, s_zero = norm(links.ride(enc_zero, 2), 0)
    branch, kept_enc = attention(n_zero, n_zero, early[:4], src_places, False, 2)
    enc_one = enc_zero + branch
    n_one, s_one = norm(enc_one, 1)
    branch, kept_enc_feed, feed_enc = feed(
        n_one, feed_enc, (gather_trip(own_dec[m], feed_dec[m]) for m in range(3))
    )
    enc_two = enc_one + branch
    memory, s_two = norm(enc_two, 2)
    n_three, s_three = norm(dec_zero, 3)
    branch, kept_dec = attention(n_three, n_three, weights[1], tgt_places, True, 1)
    dec_one = dec_zero + branch
    n_four, s_four = norm(dec_one, 4)
    branch, kept_cross = attention(n_four, memory, weights[2], src_places, False, 1)
    dec_two = dec_one + branch
    n_five, s_five = norm(dec_two, 5)
    branch, kept_dec_feed, feed_dec = feed(n_five, feed_dec)
    dec_three = dec_two + branch
    final, s_six = norm(dec_three, 6)

    logits = project(final, head_w)
    lse = jax.nn.logsumexp(logits, axis=-1)
    target_hot = (packed[2][:, None] == vocab_ids).astype(F32)
    picked = jnp.sum(logits * target_hot, axis=-1)
    loss_local = jnp.sum((lse - picked) * token_scale)
    grad_logits = ((jnp.exp(logits - lse[:, None]) - target_hot) * token_scale[:, None]).astype(BF)

    own_index = zc * 4 + yc * 2 + xc
    place = {"x": 1, "y": 2}
    for i, bit in enumerate(links.z_bits):
        place[bit] = 4 << i
    relative_masks = []
    for order in links.owner_orders():
        mask = [0]
        for bit in order[::-1]:
            mask = mask + [m ^ place[bit] for m in mask]
        relative_masks.append(np.repeat(np.array(mask, np.int32), width))
    columns = jnp.arange(INNER, dtype=jnp.int32)

    def shuffle_to(mask):
        moved = (mask ^ own_index) * width + columns % width
        return (columns[:, None] == moved[None, :]).astype(BF)

    to_own = shuffle_to(jnp.where(on_first, relative_masks[0], relative_masks[1]))
    to_other = shuffle_to(jnp.where(on_first, relative_masks[1], relative_masks[0]))

    def owner_grads(pairs, rides=0):
        tokens_n = max(p[0].shape[0] for p in pairs)

        def filled(value):
            return jnp.pad(value, ((0, tokens_n - value.shape[0]), (0, 0)))

        cols = jnp.concatenate([filled(p[0]) for p in pairs], 0)
        batch = (((1,), (1,)), ((0,), (0,)))

        def products(shuffle, half_of):
            moved = dot_nn(cols, shuffle).astype(BF).reshape(len(pairs), tokens_n, INNER)
            feats = jnp.stack([filled(half_of(p[1])) for p in pairs])
            return lax.dot_general(moved, feats, batch, preferred_element_type=F32).astype(BF)

        return links.owner_scatter(products(to_own, own_half), products(to_other, other_half), rides)

    def feed_back(kept, matrices, grad, events=((), ()), rides=((0, 0), (0, 0))):
        everyone, gate, upper, hidden = kept
        grad_all = anchor(links.plane_gather(grad.astype(BF), rides[0]), *events[0])
        _, pull = jax.vjp(gated_units, gate, upper)
        grad_gate, grad_upper = pull(dot_nt(grad_all, matrices[2]))
        gate_b, upper_b = grad_gate.astype(BF), grad_upper.astype(BF)
        grad_normed = anchor(links.plane_scatter(eighths([gate_b, upper_b], matrices[:2]), rides[1]), *events[1])
        grads = [
            dot_tn(gate_b, everyone).astype(BF),
            dot_tn(upper_b, everyone).astype(BF),
            dot_tn(hidden, grad_all).astype(BF),
        ]
        return grad_normed, grads

    def attention_back(kept, normed_q, normed_kv, matrices, where, causal, grad, rides=0, events=((), ())):
        queries, kv, context = kept
        grad_b = grad.astype(BF)
        grad_context = anchor(project(grad_b, matrices[3]).astype(BF), *events[0])
        d_query, d_kv = attend_back(where, queries, grad_context, kv, causal)
        d_kv = anchor(d_kv, *events[1])
        d_kv_own = links.sequence_scatter(d_kv, rides).astype(BF)
        d_key, d_value = d_kv_own[:, :INNER], d_kv_own[:, INNER:]
        d_normed_q = unproject(d_query, matrices[0])
        d_normed_kv = unproject(d_key, matrices[1]) + unproject(d_value, matrices[2])
        pairs = [(d_query, normed_q), (d_key, normed_kv), (d_value, normed_kv), (context, grad_b)]
        return d_normed_q, d_normed_kv, pairs

    grad_final = unproject(grad_logits, head_w)
    grad_dec, gain_six = rms_reverse(dec_three, gains[6], s_six, grad_final)
    grad_normed, feed_dec_grad = feed_back(kept_dec_feed, feed_dec, grad_dec)
    part, gain_five = rms_reverse(dec_two, gains[5], s_five, grad_normed)
    grad_dec = grad_dec + part
    dec_feed, enc_feed = [[], [], []], [[], [], []]
    links.load(*(scatter_trip(feed_dec_grad[m], dec_feed[m]) for m in range(3)))
    d_q, grad_memory, cross_grad = attention_back(
        kept_cross, n_four, memory, weights[2], src_places, False, grad_dec, 2
    )
    cross_stages = owner_grads(cross_grad + [(grad_logits, final)])
    part, gain_four = rms_reverse(dec_one, gains[4], s_four, d_q)
    grad_dec = grad_dec + part
    d_q, d_kv, dec_grad = attention_back(
        kept_dec, n_three, n_three, weights[1], tgt_places, True, grad_dec
    )
    dec_stages = owner_grads(dec_grad)
    part, gain_three = rms_reverse(dec_zero, gains[3], s_three, d_q + d_kv)
    grad_dec = grad_dec + part
    grad_enc, gain_two = rms_reverse(enc_two, gains[2], s_two, grad_memory)
    grad_normed, feed_enc_grad = feed_back(
        kept_enc_feed, feed_enc, grad_enc, ((cross_stages[0],), (cross_stages[1], dec_stages[0])), ((1, 1), (2, 1))
    )
    part, gain_one = rms_reverse(enc_one, gains[1], s_one, grad_normed)
    grad_enc = grad_enc + part
    links.unload()
    dec_rows = to_rows(jnp.stack([o[0] for o in dec_feed]))
    dec_flat = flatten(dec_rows, spread, hid, period_groups)
    links.load(*(scatter_trip(feed_enc_grad[m], enc_feed[m]) for m in range(3)))
    d_q, d_kv, enc_grad = attention_back(
        kept_enc, n_zero, n_zero, weights[0], src_places, False, grad_enc, 2,
        ((cross_stages[2], dec_stages[1]), (cross_stages[3], dec_stages[2], dec_flat)),
    )
    part, gain_zero = rms_reverse(enc_zero, gains[0], s_zero, d_q + d_kv)
    grad_enc = grad_enc + part
    embed_pair = (
        jnp.concatenate([src_hot, dec_hot], 0),
        jnp.concatenate([grad_enc, grad_dec], 0).astype(BF),
    )

    early_stages = owner_grads(enc_grad + [embed_pair], 2)
    links.unload()

    def own_chunk(value):
        if rows_high > 1:
            value = value[:, :, : D // 2].reshape(value.shape[0], width, rows_high, chunk)
            value = lax.psum_scatter(value, "rh", scatter_dimension=2, tiled=True)
            value = value.reshape(value.shape[0], width, chunk)
        return value

    enc_rows = to_rows(jnp.stack([o[0] for o in enc_feed]))
    enc_flat = flatten(enc_rows, spread, hid, period_groups)
    early_red = own_chunk(early_stages[-1])
    dec_red, cross_red = own_chunk(dec_stages[-1]), own_chunk(cross_stages[-1])
    square_local = functools.reduce(
        jnp.add, [jnp.sum(v * v) for v in (early_red, dec_red, cross_red, enc_rows, dec_rows)]
    )
    lane = jnp.arange(WIDE)
    extra = jnp.where(lane == 0, square_local, 0.0) + jnp.where(lane == 1, loss_local, 0.0)
    gain_local = jnp.stack(
        [gain_zero, gain_one, gain_two, gain_three, gain_four, gain_five, gain_six, extra]
    )
    gain_local = anchor(gain_local, enc_flat, dec_flat)
    everything = links.total(gain_local, rows_high)
    loss = everything[7, 1]
    grad_norm = jnp.sqrt(everything[7, 0] + jnp.sum(everything[:7] * everything[:7]))
    count = step_count[0].astype(F32)
    scalars = jnp.stack([1.0 / (1.0 - BETA_FIRST**count), 1.0 / (1.0 - BETA_SECOND**count)])
    slot_total = tokens * cols_n

    def attn_turn(value):
        return value.transpose(0, 1, 3, 2).reshape(12, width, chunk)

    def attn_return(value):
        return value.reshape(3, 4, width, chunk).transpose(0, 1, 3, 2)

    def table_turn(value):
        return value.transpose(0, 2, 1)

    new = finish(
        (slot_total / (3.0 * INNER)) ** 0.5,
        scalars,
        everything,
        (enc_flat, dec_flat),
        (early_red, dec_red, cross_red, join_features(everything[:7])),
        tuple(v.reshape(flat_shape) for v in (feed_weights, feed_first, feed_second)),
        tuple(attn_turn(v) for v in (attn_weights, attn_first, attn_second)),
        tuple(table_turn(v) for v in (table_weights, table_first, table_second)),
        (norm_gain_stack, gain_first, gain_second),
    )
    return (
        (loss, grad_norm)
        + tuple(attn_return(v) for v in new[3:6])
        + tuple(v.reshape(feed_weights.shape) for v in new[:3])
        + tuple(table_turn(v) for v in new[6:9])
        + tuple(new[9:])
    )


def solution(mesh):
    rows_high = mesh.shape["row"] // 2
    groups = mesh.shape["col"] // 4
    split = Mesh(mesh.devices.reshape(rows_high, 2, groups, 2, 2), ("rh", "c", "z", "y", "x"))
    row, col = ("rh", "c"), ("z", "y", "x")
    attn = P(None, None, row, col)
    feed = P(None, None, col, row)
    table = P(None, row, col)
    ids = P(row, col)
    in_specs = (ids,) * 4 + (P(row),) * 3 + (P(),) + (attn,) * 3 + (feed,) * 3 + (table,) * 3 + (P(),) * 3
    out_specs = (P(), P()) + (attn,) * 3 + (feed,) * 3 + (table,) * 3 + (P(),) * 3
    return jax.shard_map(
        functools.partial(step, (rows_high, groups)),
        mesh=split,
        in_specs=in_specs,
        out_specs=out_specs,
        check_vma=False,
    )
```

time: 948 us -> 875 us (0.923)
  starting transfers between devices: 150 us -> 93.6 us
  local copies, waits for them, and re-layouts: 80.2 us -> 49.8 us
  other arithmetic: 80.7 us -> 61.2 us
  Pallas kernels: 60.2 us -> 77.9 us
  waiting for transfers between devices: 452 us -> 462 us
    ppermute x16 -> x46, waiting for transfers between devices: 63 us -> 169 us  [swap_by_core(): return lax.ppermute(value, ('c', 'z', 'y', 'x'), pairs)]
    ppermute x34 -> x2, waiting for transfers between devices: 96.2 us -> 7.02 us  [swap(): return lax.ppermute(value, 'z', [(i, i ^ step) for i in range(self.groups)])]
    ppermute x93 -> x24, starting transfers between devices: 74.7 us -> 10.1 us  [swap(): return lax.ppermute(value, bit, [(0, 1), (1, 0)])]
    ppermute x93 -> x24, waiting for transfers between devices: 72 us -> 23 us  [swap(): return lax.ppermute(value, bit, [(0, 1), (1, 0)])]
    ppermute x12 -> x36, waiting for transfers between devices: 170 us -> 210 us  [ring(): return lax.ppermute(value, 'z', [(i, (i + step) % n) for i in range(n)])]
    ppermute x16 -> x46, starting transfers between devices: 20.1 us -> 52.1 us  [swap_by_core(): return lax.ppermute(value, ('c', 'z', 'y', 'x'), pairs)]
    ppermute x34 -> x2, starting transfers between devices: 31.4 us -> 0.78 us  [swap(): return lax.ppermute(value, 'z', [(i, i ^ step) for i in range(self.groups)])]
    dot_general x24 -> x6, matrix products: 31.9 us -> 11.8 us  [dot_tn(): lax.dot_general(a, b, (((0,), (0,)), ((), ())), preferred_element_type=F32)]
  transfers between devices with their start and end apart: 158 -> 111, of which waited for: 74 -> 65; matrix products, arithmetic and copies ran while one was open for 17% -> 17% of each run, Pallas kernels for 6% -> 5%
where the time goes in v2:
time: 875 us; the launch traced here: 865 us
  waiting for transfers between devices  462 us (53%)
  starting transfers between devices  93.6 us (11%)
  matrix products  92.7 us (11%)
  Pallas kernels  77.9 us (9%)
  other arithmetic  61.2 us (7%)
  local copies, waits for them, and re-layouts  49.8 us (6%)
  between operations  28 us (3%)
    ppermute x36, waiting for transfers between devices, ring(): return lax.ppermute(value, 'z', [(i, (i + step) % n) for i in range(n)])  210 us
    ppermute x46, waiting for transfers between devices, swap_by_core(): return lax.ppermute(value, ('c', 'z', 'y', 'x'), pairs)  169 us
    all_gather x2, waiting for transfers between devices, gather_tiles(): full = lax.all_gather(tiles[:, None], everywhere, axis=1, tiled=True)  52.5 us
    ppermute x46, starting transfers between devices, swap_by_core(): return lax.ppermute(value, ('c', 'z', 'y', 'x'), pairs)  52.1 us
    dot_general x32, matrix products, dot_nt(): lax.dot_general(a, b, (((1,), (1,)), ((), ())), preferred_element_type=F32)  37.7 us
    dot_general x48, matrix products, dot_nn(): lax.dot_general(a, b, (((1,), (0,)), ((), ())), preferred_element_type=F32)  37.6 us
    pallas_call x3, Pallas kernels, attend_back(): pl.pallas_call(functools.partial(attend_back_kernel, causal), out_shape=(...  31.6 us
    ppermute x36, starting transfers between devices, ring(): return lax.ppermute(value, 'z', [(i, (i + step) % n) for i in range(n)])  29.8 us
  transfers between devices with their start and end apart: 111, of which 65 were waited for; matrix products, arithmetic and copies ran while one was open for 17% of the time, Pallas kernels for 5%

profile of v2, /device:TPU:0, one launch (start us, length us, event | category | flops | bytes accessed | tf_op | source)
XLA Modules:
  0.0 865.2 jit_solution(7385639201970099884)
XLA Ops:
  28.0 5.5 collective-permute-start.20
  41.9 52.5 %all-gather.5.cloned.1.call-done = bf16[5,768,768]{2,1,0:T(8,128)(2,1)} async-done(((bf16[5,24,768]{2,1,0:T(8,128)(2,1)}), bf16[5,768,768]{2,1,0:T(8,128)(2,1)}) %all-gather.5.cloned.1.call-update) | async-done | bytes 5898256 | tf_op jit(solution)/shard_map/all_gather | solution.py:571
  104.3 8.3 collective-permute-done.4
  116.5 10.8 %collective-permute-done.6 = bf16[112,1536]{1,0:T(8,128)(2,1)S(1)} collective-permute-done((bf16[112,1536]{1,0:T(8,128)(2,1)S(1)}, bf16[112,1536]{1,0:T(8,128)(2,1)S(1)}, u32[]{:S(2)}, u32[]{:S(2)}) %collective-permute-start.6) | collective-permute-done | bytes 344096 | tf_op jit(solution)/shard_map/ppermute | solution.py:407
  127.3 6.2 collective-permute-done.7
  136.3 18.8 %collective-permute-done.9 = bf16[112,1536]{1,0:T(8,128)(2,1)S(1)} collective-permute-done((bf16[112,1536]{1,0:T(8,128)(2,1)S(1)}, bf16[112,1536]{1,0:T(8,128)(2,1)S(1)}, u32[]{:S(2)}, u32[]{:S(2)}) %collective-permute-start.9) | collective-permute-done | bytes 344096 | tf_op jit(solution)/shard_map/ppermute | solution.py:407
  155.0 11.9 %collective-permute-done.10 = bf16[112,1536]{1,0:T(8,128)(2,1)S(1)} collective-permute-done((bf16[112,1536]{1,0:T(8,128)(2,1)S(1)}, bf16[112,1536]{1,0:T(8,128)(2,1)S(1)}, u32[]{:S(2)}, u32[]{:S(2)}) %collective-permute-start.10) | collective-permute-done | bytes 344096 | tf_op jit(solution)/shard_map/ppermute | solution.py:407
  185.4 15.9 %collective-permute-done.13 = bf16[112,1536]{1,0:T(8,128)(2,1)S(1)} collective-permute-done((bf16[112,1536]{1,0:T(8,128)(2,1)S(1)}, bf16[112,1536]{1,0:T(8,128)(2,1)S(1)}, u32[]{:S(2)}, u32[]{:S(2)}) %collective-permute-start.13) | collective-permute-done | bytes 344096 | tf_op jit(solution)/shard_map/ppermute | solution.py:407
  204.0 13.6 %collective-permute-done.15 = bf16[112,1536]{1,0:T(8,128)(2,1)S(1)} collective-permute-done((bf16[112,1536]{1,0:T(8,128)(2,1)S(1)}, bf16[112,1536]{1,0:T(8,128)(2,1)S(1)}, u32[]{:S(2)}, u32[]{:S(2)}) %collective-permute-start.15) | collective-permute-done | bytes 344096 | tf_op jit(solution)/shard_map/ppermute | solution.py:407
  241.9 11.5 %collective-permute-done.21 = bf16[112,1536]{1,0:T(8,128)(2,1)} collective-permute-done((bf16[112,1536]{1,0:T(8,128)(2,1)S(1)}, bf16[112,1536]{1,0:T(8,128)(2,1)}, u32[]{:S(2)}, u32[]{:S(2)}) %collective-permute-start.21) | collective-permute-done | bytes 344096 | tf_op jit(solution)/shard_map/ppermute | solution.py:407
  263.3 6.9 fusion.212
  272.1 6.5 collective-permute-done.24
  279.9 6.5 collective-permute-done.25
  289.5 5.7 collective-permute-done.30
  315.2 11.6 %collective-permute-done.34 = bf16[112,1536]{1,0:T(8,128)(2,1)S(1)} collective-permute-done((bf16[112,1536]{1,0:T(8,128)(2,1)}, bf16[112,1536]{1,0:T(8,128)(2,1)S(1)}, u32[]{:S(2)}, u32[]{:S(2)}) %collective-permute-start.34) | collective-permute-done | bytes 344096 | tf_op jit(solution)/shard_map/ppermute | solution.py:407
  329.9 5.1 attend.4
  345.0 12.3 %collective-permute-done.37 = bf16[112,1536]{1,0:T(8,128)(2,1)S(1)} collective-permute-done((bf16[112,1536]{1,0:T(8,128)(2,1)S(1)}, bf16[112,1536]{1,0:T(8,128)(2,1)S(1)}, u32[]{:S(2)}, u32[]{:S(2)}) %collective-permute-start.37) | collective-permute-done | bytes 344096 | tf_op jit(solution)/shard_map/ppermute | solution.py:407
  358.7 11.0 %collective-permute-done.39 = bf16[112,1536]{1,0:T(8,128)(2,1)S(1)} collective-permute-done((bf16[112,1536]{1,0:T(8,128)(2,1)S(1)}, bf16[112,1536]{1,0:T(8,128)(2,1)S(1)}, u32[]{:S(2)}, u32[]{:S(2)}) %collective-permute-start.39) | collective-permute-done | bytes 344096 | tf_op jit(solution)/shard_map/ppermute | solution.py:407
  389.0 11.0 %collective-permute-done.43 = bf16[256,1536]{1,0:T(8,128)(2,1)S(1)} collective-permute-done((bf16[256,1536]{1,0:T(8,128)(2,1)S(1)}, bf16[256,1536]{1,0:T(8,128)(2,1)S(1)}, u32[]{:S(2)}, u32[]{:S(2)}) %collective-permute-start.43) | collective-permute-done | bytes 786464 | tf_op jit(solution)/shard_map/ppermute | solution.py:403
  418.2 6.3 collective-permute-done.45
  425.6 11.0 %collective-permute-done.46 = bf16[256,1536]{1,0:T(8,128)(2,1)S(1)} collective-permute-done((bf16[256,1536]{1,0:T(8,128)(2,1)S(1)}, bf16[256,1536]{1,0:T(8,128)(2,1)S(1)}, u32[]{:S(2)}, u32[]{:S(2)}) %collective-permute-start.46) | collective-permute-done | bytes 786464 | tf_op jit(solution)/shard_map/ppermute | solution.py:403
  442.5 5.3 multiply_convert_fusion.1
  464.7 6.0 collective-permute-done.49
  482.0 10.5 %attend_back.3 = (bf16[128,384]{1,0:T(8,128)(2,1)S(1)}, bf16[2048,768]{1,0:T(8,128)(2,1)S(1)}) custom-call(s32[18]{0:T(128)S(1)} %get-tuple-element.365.where_ref, bf16[128,384]{1,0:T(8,128)(2,1)S(1)} %fusion.23.q_ref, bf16[128,384]{1,0:T(8,128)(2,1)S(1)} %fusion.26.g_ref, bf16[2048,768]{1,0:T(8,128)(2,1)S(1)} %copy-done.9), custom_call_target="tpu_custom_call" | custom-call | flops 2013265920 | bytes 6291456 | tf_op jit(solution)/shard_map/attend_back/pallas_call | solution.py:311
  496.3 10.7 %attend_back.4 = (bf16[128,384]{1,0:T(8,128)(2,1)S(1)}, bf16[2048,768]{1,0:T(8,128)(2,1)S(1)}) custom-call(s32[18]{0:T(128)S(1)} %get-tuple-element.364.where_ref, bf16[128,384]{1,0:T(8,128)(2,1)S(1)} %fusion.20.q_ref, bf16[128,384]{1,0:T(8,128)(2,1)S(1)} %fusion.27.g_ref, bf16[2048,768]{1,0:T(8,128)(2,1)S(1)} %constant_dynamic-update-slice_fusion.5.kv_ref), custom_call_target="tpu_custom_call" | custom-call | flops 2013265920 | bytes 6291456 | tf_op jit(solution)/shard_map/attend_back/pallas_call | solution.py:311
  512.1 8.7 %collective-permute-done.52 = bf16[512,768]{1,0:T(8,128)(2,1)S(1)} collective-permute-done((bf16[512,768]{1,0:T(8,128)(2,1)S(1)}, bf16[512,768]{1,0:T(8,128)(2,1)S(1)}, u32[]{:S(2)}, u32[]{:S(2)}) %collective-permute-start.52) | collective-permute-done | bytes 786464 | tf_op jit(solution)/shard_map/ppermute | solution.py:403
  522.7 10.7 %collective-permute-done.73 = bf16[512,768]{1,0:T(8,128)(2,1)S(1)} collective-permute-done((bf16[512,768]{1,0:T(8,128)(2,1)S(1)}, bf16[512,768]{1,0:T(8,128)(2,1)S(1)}, u32[]{:S(2)}, u32[]{:S(2)}) %collective-permute-start.73) | collective-permute-done | bytes 786464 | tf_op jit(solution)/shard_map/ppermute | solution.py:403
  541.7 7.5 collective-permute-done.58
  560.3 10.1 %collective-permute-done.62 = bf16[112,1536]{1,0:T(8,128)(2,1)S(1)} collective-permute-done((bf16[112,1536]{1,0:T(8,128)(2,1)S(1)}, bf16[112,1536]{1,0:T(8,128)(2,1)S(1)}, u32[]{:S(2)}, u32[]{:S(2)}) %collective-permute-start.62) | collective-permute-done | bytes 344096 | tf_op jit(solution)/shard_map/ppermute | solution.py:407
  578.0 6.4 multiply_convert_fusion
  595.9 16.8 %collective-permute-done.71 = bf16[5,192,768]{2,1,0:T(8,128)(2,1)S(1)} collective-permute-done((bf16[5,192,768]{2,1,0:T(8,128)(2,1)S(1)}, bf16[5,192,768]{2,1,0:T(8,128)(2,1)S(1)}, u32[]{:S(2)}, u32[]{:S(2)}) %collective-permute-start.71) | collective-permute-done | bytes 1474592 | tf_op jit(solution)/shard_map/ppermute | solution.py:403
  617.8 6.9 collective-permute-done.77
  625.2 7.9 collective-permute-done.66
  636.1 6.1 collective-permute-done.70
  646.0 10.5 %attend_back.5 = (bf16[128,384]{1,0:T(8,128)(2,1)S(1)}, bf16[2048,768]{1,0:T(8,128)(2,1)S(1)}) custom-call(s32[18]{0:T(128)S(1)} %get-tuple-element.365.where_ref, bf16[128,384]{1,0:T(8,128)(2,1)S(1)} %copy-done.13, bf16[128,384]{1,0:T(8,128)(2,1)S(1)} %fusion.28.g_ref, bf16[2048,768]{1,0:T(8,128)(2,1)S(1)} %copy-done.6), custom_call_target="tpu_custom_call" | custom-call | flops 2013265920 | bytes 6291456 | tf_op jit(solution)/shard_map/attend_back/pallas_call | solution.py:311
  658.1 5.1 flatten.2.dec_ref
  677.1 9.6 %collective-permute-done.85 = bf16[112,1536]{1,0:T(8,128)(2,1)S(1)} collective-permute-done((bf16[112,1536]{1,0:T(8,128)(2,1)S(1)}, bf16[112,1536]{1,0:T(8,128)(2,1)S(1)}, u32[]{:S(2)}, u32[]{:S(2)}) %collective-permute-start.85) | collective-permute-done | bytes 344096 | tf_op jit(solution)/shard_map/ppermute | solution.py:407
  686.7 6.1 collective-permute-done.84
  698.7 7.4 collective-permute-done.88
  706.6 5.4 collective-permute-done.89
  717.2 9.3 %collective-permute-done.99 = bf16[4,48,768]{2,1,0:T(8,128)(2,1)S(1)} collective-permute-done((bf16[4,48,768]{2,1,0:T(8,128)(2,1)S(1)}, bf16[4,48,768]{2,1,0:T(8,128)(2,1)S(1)}, u32[]{:S(2)}, u32[]{:S(2)}) %collective-permute-start.99) | collective-permute-done | bytes 294944 | tf_op jit(solution)/shard_map/ppermute | solution.py:403
  745.7 8.0 collective-permute-done.92
  753.7 7.4 collective-permute-done.93
  768.5 6.4 collective-permute-done.96
  779.9 8.8 %collective-permute-done.102 = bf16[112,1536]{1,0:T(8,128)(2,1)S(1)} collective-permute-done((bf16[112,1536]{1,0:T(8,128)(2,1)S(1)}, bf16[112,1536]{1,0:T(8,128)(2,1)S(1)}, u32[]{:S(2)}, u32[]{:S(2)}) %collective-permute-start.102) | collective-permute-done | bytes 344096 | tf_op jit(solution)/shard_map/ppermute | solution.py:407
  796.6 7.1 collective-permute-done.98
  809.4 5.1 flatten.3.enc_ref
  839.9 16.8 %finish.1 = (f32[6,1288,128]{2,1,0:T(8,128)}, f32[6,1288,128]{2,1,0:T(8,128)}, f32[6,1288,128]{2,1,0:T(8,128)}, f32[12,24,736]{2,1,0:T(8,128)}, f32[12,24,736]{2...) custom-call(f32[2]{0:T(128)} %pad_maximum_fusion.47.scal_ref, ...), custom_call_target="tpu_custom_call" | custom-call | tf_op jit(solution)/shard_map/finish/pallas_call | solution.py:188
  (1066 shorter events, 361.9 us)
Async XLA Ops:
  7.2 87.2 %all-gather.5.cloned.1.call-start = ((), (), s32[]{:S(2)}) async-start(), calls=%async_computation | async-start | bytes 6082560 | tf_op jit(solution)/shard_map/all_gather | solution.py:571
  17.1 246.2 %all-gather.7.cloned.1.call-start = ((), (), s32[]{:S(2)}) async-start(), calls=%async_computation.1 | async-start | bytes 10948608 | tf_op jit(solution)/shard_map/all_gather | solution.py:571
  39.1 60.4 %collective-permute-start.2 = (bf16[112,1536]{1,0:T(8,128)(2,1)S(1)}, bf16[112,1536]{1,0:T(8,128)(2,1)S(1)}, u32[]{:S(2)}, u32[]{:S(2)}) collective-permute-start(bf16[112,1536]{1,0:T(8,128)(2,1)S(1)} %get-tuple-element.299), channel_id=1, source_target_pairs={{0,4},{4,8},{8,12},{12,0},{1,5},{5,9},{9,13},{13,1},{2,6},{6,10},{... | collective-permute-start | bytes 1032200 | tf_op jit(solution)/shard_map/ppermute | solution.py:407
  40.6 58.9 %collective-permute-start.3 = (bf16[112,1536]{1,0:T(8,128)(2,1)S(1)}, bf16[112,1536]{1,0:T(8,128)(2,1)S(1)}, u32[]{:S(2)}, u32[]{:S(2)}) collective-permute-start(bf16[112,1536]{1,0:T(8,128)(2,1)S(1)} %get-tuple-element.300), channel_id=1, source_target_pairs={{0,4},{4,8},{8,12},{12,0},{1,5},{5,9},{9,13},{13,1},{2,6},{6,10},{... | collective-permute-start | bytes 1032200 | tf_op jit(solution)/shard_map/ppermute | solution.py:407
  112.7 20.9 %collective-permute-start.5 = (bf16[256,768]{1,0:T(8,128)(2,1)S(1)}, bf16[256,768]{1,0:T(8,128)(2,1)S(1)}, u32[]{:S(2)}, u32[]{:S(2)}) collective-permute-start(bf16[256,768]{1,0:T(8,128)(2,1)S(1)} %pad_maximum_fusion.35), channel_id=1, source_target_pairs={{0,1},{1,0},{2,3},{3,2},{4,5},{5,4},{6,7},{7,6},{8,9},{9,8},{10,11... | collective-permute-start | bytes 1179656 | tf_op jit(solution)/shard_map/ppermute | solution.py:403
  116.4 17.2 %collective-permute-start.7 = (bf16[112,1536]{1,0:T(8,128)(2,1)S(1)}, bf16[112,1536]{1,0:T(8,128)(2,1)S(1)}, u32[]{:S(2)}, u32[]{:S(2)}) collective-permute-start(bf16[112,1536]{1,0:T(8,128)(2,1)S(1)} %copy-done.219), channel_id=1, source_target_pairs={{0,4},{4,8},{8,12},{12,0},{1,5},{5,9},{9,13},{13,1},{2,6},{6,10},{... | collective-permute-start | bytes 1032200 | tf_op jit(solution)/shard_map/ppermute | solution.py:407
  133.6 34.1 %collective-permute-start.8 = (bf16[512,768]{1,0:T(8,128)(2,1)S(1)}, bf16[512,768]{1,0:T(8,128)(2,1)S(1)}, u32[]{:S(2)}, u32[]{:S(2)}) collective-permute-start(bf16[512,768]{1,0:T(8,128)(2,1)S(1)} %pad_maximum_fusion.22), channel_id=1, source_target_pairs={{0,2},{1,3},{2,0},{3,1},{4,6},{5,7},{6,4},{7,5},{8,10},{9,11},{10,... | collective-permute-start | bytes 2359304 | tf_op jit(solution)/shard_map/ppermute | solution.py:403
  134.9 20.2 %collective-permute-start.9 = (bf16[112,1536]{1,0:T(8,128)(2,1)S(1)}, bf16[112,1536]{1,0:T(8,128)(2,1)S(1)}, u32[]{:S(2)}, u32[]{:S(2)}) collective-permute-start(bf16[112,1536]{1,0:T(8,128)(2,1)S(1)} %copy-done.223), channel_id=1, source_target_pairs={{0,4},{4,8},{8,12},{12,0},{1,5},{5,9},{9,13},{13,1},{2,6},{6,10},{... | collective-permute-start | bytes 1032200 | tf_op jit(solution)/shard_map/ppermute | solution.py:407
  134.9 32.0 %collective-permute-start.10 = (bf16[112,1536]{1,0:T(8,128)(2,1)S(1)}, bf16[112,1536]{1,0:T(8,128)(2,1)S(1)}, u32[]{:S(2)}, u32[]{:S(2)}) collective-permute-start(bf16[112,1536]{1,0:T(8,128)(2,1)S(1)} %collective-permute-done.7), channel_id=1, source_target_pairs={{0,4},{4,8},{8,12},{12,0},{1,5},{5,9},{9,13},{13,1},{2,6},{6,10},{... | collective-permute-start | bytes 1032200 | tf_op jit(solution)/shard_map/ppermute | solution.py:407
  184.3 17.0 %collective-permute-start.12 = (bf16[128,1536]{1,0:T(8,128)(2,1)S(1)}, bf16[128,1536]{1,0:T(8,128)(2,1)S(1)}, u32[]{:S(2)}, u32[]{:S(2)}) collective-permute-start(bf16[128,1536]{1,0:T(8,128)(2,1)S(1)} %multiply_convert_fusion.9), channel_id=1, source_target_pairs={{0,1},{1,0},{2,3},{3,2},{4,5},{5,4},{6,7},{7,6},{8,9},{9,8},{10,11... | collective-permute-start | bytes 1179656 | tf_op jit(solution)/shard_map/ppermute | solution.py:403
  185.4 15.9 %collective-permute-start.13 = (bf16[112,1536]{1,0:T(8,128)(2,1)S(1)}, bf16[112,1536]{1,0:T(8,128)(2,1)S(1)}, u32[]{:S(2)}, u32[]{:S(2)}) collective-permute-start(bf16[112,1536]{1,0:T(8,128)(2,1)S(1)} %copy-done.233), channel_id=1, source_target_pairs={{0,4},{4,8},{8,12},{12,0},{1,5},{5,9},{9,13},{13,1},{2,6},{6,10},{... | collective-permute-start | bytes 1032200 | tf_op jit(solution)/shard_map/ppermute | solution.py:407
  201.4 16.2 %collective-permute-start.14 = (bf16[256,1536]{1,0:T(8,128)(2,1)S(1)}, bf16[256,1536]{1,0:T(8,128)(2,1)S(1)}, u32[]{:S(2)}, u32[]{:S(2)}) collective-permute-start(bf16[256,1536]{1,0:T(8,128)(2,1)S(1)} %pad_maximum_fusion.23), channel_id=1, source_target_pairs={{0,2},{1,3},{2,0},{3,1},{4,6},{5,7},{6,4},{7,5},{8,10},{9,11},{10,... | collective-permute-start | bytes 2359304 | tf_op jit(solution)/shard_map/ppermute | solution.py:403
  203.3 14.3 %collective-permute-start.15 = (bf16[112,1536]{1,0:T(8,128)(2,1)S(1)}, bf16[112,1536]{1,0:T(8,128)(2,1)S(1)}, u32[]{:S(2)}, u32[]{:S(2)}) collective-permute-start(bf16[112,1536]{1,0:T(8,128)(2,1)S(1)} %copy-done.237), channel_id=1, source_target_pairs={{0,4},{4,8},{8,12},{12,0},{1,5},{5,9},{9,13},{13,1},{2,6},{6,10},{... | collective-permute-start | bytes 1032200 | tf_op jit(solution)/shard_map/ppermute | solution.py:407
  238.3 15.1 %collective-permute-start.19 = (bf16[256,1536]{1,0:T(8,128)(2,1)S(1)}, bf16[256,1536]{1,0:T(8,128)(2,1)S(1)}, u32[]{:S(2)}, u32[]{:S(2)}) collective-permute-start(bf16[256,1536]{1,0:T(8,128)(2,1)S(1)} %slice.1647), channel_id=1, source_target_pairs={{0,2},{1,3},{2,0},{3,1},{4,6},{5,7},{6,4},{7,5},{8,10},{9,11},{10,... | collective-permute-start | bytes 2359304 | tf_op jit(solution)/shard_map/ppermute | solution.py:403
  240.6 19.9 %collective-permute-start.23 = (bf16[112,1536]{1,0:T(8,128)(2,1)S(1)}, bf16[112,1536]{1,0:T(8,128)(2,1)}, u32[]{:S(2)}, u32[]{:S(2)}) collective-permute-start(bf16[112,1536]{1,0:T(8,128)(2,1)S(1)} %get-tuple-element.297), channel_id=1, source_target_pairs={{0,4},{4,8},{8,12},{12,0},{1,5},{5,9},{9,13},{13,1},{2,6},{6,10},{... | collective-permute-start | bytes 1032200 | tf_op jit(solution)/shard_map/ppermute | solution.py:407
  255.6 24.3 %collective-permute-start.26 = (bf16[112,1536]{1,0:T(8,128)(2,1)}, bf16[112,1536]{1,0:T(8,128)(2,1)}, u32[]{:S(2)}, u32[]{:S(2)}) collective-permute-start(bf16[112,1536]{1,0:T(8,128)(2,1)} %collective-permute-done.21), channel_id=1, source_target_pairs={{0,4},{4,8},{8,12},{12,0},{1,5},{5,9},{9,13},{13,1},{2,6},{6,10},{... | collective-permute-start | bytes 1032200 | tf_op jit(solution)/shard_map/ppermute | solution.py:407
  261.6 35.0 %collective-permute-start.28 = (bf16[112,1536]{1,0:T(8,128)(2,1)}, bf16[112,1536]{1,0:T(8,128)(2,1)}, u32[]{:S(2)}, u32[]{:S(2)}) collective-permute-start(bf16[112,1536]{1,0:T(8,128)(2,1)} %collective-permute-done.23), channel_id=1, source_target_pairs={{0,4},{4,8},{8,12},{12,0},{1,5},{5,9},{9,13},{13,1},{2,6},{6,10},{... | collective-permute-start | bytes 1032200 | tf_op jit(solution)/shard_map/ppermute | solution.py:407
  286.5 15.1 %collective-permute-start.27 = (bf16[512,768]{1,0:T(8,128)(2,1)S(1)}, bf16[512,768]{1,0:T(8,128)(2,1)S(1)}, u32[]{:S(2)}, u32[]{:S(2)}) collective-permute-start(bf16[512,768]{1,0:T(8,128)(2,1)S(1)} %pad_maximum_fusion.25), channel_id=1, source_target_pairs={{0,2},{1,3},{2,0},{3,1},{4,6},{5,7},{6,4},{7,5},{8,10},{9,11},{10,... | collective-permute-start | bytes 2359304 | tf_op jit(solution)/shard_map/ppermute | solution.py:403
  303.0 25.3 %collective-permute-start.29 = (bf16[1024,768]{1,0:T(8,128)(2,1)}, bf16[1024,768]{1,0:T(8,128)(2,1)}, u32[]{:S(2)}, u32[]{:S(2)}) collective-permute-start(bf16[1024,768]{1,0:T(8,128)(2,1)} %pad_maximum_fusion.10), channel_id=1, source_target_pairs={{0,16},{16,0},{1,17},{17,1},{2,18},{18,2},{3,19},{19,3},{4,20},{20... | collective-permute-start | bytes 4718600 | tf_op jit(solution)/shard_map/ppermute | solution.py:395
  310.8 16.1 %collective-permute-start.33 = (bf16[512,768]{1,0:T(8,128)(2,1)S(1)}, bf16[512,768]{1,0:T(8,128)(2,1)S(1)}, u32[]{:S(2)}, u32[]{:S(2)}) collective-permute-start(bf16[512,768]{1,0:T(8,128)(2,1)S(1)} %pad_maximum_fusion.26), channel_id=1, source_target_pairs={{0,2},{1,3},{2,0},{3,1},{4,6},{5,7},{6,4},{7,5},{8,10},{9,11},{10,... | collective-permute-start | bytes 2359304 | tf_op jit(solution)/shard_map/ppermute | solution.py:403
  462.7 73.0 %collective-permute-start.56 = (bf16[112,1536]{1,0:T(8,128)(2,1)S(1)}, bf16[112,1536]{1,0:T(8,128)(2,1)S(1)}, u32[]{:S(2)}, u32[]{:S(2)}) collective-permute-start(bf16[112,1536]{1,0:T(8,128)(2,1)S(1)} %slice.1166), channel_id=1, source_target_pairs={{0,12},{4,0},{8,4},{12,8},{1,13},{5,1},{9,5},{13,9},{2,14},{6,2},{... | collective-permute-start | bytes 1032200 | tf_op jit(solution)/shard_map/ppermute | solution.py:407
  474.4 37.6 %collective-permute-start.54 = (bf16[112,1536]{1,0:T(8,128)(2,1)S(1)}, bf16[112,1536]{1,0:T(8,128)(2,1)S(1)}, u32[]{:S(2)}, u32[]{:S(2)}) collective-permute-start(bf16[112,1536]{1,0:T(8,128)(2,1)S(1)} %slice.1163), channel_id=1, source_target_pairs={{0,12},{4,0},{8,4},{12,8},{1,13},{5,1},{9,5},{13,9},{2,14},{6,2},{... | collective-permute-start | bytes 1032200 | tf_op jit(solution)/shard_map/ppermute | solution.py:407
  474.5 37.5 %collective-permute-start.53 = (bf16[112,1536]{1,0:T(8,128)(2,1)S(1)}, bf16[112,1536]{1,0:T(8,128)(2,1)S(1)}, u32[]{:S(2)}, u32[]{:S(2)}) collective-permute-start(bf16[112,1536]{1,0:T(8,128)(2,1)S(1)} %slice.1162), channel_id=1, source_target_pairs={{0,12},{4,0},{8,4},{12,8},{1,13},{5,1},{9,5},{13,9},{2,14},{6,2},{... | collective-permute-start | bytes 1032200 | tf_op jit(solution)/shard_map/ppermute | solution.py:407
  494.6 13.7 %collective-permute-start.51 = (bf16[1024,768]{1,0:T(8,128)(2,1)S(1)}, bf16[1024,768]{1,0:T(8,128)(2,1)S(1)}, u32[]{:S(2)}, u32[]{:S(2)}) collective-permute-start(bf16[1024,768]{1,0:T(8,128)(2,1)S(1)} %slice.979), channel_id=1, source_target_pairs={{0,16},{16,0},{1,17},{17,1},{2,18},{18,2},{3,19},{19,3},{4,20},{20... | collective-permute-start | bytes 4718600 | tf_op jit(solution)/shard_map/ppermute | solution.py:395
  511.0 22.5 %collective-permute-start.73 = (bf16[512,768]{1,0:T(8,128)(2,1)S(1)}, bf16[512,768]{1,0:T(8,128)(2,1)S(1)}, u32[]{:S(2)}, u32[]{:S(2)}) collective-permute-start(bf16[512,768]{1,0:T(8,128)(2,1)S(1)} %slice.1642), channel_id=1, source_target_pairs={{0,2},{1,3},{2,0},{3,1},{4,6},{5,7},{6,4},{7,5},{8,10},{9,11},{10,... | collective-permute-start | bytes 2359304 | tf_op jit(solution)/shard_map/ppermute | solution.py:403
  520.9 14.9 %collective-permute-start.57 = (bf16[112,1536]{1,0:T(8,128)(2,1)S(1)}, bf16[112,1536]{1,0:T(8,128)(2,1)S(1)}, u32[]{:S(2)}, u32[]{:S(2)}) collective-permute-start(bf16[112,1536]{1,0:T(8,128)(2,1)S(1)} %add_convert_fusion.13), channel_id=1, source_target_pairs={{0,12},{4,0},{8,4},{12,8},{1,13},{5,1},{9,5},{13,9},{2,14},{6,2},{... | collective-permute-start | bytes 1032200 | tf_op jit(solution)/shard_map/ppermute | solution.py:407
  521.2 14.6 %collective-permute-start.55 = (bf16[256,768]{1,0:T(8,128)(2,1)S(1)}, bf16[256,768]{1,0:T(8,128)(2,1)S(1)}, u32[]{:S(2)}, u32[]{:S(2)}) collective-permute-start(bf16[256,768]{1,0:T(8,128)(2,1)S(1)} %slice.1653), channel_id=1, source_target_pairs={{0,1},{1,0},{2,3},{3,2},{4,5},{5,4},{6,7},{7,6},{8,9},{9,8},{10,11... | collective-permute-start | bytes 1179656 | tf_op jit(solution)/shard_map/ppermute | solution.py:403
  535.3 20.4 %collective-permute-start.60 = (bf16[112,1536]{1,0:T(8,128)(2,1)S(1)}, bf16[112,1536]{1,0:T(8,128)(2,1)S(1)}, u32[]{:S(2)}, u32[]{:S(2)}) collective-permute-start(bf16[112,1536]{1,0:T(8,128)(2,1)S(1)} %add_convert_fusion.12), channel_id=1, source_target_pairs={{0,12},{4,0},{8,4},{12,8},{1,13},{5,1},{9,5},{13,9},{2,14},{6,2},{... | collective-permute-start | bytes 1032200 | tf_op jit(solution)/shard_map/ppermute | solution.py:407
  554.1 19.3 %collective-permute-start.76 = (bf16[4,384,768]{2,1,0:T(8,128)(2,1)S(1)}, bf16[4,384,768]{2,1,0:T(8,128)(2,1)S(1)}, u32[]{:S(2)}, u32[]{:S(2)}) collective-permute-start(bf16[4,384,768]{2,1,0:T(8,128)(2,1)S(1)} %convolution_convert_fusion.12), channel_id=1, source_target_pairs={{0,16},{16,0},{1,17},{17,1},{2,18},{18,2},{3,19},{19,3},{4,20},{20... | collective-permute-start | bytes 7077896 | tf_op jit(solution)/shard_map/ppermute | solution.py:395
  555.1 20.4 %collective-permute-start.64 = (bf16[5,384,768]{2,1,0:T(8,128)(2,1)S(1)}, bf16[5,384,768]{2,1,0:T(8,128)(2,1)S(1)}, u32[]{:S(2)}, u32[]{:S(2)}) collective-permute-start(bf16[5,384,768]{2,1,0:T(8,128)(2,1)S(1)} %convolution_convert_fusion.11), channel_id=1, source_target_pairs={{0,16},{16,0},{1,17},{17,1},{2,18},{18,2},{3,19},{19,3},{4,20},{20... | collective-permute-start | bytes 8847368 | tf_op jit(solution)/shard_map/ppermute | solution.py:395
  560.3 65.0 %collective-permute-start.68 = (bf16[112,1536]{1,0:T(8,128)(2,1)S(1)}, bf16[112,1536]{1,0:T(8,128)(2,1)S(1)}, u32[]{:S(2)}, u32[]{:S(2)}) collective-permute-start(bf16[112,1536]{1,0:T(8,128)(2,1)S(1)} %add_convert_fusion.9), channel_id=1, source_target_pairs={{0,12},{4,0},{8,4},{12,8},{1,13},{5,1},{9,5},{13,9},{2,14},{6,2},{... | collective-permute-start | bytes 1032200 | tf_op jit(solution)/shard_map/ppermute | solution.py:407
  574.3 19.9 %collective-permute-start.78 = (bf16[4,192,768]{2,1,0:T(8,128)(2,1)S(1)}, bf16[4,192,768]{2,1,0:T(8,128)(2,1)S(1)}, u32[]{:S(2)}, u32[]{:S(2)}) collective-permute-start(bf16[4,192,768]{2,1,0:T(8,128)(2,1)S(1)} %slice.1640), channel_id=1, source_target_pairs={{0,1},{1,0},{2,3},{3,2},{4,5},{5,4},{6,7},{7,6},{8,9},{9,8},{10,11... | collective-permute-start | bytes 3538952 | tf_op jit(solution)/shard_map/ppermute | solution.py:403
  576.7 36.0 %collective-permute-start.71 = (bf16[5,192,768]{2,1,0:T(8,128)(2,1)S(1)}, bf16[5,192,768]{2,1,0:T(8,128)(2,1)S(1)}, u32[]{:S(2)}, u32[]{:S(2)}) collective-permute-start(bf16[5,192,768]{2,1,0:T(8,128)(2,1)S(1)} %slice.1639), channel_id=1, source_target_pairs={{0,1},{1,0},{2,3},{3,2},{4,5},{5,4},{6,7},{7,6},{8,9},{9,8},{10,11... | collective-permute-start | bytes 4423688 | tf_op jit(solution)/shard_map/ppermute | solution.py:403
  589.1 25.0 %collective-permute-start.65 = (bf16[512,1536]{1,0:T(8,128)(2,1)}, bf16[512,1536]{1,0:T(8,128)(2,1)S(1)}, u32[]{:S(2)}, u32[]{:S(2)}) collective-permute-start(bf16[512,1536]{1,0:T(8,128)(2,1)} %fusion.1), channel_id=1, source_target_pairs={{0,16},{16,0},{1,17},{17,1},{2,18},{18,2},{3,19},{19,3},{4,20},{20... | collective-permute-start | bytes 4718600 | tf_op jit(solution)/shard_map/ppermute | solution.py:395
  589.2 36.1 %collective-permute-start.67 = (bf16[112,1536]{1,0:T(8,128)(2,1)S(1)}, bf16[112,1536]{1,0:T(8,128)(2,1)S(1)}, u32[]{:S(2)}, u32[]{:S(2)}) collective-permute-start(bf16[112,1536]{1,0:T(8,128)(2,1)S(1)} %add_convert_fusion.10), channel_id=1, source_target_pairs={{0,12},{4,0},{8,4},{12,8},{1,13},{5,1},{9,5},{13,9},{2,14},{6,2},{... | collective-permute-start | bytes 1032200 | tf_op jit(solution)/shard_map/ppermute | solution.py:407
  594.6 23.1 %collective-permute-start.80 = (bf16[4,96,768]{2,1,0:T(8,128)(2,1)S(1)}, bf16[4,96,768]{2,1,0:T(8,128)(2,1)S(1)}, u32[]{:S(2)}, u32[]{:S(2)}) collective-permute-start(bf16[4,96,768]{2,1,0:T(8,128)(2,1)S(1)} %slice.1650), channel_id=1, source_target_pairs={{0,2},{1,3},{2,0},{3,1},{4,6},{5,7},{6,4},{7,5},{8,10},{9,11},{10,... | collective-permute-start | bytes 1769480 | tf_op jit(solution)/shard_map/ppermute | solution.py:403
  616.3 16.8 %collective-permute-start.66 = (bf16[256,1536]{1,0:T(8,128)(2,1)S(1)}, bf16[256,1536]{1,0:T(8,128)(2,1)S(1)}, u32[]{:S(2)}, u32[]{:S(2)}) collective-permute-start(bf16[256,1536]{1,0:T(8,128)(2,1)S(1)} %slice.1643), channel_id=1, source_target_pairs={{0,2},{1,3},{2,0},{3,1},{4,6},{5,7},{6,4},{7,5},{8,10},{9,11},{10,... | collective-permute-start | bytes 2359304 | tf_op jit(solution)/shard_map/ppermute | solution.py:403
  667.9 30.8 %collective-permute-start.87 = (bf16[112,1536]{1,0:T(8,128)(2,1)S(1)}, bf16[112,1536]{1,0:T(8,128)(2,1)S(1)}, u32[]{:S(2)}, u32[]{:S(2)}) collective-permute-start(bf16[112,1536]{1,0:T(8,128)(2,1)S(1)} %slice.1219), channel_id=1, source_target_pairs={{0,12},{4,0},{8,4},{12,8},{1,13},{5,1},{9,5},{13,9},{2,14},{6,2},{... | collective-permute-start | bytes 1032200 | tf_op jit(solution)/shard_map/ppermute | solution.py:407
  672.7 20.1 %collective-permute-start.83 = (bf16[512,768]{1,0:T(8,128)(2,1)S(1)}, bf16[512,768]{1,0:T(8,128)(2,1)S(1)}, u32[]{:S(2)}, u32[]{:S(2)}) collective-permute-start(bf16[512,768]{1,0:T(8,128)(2,1)S(1)} %slice.1641), channel_id=1, source_target_pairs={{0,2},{1,3},{2,0},{3,1},{4,6},{5,7},{6,4},{7,5},{8,10},{9,11},{10,... | collective-permute-start | bytes 2359304 | tf_op jit(solution)/shard_map/ppermute | solution.py:403
  676.0 16.8 %collective-permute-start.84 = (bf16[112,1536]{1,0:T(8,128)(2,1)S(1)}, bf16[112,1536]{1,0:T(8,128)(2,1)S(1)}, u32[]{:S(2)}, u32[]{:S(2)}) collective-permute-start(bf16[112,1536]{1,0:T(8,128)(2,1)S(1)} %slice.1215), channel_id=1, source_target_pairs={{0,12},{4,0},{8,4},{12,8},{1,13},{5,1},{9,5},{13,9},{2,14},{6,2},{... | collective-permute-start | bytes 1032200 | tf_op jit(solution)/shard_map/ppermute | solution.py:407
  716.9 13.6 %collective-permute-start.90 = (bf16[5,384,768]{2,1,0:T(8,128)(2,1)S(1)}, bf16[5,384,768]{2,1,0:T(8,128)(2,1)S(1)}, u32[]{:S(2)}, u32[]{:S(2)}) collective-permute-start(bf16[5,384,768]{2,1,0:T(8,128)(2,1)S(1)} %convolution_convert_fusion.10), channel_id=1, source_target_pairs={{0,16},{16,0},{1,17},{17,1},{2,18},{18,2},{3,19},{19,3},{4,20},{20... | collective-permute-start | bytes 8847368 | tf_op jit(solution)/shard_map/ppermute | solution.py:395
  731.7 29.3 %collective-permute-start.91 = (bf16[5,192,768]{2,1,0:T(8,128)(2,1)S(1)}, bf16[5,192,768]{2,1,0:T(8,128)(2,1)S(1)}, u32[]{:S(2)}, u32[]{:S(2)}) collective-permute-start(bf16[5,192,768]{2,1,0:T(8,128)(2,1)S(1)} %slice.1638), channel_id=1, source_target_pairs={{0,1},{1,0},{2,3},{3,2},{4,5},{5,4},{6,7},{7,6},{8,9},{9,8},{10,11... | collective-permute-start | bytes 4423688 | tf_op jit(solution)/shard_map/ppermute | solution.py:403
  738.2 57.0 %collective-permute-start.101 = (bf16[5,24,768]{2,1,0:T(8,128)(2,1)S(1)}, bf16[5,24,768]{2,1,0:T(8,128)(2,1)S(1)}, u32[]{:S(2)}, u32[]{:S(2)}) collective-permute-start(bf16[5,24,768]{2,1,0:T(8,128)(2,1)S(1)} %slice.1660), channel_id=1, source_target_pairs={{0,8},{1,9},{2,10},{3,11},{4,12},{5,13},{6,14},{7,15},{8,0},{9,1},... | collective-permute-start | bytes 552968 | tf_op jit(solution)/shard_map/ppermute | solution.py:403
  738.4 15.3 %collective-permute-start.92 = (bf16[112,1536]{1,0:T(8,128)(2,1)S(1)}, bf16[112,1536]{1,0:T(8,128)(2,1)S(1)}, u32[]{:S(2)}, u32[]{:S(2)}) collective-permute-start(bf16[112,1536]{1,0:T(8,128)(2,1)S(1)} %add_convert_fusion.6), channel_id=1, source_target_pairs={{0,12},{4,0},{8,4},{12,8},{1,13},{5,1},{9,5},{13,9},{2,14},{6,2},{... | collective-permute-start | bytes 1032200 | tf_op jit(solution)/shard_map/ppermute | solution.py:407
  742.1 19.0 %collective-permute-start.93 = (bf16[112,1536]{1,0:T(8,128)(2,1)S(1)}, bf16[112,1536]{1,0:T(8,128)(2,1)S(1)}, u32[]{:S(2)}, u32[]{:S(2)}) collective-permute-start(bf16[112,1536]{1,0:T(8,128)(2,1)S(1)} %add_convert_fusion.5), channel_id=1, source_target_pairs={{0,12},{4,0},{8,4},{12,8},{1,13},{5,1},{9,5},{13,9},{2,14},{6,2},{... | collective-permute-start | bytes 1032200 | tf_op jit(solution)/shard_map/ppermute | solution.py:407
  743.0 25.4 %collective-permute-start.95 = (bf16[112,1536]{1,0:T(8,128)(2,1)S(1)}, bf16[112,1536]{1,0:T(8,128)(2,1)S(1)}, u32[]{:S(2)}, u32[]{:S(2)}) collective-permute-start(bf16[112,1536]{1,0:T(8,128)(2,1)S(1)} %add_convert_fusion.4), channel_id=1, source_target_pairs={{0,12},{4,0},{8,4},{12,8},{1,13},{5,1},{9,5},{13,9},{2,14},{6,2},{... | collective-permute-start | bytes 1032200 | tf_op jit(solution)/shard_map/ppermute | solution.py:407
  776.5 17.8 %collective-permute-start.97 = (bf16[5,48,768]{2,1,0:T(8,128)(2,1)S(1)}, bf16[5,48,768]{2,1,0:T(8,128)(2,1)S(1)}, u32[]{:S(2)}, u32[]{:S(2)}) collective-permute-start(bf16[5,48,768]{2,1,0:T(8,128)(2,1)S(1)} %slice.1654), channel_id=1, source_target_pairs={{0,4},{1,5},{2,6},{3,7},{4,0},{5,1},{6,2},{7,3},{8,12},{9,13},{10,... | collective-permute-start | bytes 1105928 | tf_op jit(solution)/shard_map/ppermute | solution.py:403
  789.8 17.2 %collective-permute-start.103 = (bf16[3,112,768]{2,1,0:T(8,128)(2,1)}, bf16[3,112,768]{2,1,0:T(8,128)(2,1)}, u32[]{:S(2)}, u32[]{:S(2)}) collective-permute-start(bf16[3,112,768]{2,1,0:T(8,128)(2,1)} %select_convert_fusion), channel_id=1, source_target_pairs={{0,16},{16,0},{1,17},{17,1},{2,18},{18,2},{3,19},{19,3},{4,20},{20... | collective-permute-start | bytes 1548296 | tf_op jit(solution)/shard_map/ppermute | solution.py:395
  (326 other events, 3007.0 us)
Sparse Core Ops, SparseCore 0:
  17.2 77.1 all-gather.4
  97.4 118.3 all-gather.6

commit v3 on v2

--- a/solution.py
+++ b/solution.py
@@ -89,22 +89,20 @@
 
 def flatten_kernel(hid, groups, grad_ref, spread_ref, out_ref):
     chunks = PERIOD // LANES
-    high = grad_ref[0].astype(BF)
-    low = (grad_ref[0] - high.astype(F32)).astype(BF)
+    grads = grad_ref[0].astype(BF)
     for t in range(chunks):
         total = jnp.zeros((groups, LANES), F32)
         for piece_t, lane, j, first, length in flat_pieces(hid):
             if piece_t == t:
-                for part in (high, low):
-                    rows = part[first : first + length, :]
-                    parts = []
-                    if lane > 0:
-                        parts.append(jnp.zeros((lane, rows.shape[1]), BF))
-                    parts.append(rows)
-                    if lane + length < LANES:
-                        parts.append(jnp.zeros((LANES - lane - length, rows.shape[1]), BF))
-                    rows = jnp.concatenate(parts, 0) if len(parts) > 1 else rows
-                    total = total + dot_nt(spread_ref[j], rows)
+                rows = grads[first : first + length, :]
+                parts = []
+                if lane > 0:
+                    parts.append(jnp.zeros((lane, rows.shape[1]), BF))
+                parts.append(rows)
+                if lane + length < LANES:
+                    parts.append(jnp.zeros((LANES - lane - length, rows.shape[1]), BF))
+                rows = jnp.concatenate(parts, 0) if len(parts) > 1 else rows
+                total = total + dot_nt(spread_ref[j], rows)
         out_ref[0, pl.ds(t, groups, stride=chunks), :] = total
 
 
@@ -749,19 +747,21 @@
 
         return links.owner_scatter(products(to_own, own_half), products(to_other, other_half), rides)
 
-    def feed_back(kept, matrices, grad, events=((), ()), rides=((0, 0), (0, 0))):
+    def feed_back(kept, matrices, grad, outs, events=((), ()), rides=((0, 0), (0, 0))):
         everyone, gate, upper, hidden = kept
         grad_all = anchor(links.plane_gather(grad.astype(BF), rides[0]), *events[0])
+        links.unload()
         _, pull = jax.vjp(gated_units, gate, upper)
         grad_gate, grad_upper = pull(dot_nt(grad_all, matrices[2]))
         gate_b, upper_b = grad_gate.astype(BF), grad_upper.astype(BF)
-        grad_normed = anchor(links.plane_scatter(eighths([gate_b, upper_b], matrices[:2]), rides[1]), *events[1])
-        grads = [
+        grads = (
             dot_tn(gate_b, everyone).astype(BF),
             dot_tn(upper_b, everyone).astype(BF),
             dot_tn(hidden, grad_all).astype(BF),
-        ]
-        return grad_normed, grads
+        )
+        links.load(*(scatter_trip(grads[m], outs[m]) for m in (2, 0, 1)))
+        grad_normed = links.plane_scatter(eighths([gate_b, upper_b], matrices[:2]), rides[1])
+        return anchor(grad_normed, *events[1])
 
     def attention_back(kept, normed_q, normed_kv, matrices, where, causal, grad, rides=0, events=((), ())):
         queries, kv, context = kept
@@ -778,11 +778,10 @@
 
     grad_final = unproject(grad_logits, head_w)
     grad_dec, gain_six = rms_reverse(dec_three, gains[6], s_six, grad_final)
-    grad_normed, feed_dec_grad = feed_back(kept_dec_feed, feed_dec, grad_dec)
+    dec_feed, enc_feed = [[], [], []], [[], [], []]
+    grad_normed = feed_back(kept_dec_feed, feed_dec, grad_dec, dec_feed, rides=((0, 0), (1, 1)))
     part, gain_five = rms_reverse(dec_two, gains[5], s_five, grad_normed)
     grad_dec = grad_dec + part
-    dec_feed, enc_feed = [[], [], []], [[], [], []]
-    links.load(*(scatter_trip(feed_dec_grad[m], dec_feed[m]) for m in range(3)))
     d_q, grad_memory, cross_grad = attention_back(
         kept_cross, n_four, memory, weights[2], src_places, False, grad_dec, 2
     )
@@ -796,15 +795,18 @@
     part, gain_three = rms_reverse(dec_zero, gains[3], s_three, d_q + d_kv)
     grad_dec = grad_dec + part
     grad_enc, gain_two = rms_reverse(enc_two, gains[2], s_two, grad_memory)
-    grad_normed, feed_enc_grad = feed_back(
-        kept_enc_feed, feed_enc, grad_enc, ((cross_stages[0],), (cross_stages[1], dec_stages[0])), ((1, 1), (2, 1))
-    )
+    grad_normed = feed_back(
+        kept_enc_feed,
+        feed_enc,
+        grad_enc,
+        enc_feed,
+        ((cross_stages[0],), (cross_stages[1], dec_stages[0])),
+        ((2, 1), (2, 1)),
+    )
+    dec_rows = to_rows(jnp.stack([o[0] for o in dec_feed]))
+    dec_flat = flatten(dec_rows, spread, hid, period_groups)
     part, gain_one = rms_reverse(enc_one, gains[1], s_one, grad_normed)
     grad_enc = grad_enc + part
-    links.unload()
-    dec_rows = to_rows(jnp.stack([o[0] for o in dec_feed]))
-    dec_flat = flatten(dec_rows, spread, hid, period_groups)
-    links.load(*(scatter_trip(feed_enc_grad[m], enc_feed[m]) for m in range(3)))
     d_q, d_kv, enc_grad = attention_back(
         kept_enc, n_zero, n_zero, weights[0], src_places, False, grad_enc, 2,
         ((cross_stages[2], dec_stages[1]), (cross_stages[3], dec_stages[2], dec_flat)),

time: 875 us -> 853 us (0.975)
  waiting for transfers between devices: 462 us -> 428 us
  starting transfers between devices: 93.6 us -> 116 us
    ppermute x46, waiting for transfers between devices: 169 us -> 142 us  [swap_by_core(): return lax.ppermute(value, ('c', 'z', 'y', 'x'), pairs)]
    ppermute x36, starting transfers between devices: 29.8 us -> 48.6 us  [ring(): return lax.ppermute(value, 'z', [(i, (i + step) % n) for i in range(n)])]
    unnamed x550 -> x538, local copies, waits for them, and re-layouts: 21 us -> 20 us
  transfers between devices with their start and end apart: 111 -> 111, of which waited for: 65 -> 63; matrix products, arithmetic and copies ran while one was open for 17% -> 17% of each run, Pallas kernels for 5% -> 5%
where the time goes in v3:
time: 853 us; the launch traced here: 843 us
  waiting for transfers between devices  428 us (50%)
  starting transfers between devices  116 us (14%)
  matrix products  90.7 us (11%)
  Pallas kernels  73.3 us (9%)
  other arithmetic  57.9 us (7%)
  local copies, waits for them, and re-layouts  48.7 us (6%)
  between operations  28 us (3%)
    ppermute x36, waiting for transfers between devices, ring(): return lax.ppermute(value, 'z', [(i, (i + step) % n) for i in range(n)])  207 us
    ppermute x46, waiting for transfers between devices, swap_by_core(): return lax.ppermute(value, ('c', 'z', 'y', 'x'), pairs)  142 us
    all_gather x2, waiting for transfers between devices, gather_tiles(): full = lax.all_gather(tiles[:, None], everywhere, axis=1, tiled=True)  52.5 us
    ppermute x46, starting transfers between devices, swap_by_core(): return lax.ppermute(value, ('c', 'z', 'y', 'x'), pairs)  51.4 us
    ppermute x36, starting transfers between devices, ring(): return lax.ppermute(value, 'z', [(i, (i + step) % n) for i in range(n)])  48.6 us
    dot_general x32, matrix products, dot_nt(): lax.dot_general(a, b, (((1,), (1,)), ((), ())), preferred_element_type=F32)  36.9 us
    dot_general x48, matrix products, dot_nn(): lax.dot_general(a, b, (((1,), (0,)), ((), ())), preferred_element_type=F32)  35.9 us
    pallas_call x3, Pallas kernels, attend_back(): pl.pallas_call(functools.partial(attend_back_kernel, causal), out_shape=(...  31.6 us
  transfers between devices with their start and end apart: 111, of which 63 were waited for; matrix products, arithmetic and copies ran while one was open for 17% of the time, Pallas kernels for 5%

profile of v3, /device:TPU:0, one launch (start us, length us, event | category | flops | bytes accessed | tf_op | source)
XLA Modules:
  0.0 843.2 jit_solution(171993095511659783)
XLA Ops:
  27.9 5.5 collective-permute-start.20
  41.8 52.5 %all-gather.5.cloned.1.call-done = bf16[5,768,768]{2,1,0:T(8,128)(2,1)} async-done(((bf16[5,24,768]{2,1,0:T(8,128)(2,1)}), bf16[5,768,768]{2,1,0:T(8,128)(2,1)}) %all-gather.5.cloned.1.call-update) | async-done | bytes 5898256 | tf_op jit(solution)/shard_map/all_gather | solution.py:569
  104.3 8.4 collective-permute-done.4
  116.5 10.6 %collective-permute-done.6 = bf16[112,1536]{1,0:T(8,128)(2,1)S(1)} collective-permute-done((bf16[112,1536]{1,0:T(8,128)(2,1)S(1)}, bf16[112,1536]{1,0:T(8,128)(2,1)S(1)}, u32[]{:S(2)}, u32[]{:S(2)}) %collective-permute-start.6) | collective-permute-done | bytes 344096 | tf_op jit(solution)/shard_map/ppermute | solution.py:405
  127.2 6.4 collective-permute-done.7
  136.3 18.7 %collective-permute-done.9 = bf16[112,1536]{1,0:T(8,128)(2,1)S(1)} collective-permute-done((bf16[112,1536]{1,0:T(8,128)(2,1)S(1)}, bf16[112,1536]{1,0:T(8,128)(2,1)S(1)}, u32[]{:S(2)}, u32[]{:S(2)}) %collective-permute-start.9) | collective-permute-done | bytes 344096 | tf_op jit(solution)/shard_map/ppermute | solution.py:405
  155.0 11.9 %collective-permute-done.10 = bf16[112,1536]{1,0:T(8,128)(2,1)S(1)} collective-permute-done((bf16[112,1536]{1,0:T(8,128)(2,1)S(1)}, bf16[112,1536]{1,0:T(8,128)(2,1)S(1)}, u32[]{:S(2)}, u32[]{:S(2)}) %collective-permute-start.10) | collective-permute-done | bytes 344096 | tf_op jit(solution)/shard_map/ppermute | solution.py:405
  177.1 4.9 attend.3
  185.5 15.8 %collective-permute-done.13 = bf16[112,1536]{1,0:T(8,128)(2,1)S(1)} collective-permute-done((bf16[112,1536]{1,0:T(8,128)(2,1)S(1)}, bf16[112,1536]{1,0:T(8,128)(2,1)S(1)}, u32[]{:S(2)}, u32[]{:S(2)}) %collective-permute-start.13) | collective-permute-done | bytes 344096 | tf_op jit(solution)/shard_map/ppermute | solution.py:405
  204.0 13.6 %collective-permute-done.15 = bf16[112,1536]{1,0:T(8,128)(2,1)S(1)} collective-permute-done((bf16[112,1536]{1,0:T(8,128)(2,1)S(1)}, bf16[112,1536]{1,0:T(8,128)(2,1)S(1)}, u32[]{:S(2)}, u32[]{:S(2)}) %collective-permute-start.15) | collective-permute-done | bytes 344096 | tf_op jit(solution)/shard_map/ppermute | solution.py:405
  241.9 11.5 %collective-permute-done.21 = bf16[112,1536]{1,0:T(8,128)(2,1)} collective-permute-done((bf16[112,1536]{1,0:T(8,128)(2,1)S(1)}, bf16[112,1536]{1,0:T(8,128)(2,1)}, u32[]{:S(2)}, u32[]{:S(2)}) %collective-permute-start.21) | collective-permute-done | bytes 344096 | tf_op jit(solution)/shard_map/ppermute | solution.py:405
  255.5 5.0 collective-permute-done.23
  263.2 6.9 fusion.212
  272.0 6.5 collective-permute-done.24
  279.8 6.5 collective-permute-done.25
  289.4 5.7 collective-permute-done.30
  296.5 5.2 collective-permute-done.27
  315.0 11.6 %collective-permute-done.34 = bf16[112,1536]{1,0:T(8,128)(2,1)S(1)} collective-permute-done((bf16[112,1536]{1,0:T(8,128)(2,1)}, bf16[112,1536]{1,0:T(8,128)(2,1)S(1)}, u32[]{:S(2)}, u32[]{:S(2)}) %collective-permute-start.34) | collective-permute-done | bytes 344096 | tf_op jit(solution)/shard_map/ppermute | solution.py:405
  329.7 5.0 attend.4
  337.1 4.9 attend.5
  344.8 12.5 %collective-permute-done.37 = bf16[112,1536]{1,0:T(8,128)(2,1)S(1)} collective-permute-done((bf16[112,1536]{1,0:T(8,128)(2,1)S(1)}, bf16[112,1536]{1,0:T(8,128)(2,1)S(1)}, u32[]{:S(2)}, u32[]{:S(2)}) %collective-permute-start.37) | collective-permute-done | bytes 344096 | tf_op jit(solution)/shard_map/ppermute | solution.py:405
  358.4 11.4 %collective-permute-done.39 = bf16[112,1536]{1,0:T(8,128)(2,1)S(1)} collective-permute-done((bf16[112,1536]{1,0:T(8,128)(2,1)S(1)}, bf16[112,1536]{1,0:T(8,128)(2,1)S(1)}, u32[]{:S(2)}, u32[]{:S(2)}) %collective-permute-start.39) | collective-permute-done | bytes 344096 | tf_op jit(solution)/shard_map/ppermute | solution.py:405
  388.7 11.4 %collective-permute-done.43 = bf16[256,1536]{1,0:T(8,128)(2,1)S(1)} collective-permute-done((bf16[256,1536]{1,0:T(8,128)(2,1)S(1)}, bf16[256,1536]{1,0:T(8,128)(2,1)S(1)}, u32[]{:S(2)}, u32[]{:S(2)}) %collective-permute-start.43) | collective-permute-done | bytes 786464 | tf_op jit(solution)/shard_map/ppermute | solution.py:401
  418.0 6.5 collective-permute-done.45
  425.3 11.4 %collective-permute-done.46 = bf16[256,1536]{1,0:T(8,128)(2,1)S(1)} collective-permute-done((bf16[256,1536]{1,0:T(8,128)(2,1)S(1)}, bf16[256,1536]{1,0:T(8,128)(2,1)S(1)}, u32[]{:S(2)}, u32[]{:S(2)}) %collective-permute-start.46) | collective-permute-done | bytes 786464 | tf_op jit(solution)/shard_map/ppermute | solution.py:401
  442.6 5.3 multiply_convert_fusion.1
  467.7 6.2 collective-permute-done.49
  475.7 8.9 %collective-permute-done.52 = bf16[112,1536]{1,0:T(8,128)(2,1)S(1)} collective-permute-done((bf16[112,1536]{1,0:T(8,128)(2,1)S(1)}, bf16[112,1536]{1,0:T(8,128)(2,1)S(1)}, u32[]{:S(2)}, u32[]{:S(2)}) %collective-permute-start.52) | collective-permute-done | bytes 344096 | tf_op jit(solution)/shard_map/ppermute | solution.py:405
  487.3 10.5 %attend_back.3 = (bf16[128,384]{1,0:T(8,128)(2,1)S(1)}, bf16[2048,768]{1,0:T(8,128)(2,1)S(1)}) custom-call(s32[18]{0:T(128)S(1)} %get-tuple-element.369.where_ref, bf16[128,384]{1,0:T(8,128)(2,1)S(1)} %fusion.23.q_ref, bf16[128,384]{1,0:T(8,128)(2,1)S(1)} %fusion.26.g_ref, bf16[2048,768]{1,0:T(8,128)(2,1)S(1)} %copy-done.9), custom_call_target="tpu_custom_call" | custom-call | flops 2013265920 | bytes 6291456 | tf_op jit(solution)/shard_map/attend_back/pallas_call | solution.py:309
  500.8 10.7 %attend_back.4 = (bf16[128,384]{1,0:T(8,128)(2,1)S(1)}, bf16[2048,768]{1,0:T(8,128)(2,1)S(1)}) custom-call(s32[18]{0:T(128)S(1)} %get-tuple-element.368.where_ref, bf16[128,384]{1,0:T(8,128)(2,1)S(1)} %fusion.20.q_ref, bf16[128,384]{1,0:T(8,128)(2,1)S(1)} %fusion.27.g_ref, bf16[2048,768]{1,0:T(8,128)(2,1)S(1)} %constant_dynamic-update-slice_fusion.5.kv_ref), custom_call_target="tpu_custom_call" | custom-call | flops 2013265920 | bytes 6291456 | tf_op jit(solution)/shard_map/attend_back/pallas_call | solution.py:309
  531.8 7.8 collective-permute-done.76
  553.1 6.0 collective-permute-done.78
  564.1 5.1 collective-permute-start.65
  586.2 5.6 multiply_convert_fusion
  597.9 5.1 collective-permute-start.70
  607.6 7.0 collective-permute-done.74
  631.6 11.1 %collective-permute-done.71 = bf16[112,1536]{1,0:T(8,128)(2,1)S(1)} collective-permute-done((bf16[112,1536]{1,0:T(8,128)(2,1)S(1)}, bf16[112,1536]{1,0:T(8,128)(2,1)S(1)}, u32[]{:S(2)}, u32[]{:S(2)}) %collective-permute-start.71) | collective-permute-done | bytes 344096 | tf_op jit(solution)/shard_map/ppermute | solution.py:405
  653.5 10.5 %attend_back.5 = (bf16[128,384]{1,0:T(8,128)(2,1)S(1)}, bf16[2048,768]{1,0:T(8,128)(2,1)S(1)}) custom-call(s32[18]{0:T(128)S(1)} %get-tuple-element.369.where_ref, bf16[128,384]{1,0:T(8,128)(2,1)S(1)} %copy-done.13, bf16[128,384]{1,0:T(8,128)(2,1)S(1)} %fusion.28.g_ref, bf16[2048,768]{1,0:T(8,128)(2,1)S(1)} %copy-done.6), custom_call_target="tpu_custom_call" | custom-call | flops 2013265920 | bytes 6291456 | tf_op jit(solution)/shard_map/attend_back/pallas_call | solution.py:309
  674.6 11.6 %collective-permute-done.87 = bf16[112,1536]{1,0:T(8,128)(2,1)S(1)} collective-permute-done((bf16[112,1536]{1,0:T(8,128)(2,1)S(1)}, bf16[112,1536]{1,0:T(8,128)(2,1)S(1)}, u32[]{:S(2)}, u32[]{:S(2)}) %collective-permute-start.87) | collective-permute-done | bytes 344096 | tf_op jit(solution)/shard_map/ppermute | solution.py:405
  686.2 6.0 collective-permute-done.88
  698.4 7.4 collective-permute-done.91
  706.3 5.4 collective-permute-done.92
  716.8 9.3 %collective-permute-done.100 = bf16[4,48,768]{2,1,0:T(8,128)(2,1)S(1)} collective-permute-done((bf16[4,48,768]{2,1,0:T(8,128)(2,1)S(1)}, bf16[4,48,768]{2,1,0:T(8,128)(2,1)S(1)}, u32[]{:S(2)}, u32[]{:S(2)}) %collective-permute-start.100) | collective-permute-done | bytes 294944 | tf_op jit(solution)/shard_map/ppermute | solution.py:401
  742.9 10.4 %collective-permute-done.95 = bf16[112,1536]{1,0:T(8,128)(2,1)S(1)} collective-permute-done((bf16[112,1536]{1,0:T(8,128)(2,1)S(1)}, bf16[112,1536]{1,0:T(8,128)(2,1)S(1)}, u32[]{:S(2)}, u32[]{:S(2)}) %collective-permute-start.95) | collective-permute-done | bytes 344096 | tf_op jit(solution)/shard_map/ppermute | solution.py:405
  753.3 6.4 collective-permute-done.96
  762.0 9.7 %collective-permute-done.97 = bf16[5,96,768]{2,1,0:T(8,128)(2,1)S(1)} collective-permute-done((bf16[5,96,768]{2,1,0:T(8,128)(2,1)S(1)}, bf16[5,96,768]{2,1,0:T(8,128)(2,1)S(1)}, u32[]{:S(2)}, u32[]{:S(2)}) %collective-permute-start.97) | collective-permute-done | bytes 737312 | tf_op jit(solution)/shard_map/ppermute | solution.py:401
  777.8 5.5 collective-permute-done.98
  818.0 16.8 %finish.1 = (f32[6,1288,128]{2,1,0:T(8,128)}, f32[6,1288,128]{2,1,0:T(8,128)}, f32[6,1288,128]{2,1,0:T(8,128)}, f32[12,24,736]{2,1,0:T(8,128)}, f32[12,24,736]{2...) custom-call(f32[2]{0:T(128)} %pad_maximum_fusion.47.scal_ref, ...), custom_call_target="tpu_custom_call" | custom-call | tf_op jit(solution)/shard_map/finish/pallas_call | solution.py:186
  (1054 shorter events, 356.6 us)
Async XLA Ops:
  7.2 87.2 %all-gather.5.cloned.1.call-start = ((), (), s32[]{:S(2)}) async-start(), calls=%async_computation | async-start | bytes 6082560 | tf_op jit(solution)/shard_map/all_gather | solution.py:569
  17.1 246.2 %all-gather.7.cloned.1.call-start = ((), (), s32[]{:S(2)}) async-start(), calls=%async_computation.1 | async-start | bytes 10948608 | tf_op jit(solution)/shard_map/all_gather | solution.py:569
  39.0 60.4 %collective-permute-start.2 = (bf16[112,1536]{1,0:T(8,128)(2,1)S(1)}, bf16[112,1536]{1,0:T(8,128)(2,1)S(1)}, u32[]{:S(2)}, u32[]{:S(2)}) collective-permute-start(bf16[112,1536]{1,0:T(8,128)(2,1)S(1)} %get-tuple-element.303), channel_id=1, source_target_pairs={{0,4},{4,8},{8,12},{12,0},{1,5},{5,9},{9,13},{13,1},{2,6},{6,10},{... | collective-permute-start | bytes 1032200 | tf_op jit(solution)/shard_map/ppermute | solution.py:405
  40.5 58.9 %collective-permute-start.3 = (bf16[112,1536]{1,0:T(8,128)(2,1)S(1)}, bf16[112,1536]{1,0:T(8,128)(2,1)S(1)}, u32[]{:S(2)}, u32[]{:S(2)}) collective-permute-start(bf16[112,1536]{1,0:T(8,128)(2,1)S(1)} %get-tuple-element.304), channel_id=1, source_target_pairs={{0,4},{4,8},{8,12},{12,0},{1,5},{5,9},{9,13},{13,1},{2,6},{6,10},{... | collective-permute-start | bytes 1032200 | tf_op jit(solution)/shard_map/ppermute | solution.py:405
  112.7 20.8 %collective-permute-start.5 = (bf16[256,768]{1,0:T(8,128)(2,1)S(1)}, bf16[256,768]{1,0:T(8,128)(2,1)S(1)}, u32[]{:S(2)}, u32[]{:S(2)}) collective-permute-start(bf16[256,768]{1,0:T(8,128)(2,1)S(1)} %pad_maximum_fusion.35), channel_id=1, source_target_pairs={{0,1},{1,0},{2,3},{3,2},{4,5},{5,4},{6,7},{7,6},{8,9},{9,8},{10,11... | collective-permute-start | bytes 1179656 | tf_op jit(solution)/shard_map/ppermute | solution.py:401
  116.5 17.0 %collective-permute-start.7 = (bf16[112,1536]{1,0:T(8,128)(2,1)S(1)}, bf16[112,1536]{1,0:T(8,128)(2,1)S(1)}, u32[]{:S(2)}, u32[]{:S(2)}) collective-permute-start(bf16[112,1536]{1,0:T(8,128)(2,1)S(1)} %copy-done.212), channel_id=1, source_target_pairs={{0,4},{4,8},{8,12},{12,0},{1,5},{5,9},{9,13},{13,1},{2,6},{6,10},{... | collective-permute-start | bytes 1032200 | tf_op jit(solution)/shard_map/ppermute | solution.py:405
  133.6 34.0 %collective-permute-start.8 = (bf16[512,768]{1,0:T(8,128)(2,1)S(1)}, bf16[512,768]{1,0:T(8,128)(2,1)S(1)}, u32[]{:S(2)}, u32[]{:S(2)}) collective-permute-start(bf16[512,768]{1,0:T(8,128)(2,1)S(1)} %pad_maximum_fusion.22), channel_id=1, source_target_pairs={{0,2},{1,3},{2,0},{3,1},{4,6},{5,7},{6,4},{7,5},{8,10},{9,11},{10,... | collective-permute-start | bytes 2359304 | tf_op jit(solution)/shard_map/ppermute | solution.py:401
  134.8 20.2 %collective-permute-start.9 = (bf16[112,1536]{1,0:T(8,128)(2,1)S(1)}, bf16[112,1536]{1,0:T(8,128)(2,1)S(1)}, u32[]{:S(2)}, u32[]{:S(2)}) collective-permute-start(bf16[112,1536]{1,0:T(8,128)(2,1)S(1)} %copy-done.216), channel_id=1, source_target_pairs={{0,4},{4,8},{8,12},{12,0},{1,5},{5,9},{9,13},{13,1},{2,6},{6,10},{... | collective-permute-start | bytes 1032200 | tf_op jit(solution)/shard_map/ppermute | solution.py:405
  135.0 31.9 %collective-permute-start.10 = (bf16[112,1536]{1,0:T(8,128)(2,1)S(1)}, bf16[112,1536]{1,0:T(8,128)(2,1)S(1)}, u32[]{:S(2)}, u32[]{:S(2)}) collective-permute-start(bf16[112,1536]{1,0:T(8,128)(2,1)S(1)} %collective-permute-done.7), channel_id=1, source_target_pairs={{0,4},{4,8},{8,12},{12,0},{1,5},{5,9},{9,13},{13,1},{2,6},{6,10},{... | collective-permute-start | bytes 1032200 | tf_op jit(solution)/shard_map/ppermute | solution.py:405
  184.3 17.1 %collective-permute-start.12 = (bf16[128,1536]{1,0:T(8,128)(2,1)S(1)}, bf16[128,1536]{1,0:T(8,128)(2,1)S(1)}, u32[]{:S(2)}, u32[]{:S(2)}) collective-permute-start(bf16[128,1536]{1,0:T(8,128)(2,1)S(1)} %multiply_convert_fusion.9), channel_id=1, source_target_pairs={{0,1},{1,0},{2,3},{3,2},{4,5},{5,4},{6,7},{7,6},{8,9},{9,8},{10,11... | collective-permute-start | bytes 1179656 | tf_op jit(solution)/shard_map/ppermute | solution.py:401
  185.5 15.8 %collective-permute-start.13 = (bf16[112,1536]{1,0:T(8,128)(2,1)S(1)}, bf16[112,1536]{1,0:T(8,128)(2,1)S(1)}, u32[]{:S(2)}, u32[]{:S(2)}) collective-permute-start(bf16[112,1536]{1,0:T(8,128)(2,1)S(1)} %copy-done.229), channel_id=1, source_target_pairs={{0,4},{4,8},{8,12},{12,0},{1,5},{5,9},{9,13},{13,1},{2,6},{6,10},{... | collective-permute-start | bytes 1032200 | tf_op jit(solution)/shard_map/ppermute | solution.py:405
  201.4 16.1 %collective-permute-start.14 = (bf16[256,1536]{1,0:T(8,128)(2,1)S(1)}, bf16[256,1536]{1,0:T(8,128)(2,1)S(1)}, u32[]{:S(2)}, u32[]{:S(2)}) collective-permute-start(bf16[256,1536]{1,0:T(8,128)(2,1)S(1)} %pad_maximum_fusion.23), channel_id=1, source_target_pairs={{0,2},{1,3},{2,0},{3,1},{4,6},{5,7},{6,4},{7,5},{8,10},{9,11},{10,... | collective-permute-start | bytes 2359304 | tf_op jit(solution)/shard_map/ppermute | solution.py:401
  203.2 14.3 %collective-permute-start.15 = (bf16[112,1536]{1,0:T(8,128)(2,1)S(1)}, bf16[112,1536]{1,0:T(8,128)(2,1)S(1)}, u32[]{:S(2)}, u32[]{:S(2)}) collective-permute-start(bf16[112,1536]{1,0:T(8,128)(2,1)S(1)} %copy-done.226), channel_id=1, source_target_pairs={{0,4},{4,8},{8,12},{12,0},{1,5},{5,9},{9,13},{13,1},{2,6},{6,10},{... | collective-permute-start | bytes 1032200 | tf_op jit(solution)/shard_map/ppermute | solution.py:405
  238.2 15.1 %collective-permute-start.19 = (bf16[256,1536]{1,0:T(8,128)(2,1)S(1)}, bf16[256,1536]{1,0:T(8,128)(2,1)S(1)}, u32[]{:S(2)}, u32[]{:S(2)}) collective-permute-start(bf16[256,1536]{1,0:T(8,128)(2,1)S(1)} %slice.1647), channel_id=1, source_target_pairs={{0,2},{1,3},{2,0},{3,1},{4,6},{5,7},{6,4},{7,5},{8,10},{9,11},{10,... | collective-permute-start | bytes 2359304 | tf_op jit(solution)/shard_map/ppermute | solution.py:401
  240.5 20.0 %collective-permute-start.23 = (bf16[112,1536]{1,0:T(8,128)(2,1)S(1)}, bf16[112,1536]{1,0:T(8,128)(2,1)}, u32[]{:S(2)}, u32[]{:S(2)}) collective-permute-start(bf16[112,1536]{1,0:T(8,128)(2,1)S(1)} %get-tuple-element.301), channel_id=1, source_target_pairs={{0,4},{4,8},{8,12},{12,0},{1,5},{5,9},{9,13},{13,1},{2,6},{6,10},{... | collective-permute-start | bytes 1032200 | tf_op jit(solution)/shard_map/ppermute | solution.py:405
  255.5 24.3 %collective-permute-start.26 = (bf16[112,1536]{1,0:T(8,128)(2,1)}, bf16[112,1536]{1,0:T(8,128)(2,1)}, u32[]{:S(2)}, u32[]{:S(2)}) collective-permute-start(bf16[112,1536]{1,0:T(8,128)(2,1)} %collective-permute-done.21), channel_id=1, source_target_pairs={{0,4},{4,8},{8,12},{12,0},{1,5},{5,9},{9,13},{13,1},{2,6},{6,10},{... | collective-permute-start | bytes 1032200 | tf_op jit(solution)/shard_map/ppermute | solution.py:405
  261.5 34.9 %collective-permute-start.28 = (bf16[112,1536]{1,0:T(8,128)(2,1)}, bf16[112,1536]{1,0:T(8,128)(2,1)}, u32[]{:S(2)}, u32[]{:S(2)}) collective-permute-start(bf16[112,1536]{1,0:T(8,128)(2,1)} %collective-permute-done.23), channel_id=1, source_target_pairs={{0,4},{4,8},{8,12},{12,0},{1,5},{5,9},{9,13},{13,1},{2,6},{6,10},{... | collective-permute-start | bytes 1032200 | tf_op jit(solution)/shard_map/ppermute | solution.py:405
  286.4 15.2 %collective-permute-start.27 = (bf16[512,768]{1,0:T(8,128)(2,1)S(1)}, bf16[512,768]{1,0:T(8,128)(2,1)S(1)}, u32[]{:S(2)}, u32[]{:S(2)}) collective-permute-start(bf16[512,768]{1,0:T(8,128)(2,1)S(1)} %pad_maximum_fusion.25), channel_id=1, source_target_pairs={{0,2},{1,3},{2,0},{3,1},{4,6},{5,7},{6,4},{7,5},{8,10},{9,11},{10,... | collective-permute-start | bytes 2359304 | tf_op jit(solution)/shard_map/ppermute | solution.py:401
  303.1 25.1 %collective-permute-start.29 = (bf16[1024,768]{1,0:T(8,128)(2,1)}, bf16[1024,768]{1,0:T(8,128)(2,1)}, u32[]{:S(2)}, u32[]{:S(2)}) collective-permute-start(bf16[1024,768]{1,0:T(8,128)(2,1)} %pad_maximum_fusion.10), channel_id=1, source_target_pairs={{0,16},{16,0},{1,17},{17,1},{2,18},{18,2},{3,19},{19,3},{4,20},{20... | collective-permute-start | bytes 4718600 | tf_op jit(solution)/shard_map/ppermute | solution.py:393
  310.6 16.1 %collective-permute-start.33 = (bf16[512,768]{1,0:T(8,128)(2,1)S(1)}, bf16[512,768]{1,0:T(8,128)(2,1)S(1)}, u32[]{:S(2)}, u32[]{:S(2)}) collective-permute-start(bf16[512,768]{1,0:T(8,128)(2,1)S(1)} %pad_maximum_fusion.26), channel_id=1, source_target_pairs={{0,2},{1,3},{2,0},{3,1},{4,6},{5,7},{6,4},{7,5},{8,10},{9,11},{10,... | collective-permute-start | bytes 2359304 | tf_op jit(solution)/shard_map/ppermute | solution.py:401
  466.2 74.3 %collective-permute-start.58 = (bf16[112,1536]{1,0:T(8,128)(2,1)S(1)}, bf16[112,1536]{1,0:T(8,128)(2,1)S(1)}, u32[]{:S(2)}, u32[]{:S(2)}) collective-permute-start(bf16[112,1536]{1,0:T(8,128)(2,1)S(1)} %slice.1168), channel_id=1, source_target_pairs={{0,12},{4,0},{8,4},{12,8},{1,13},{5,1},{9,5},{13,9},{2,14},{6,2},{... | collective-permute-start | bytes 1032200 | tf_op jit(solution)/shard_map/ppermute | solution.py:405
  466.3 18.3 %collective-permute-start.52 = (bf16[112,1536]{1,0:T(8,128)(2,1)S(1)}, bf16[112,1536]{1,0:T(8,128)(2,1)S(1)}, u32[]{:S(2)}, u32[]{:S(2)}) collective-permute-start(bf16[112,1536]{1,0:T(8,128)(2,1)S(1)} %slice.1159), channel_id=1, source_target_pairs={{0,12},{4,0},{8,4},{12,8},{1,13},{5,1},{9,5},{13,9},{2,14},{6,2},{... | collective-permute-start | bytes 1032200 | tf_op jit(solution)/shard_map/ppermute | solution.py:405
  475.6 42.4 %collective-permute-start.55 = (bf16[112,1536]{1,0:T(8,128)(2,1)S(1)}, bf16[112,1536]{1,0:T(8,128)(2,1)S(1)}, u32[]{:S(2)}, u32[]{:S(2)}) collective-permute-start(bf16[112,1536]{1,0:T(8,128)(2,1)S(1)} %add_convert_fusion.13), channel_id=1, source_target_pairs={{0,12},{4,0},{8,4},{12,8},{1,13},{5,1},{9,5},{13,9},{2,14},{6,2},{... | collective-permute-start | bytes 1032200 | tf_op jit(solution)/shard_map/ppermute | solution.py:405
  500.4 14.1 %collective-permute-start.53 = (bf16[1024,768]{1,0:T(8,128)(2,1)S(1)}, bf16[1024,768]{1,0:T(8,128)(2,1)S(1)}, u32[]{:S(2)}, u32[]{:S(2)}) collective-permute-start(bf16[1024,768]{1,0:T(8,128)(2,1)S(1)} %slice.981), channel_id=1, source_target_pairs={{0,16},{16,0},{1,17},{17,1},{2,18},{18,2},{3,19},{19,3},{4,20},{20... | collective-permute-start | bytes 4718600 | tf_op jit(solution)/shard_map/ppermute | solution.py:393
  517.2 22.4 %collective-permute-start.76 = (bf16[512,768]{1,0:T(8,128)(2,1)S(1)}, bf16[512,768]{1,0:T(8,128)(2,1)S(1)}, u32[]{:S(2)}, u32[]{:S(2)}) collective-permute-start(bf16[512,768]{1,0:T(8,128)(2,1)S(1)} %slice.1642), channel_id=1, source_target_pairs={{0,2},{1,3},{2,0},{3,1},{4,6},{5,7},{6,4},{7,5},{8,10},{9,11},{10,... | collective-permute-start | bytes 2359304 | tf_op jit(solution)/shard_map/ppermute | solution.py:401
  527.0 13.5 %collective-permute-start.59 = (bf16[112,1536]{1,0:T(8,128)(2,1)S(1)}, bf16[112,1536]{1,0:T(8,128)(2,1)S(1)}, u32[]{:S(2)}, u32[]{:S(2)}) collective-permute-start(bf16[112,1536]{1,0:T(8,128)(2,1)S(1)} %add_convert_fusion.11), channel_id=1, source_target_pairs={{0,12},{4,0},{8,4},{12,8},{1,13},{5,1},{9,5},{13,9},{2,14},{6,2},{... | collective-permute-start | bytes 1032200 | tf_op jit(solution)/shard_map/ppermute | solution.py:405
  528.8 33.6 %collective-permute-start.62 = (bf16[112,1536]{1,0:T(8,128)(2,1)S(1)}, bf16[112,1536]{1,0:T(8,128)(2,1)S(1)}, u32[]{:S(2)}, u32[]{:S(2)}) collective-permute-start(bf16[112,1536]{1,0:T(8,128)(2,1)S(1)} %add_convert_fusion.10), channel_id=1, source_target_pairs={{0,12},{4,0},{8,4},{12,8},{1,13},{5,1},{9,5},{13,9},{2,14},{6,2},{... | collective-permute-start | bytes 1032200 | tf_op jit(solution)/shard_map/ppermute | solution.py:405
  541.2 21.2 %collective-permute-start.63 = (bf16[112,1536]{1,0:T(8,128)(2,1)S(1)}, bf16[112,1536]{1,0:T(8,128)(2,1)S(1)}, u32[]{:S(2)}, u32[]{:S(2)}) collective-permute-start(bf16[112,1536]{1,0:T(8,128)(2,1)S(1)} %add_convert_fusion.9), channel_id=1, source_target_pairs={{0,12},{4,0},{8,4},{12,8},{1,13},{5,1},{9,5},{13,9},{2,14},{6,2},{... | collective-permute-start | bytes 1032200 | tf_op jit(solution)/shard_map/ppermute | solution.py:405
  560.5 20.6 %collective-permute-start.79 = (bf16[4,384,768]{2,1,0:T(8,128)(2,1)S(1)}, bf16[4,384,768]{2,1,0:T(8,128)(2,1)S(1)}, u32[]{:S(2)}, u32[]{:S(2)}) collective-permute-start(bf16[4,384,768]{2,1,0:T(8,128)(2,1)S(1)} %convolution_convert_fusion.12), channel_id=1, source_target_pairs={{0,16},{16,0},{1,17},{17,1},{2,18},{18,2},{3,19},{19,3},{4,20},{20... | collective-permute-start | bytes 7077896 | tf_op jit(solution)/shard_map/ppermute | solution.py:393
  561.6 22.1 %collective-permute-start.67 = (bf16[5,384,768]{2,1,0:T(8,128)(2,1)S(1)}, bf16[5,384,768]{2,1,0:T(8,128)(2,1)S(1)}, u32[]{:S(2)}, u32[]{:S(2)}) collective-permute-start(bf16[5,384,768]{2,1,0:T(8,128)(2,1)S(1)} %convolution_convert_fusion.11), channel_id=1, source_target_pairs={{0,16},{16,0},{1,17},{17,1},{2,18},{18,2},{3,19},{19,3},{4,20},{20... | collective-permute-start | bytes 8847368 | tf_op jit(solution)/shard_map/ppermute | solution.py:393
  582.5 44.3 %collective-permute-start.81 = (bf16[4,192,768]{2,1,0:T(8,128)(2,1)S(1)}, bf16[4,192,768]{2,1,0:T(8,128)(2,1)S(1)}, u32[]{:S(2)}, u32[]{:S(2)}) collective-permute-start(bf16[4,192,768]{2,1,0:T(8,128)(2,1)S(1)} %slice.1640), channel_id=1, source_target_pairs={{0,1},{1,0},{2,3},{3,2},{4,5},{5,4},{6,7},{7,6},{8,9},{9,8},{10,11... | collective-permute-start | bytes 3538952 | tf_op jit(solution)/shard_map/ppermute | solution.py:401
  584.8 29.8 %collective-permute-start.74 = (bf16[5,192,768]{2,1,0:T(8,128)(2,1)S(1)}, bf16[5,192,768]{2,1,0:T(8,128)(2,1)S(1)}, u32[]{:S(2)}, u32[]{:S(2)}) collective-permute-start(bf16[5,192,768]{2,1,0:T(8,128)(2,1)S(1)} %slice.1639), channel_id=1, source_target_pairs={{0,1},{1,0},{2,3},{3,2},{4,5},{5,4},{6,7},{7,6},{8,9},{9,8},{10,11... | collective-permute-start | bytes 4423688 | tf_op jit(solution)/shard_map/ppermute | solution.py:401
  596.0 20.6 %collective-permute-start.68 = (bf16[512,1536]{1,0:T(8,128)(2,1)}, bf16[512,1536]{1,0:T(8,128)(2,1)S(1)}, u32[]{:S(2)}, u32[]{:S(2)}) collective-permute-start(bf16[512,1536]{1,0:T(8,128)(2,1)} %fusion.1), channel_id=1, source_target_pairs={{0,16},{16,0},{1,17},{17,1},{2,18},{18,2},{3,19},{19,3},{4,20},{20... | collective-permute-start | bytes 4718600 | tf_op jit(solution)/shard_map/ppermute | solution.py:393
  597.9 31.7 %collective-permute-start.70 = (bf16[112,1536]{1,0:T(8,128)(2,1)S(1)}, bf16[112,1536]{1,0:T(8,128)(2,1)S(1)}, u32[]{:S(2)}, u32[]{:S(2)}) collective-permute-start(bf16[112,1536]{1,0:T(8,128)(2,1)S(1)} %slice.1183), channel_id=1, source_target_pairs={{0,12},{4,0},{8,4},{12,8},{1,13},{5,1},{9,5},{13,9},{2,14},{6,2},{... | collective-permute-start | bytes 1032200 | tf_op jit(solution)/shard_map/ppermute | solution.py:405
  619.7 23.1 %collective-permute-start.69 = (bf16[256,1536]{1,0:T(8,128)(2,1)S(1)}, bf16[256,1536]{1,0:T(8,128)(2,1)S(1)}, u32[]{:S(2)}, u32[]{:S(2)}) collective-permute-start(bf16[256,1536]{1,0:T(8,128)(2,1)S(1)} %slice.1643), channel_id=1, source_target_pairs={{0,2},{1,3},{2,0},{3,1},{4,6},{5,7},{6,4},{7,5},{8,10},{9,11},{10,... | collective-permute-start | bytes 2359304 | tf_op jit(solution)/shard_map/ppermute | solution.py:401
  622.1 26.5 %collective-permute-start.73 = (bf16[112,1536]{1,0:T(8,128)(2,1)S(1)}, bf16[112,1536]{1,0:T(8,128)(2,1)S(1)}, u32[]{:S(2)}, u32[]{:S(2)}) collective-permute-start(bf16[112,1536]{1,0:T(8,128)(2,1)S(1)} %slice.1188), channel_id=1, source_target_pairs={{0,12},{4,0},{8,4},{12,8},{1,13},{5,1},{9,5},{13,9},{2,14},{6,2},{... | collective-permute-start | bytes 1032200 | tf_op jit(solution)/shard_map/ppermute | solution.py:405
  626.8 15.9 %collective-permute-start.71 = (bf16[112,1536]{1,0:T(8,128)(2,1)S(1)}, bf16[112,1536]{1,0:T(8,128)(2,1)S(1)}, u32[]{:S(2)}, u32[]{:S(2)}) collective-permute-start(bf16[112,1536]{1,0:T(8,128)(2,1)S(1)} %slice.1184), channel_id=1, source_target_pairs={{0,12},{4,0},{8,4},{12,8},{1,13},{5,1},{9,5},{13,9},{2,14},{6,2},{... | collective-permute-start | bytes 1032200 | tf_op jit(solution)/shard_map/ppermute | solution.py:405
  627.4 16.8 %collective-permute-start.83 = (bf16[4,96,768]{2,1,0:T(8,128)(2,1)S(1)}, bf16[4,96,768]{2,1,0:T(8,128)(2,1)S(1)}, u32[]{:S(2)}, u32[]{:S(2)}) collective-permute-start(bf16[4,96,768]{2,1,0:T(8,128)(2,1)S(1)} %slice.1650), channel_id=1, source_target_pairs={{0,2},{1,3},{2,0},{3,1},{4,6},{5,7},{6,4},{7,5},{8,10},{9,11},{10,... | collective-permute-start | bytes 1769480 | tf_op jit(solution)/shard_map/ppermute | solution.py:401
  629.6 18.9 %collective-permute-start.82 = (bf16[5,48,768]{2,1,0:T(8,128)(2,1)S(1)}, bf16[5,48,768]{2,1,0:T(8,128)(2,1)S(1)}, u32[]{:S(2)}, u32[]{:S(2)}) collective-permute-start(bf16[5,48,768]{2,1,0:T(8,128)(2,1)S(1)} %slice.1655), channel_id=1, source_target_pairs={{0,4},{1,5},{2,6},{3,7},{4,0},{5,1},{6,2},{7,3},{8,12},{9,13},{10,... | collective-permute-start | bytes 1105928 | tf_op jit(solution)/shard_map/ppermute | solution.py:401
  666.0 32.4 %collective-permute-start.90 = (bf16[112,1536]{1,0:T(8,128)(2,1)S(1)}, bf16[112,1536]{1,0:T(8,128)(2,1)S(1)}, u32[]{:S(2)}, u32[]{:S(2)}) collective-permute-start(bf16[112,1536]{1,0:T(8,128)(2,1)S(1)} %add_convert_fusion.5), channel_id=1, source_target_pairs={{0,12},{4,0},{8,4},{12,8},{1,13},{5,1},{9,5},{13,9},{2,14},{6,2},{... | collective-permute-start | bytes 1032200 | tf_op jit(solution)/shard_map/ppermute | solution.py:405
  670.4 15.8 %collective-permute-start.87 = (bf16[112,1536]{1,0:T(8,128)(2,1)S(1)}, bf16[112,1536]{1,0:T(8,128)(2,1)S(1)}, u32[]{:S(2)}, u32[]{:S(2)}) collective-permute-start(bf16[112,1536]{1,0:T(8,128)(2,1)S(1)} %add_convert_fusion.7), channel_id=1, source_target_pairs={{0,12},{4,0},{8,4},{12,8},{1,13},{5,1},{9,5},{13,9},{2,14},{6,2},{... | collective-permute-start | bytes 1032200 | tf_op jit(solution)/shard_map/ppermute | solution.py:405
  670.9 21.3 %collective-permute-start.86 = (bf16[512,768]{1,0:T(8,128)(2,1)S(1)}, bf16[512,768]{1,0:T(8,128)(2,1)S(1)}, u32[]{:S(2)}, u32[]{:S(2)}) collective-permute-start(bf16[512,768]{1,0:T(8,128)(2,1)S(1)} %slice.1641), channel_id=1, source_target_pairs={{0,2},{1,3},{2,0},{3,1},{4,6},{5,7},{6,4},{7,5},{8,10},{9,11},{10,... | collective-permute-start | bytes 2359304 | tf_op jit(solution)/shard_map/ppermute | solution.py:401
  672.9 19.2 %collective-permute-start.88 = (bf16[112,1536]{1,0:T(8,128)(2,1)S(1)}, bf16[112,1536]{1,0:T(8,128)(2,1)S(1)}, u32[]{:S(2)}, u32[]{:S(2)}) collective-permute-start(bf16[112,1536]{1,0:T(8,128)(2,1)S(1)} %add_convert_fusion.6), channel_id=1, source_target_pairs={{0,12},{4,0},{8,4},{12,8},{1,13},{5,1},{9,5},{13,9},{2,14},{6,2},{... | collective-permute-start | bytes 1032200 | tf_op jit(solution)/shard_map/ppermute | solution.py:405
  716.5 13.6 %collective-permute-start.93 = (bf16[5,384,768]{2,1,0:T(8,128)(2,1)S(1)}, bf16[5,384,768]{2,1,0:T(8,128)(2,1)S(1)}, u32[]{:S(2)}, u32[]{:S(2)}) collective-permute-start(bf16[5,384,768]{2,1,0:T(8,128)(2,1)S(1)} %convolution_convert_fusion.10), channel_id=1, source_target_pairs={{0,16},{16,0},{1,17},{17,1},{2,18},{18,2},{3,19},{19,3},{4,20},{20... | collective-permute-start | bytes 8847368 | tf_op jit(solution)/shard_map/ppermute | solution.py:393
  731.4 28.4 %collective-permute-start.94 = (bf16[5,192,768]{2,1,0:T(8,128)(2,1)S(1)}, bf16[5,192,768]{2,1,0:T(8,128)(2,1)S(1)}, u32[]{:S(2)}, u32[]{:S(2)}) collective-permute-start(bf16[5,192,768]{2,1,0:T(8,128)(2,1)S(1)} %slice.1638), channel_id=1, source_target_pairs={{0,1},{1,0},{2,3},{3,2},{4,5},{5,4},{6,7},{7,6},{8,9},{9,8},{10,11... | collective-permute-start | bytes 4423688 | tf_op jit(solution)/shard_map/ppermute | solution.py:401
  737.8 38.6 %collective-permute-start.102 = (bf16[5,24,768]{2,1,0:T(8,128)(2,1)S(1)}, bf16[5,24,768]{2,1,0:T(8,128)(2,1)S(1)}, u32[]{:S(2)}, u32[]{:S(2)}) collective-permute-start(bf16[5,24,768]{2,1,0:T(8,128)(2,1)S(1)} %slice.1660), channel_id=1, source_target_pairs={{0,8},{1,9},{2,10},{3,11},{4,12},{5,13},{6,14},{7,15},{8,0},{9,1},... | collective-permute-start | bytes 552968 | tf_op jit(solution)/shard_map/ppermute | solution.py:401
  738.0 15.3 %collective-permute-start.95 = (bf16[112,1536]{1,0:T(8,128)(2,1)S(1)}, bf16[112,1536]{1,0:T(8,128)(2,1)S(1)}, u32[]{:S(2)}, u32[]{:S(2)}) collective-permute-start(bf16[112,1536]{1,0:T(8,128)(2,1)S(1)} %add_convert_fusion.3), channel_id=1, source_target_pairs={{0,12},{4,0},{8,4},{12,8},{1,13},{5,1},{9,5},{13,9},{2,14},{6,2},{... | collective-permute-start | bytes 1032200 | tf_op jit(solution)/shard_map/ppermute | solution.py:405
  741.7 18.1 %collective-permute-start.96 = (bf16[112,1536]{1,0:T(8,128)(2,1)S(1)}, bf16[112,1536]{1,0:T(8,128)(2,1)S(1)}, u32[]{:S(2)}, u32[]{:S(2)}) collective-permute-start(bf16[112,1536]{1,0:T(8,128)(2,1)S(1)} %add_convert_fusion.2), channel_id=1, source_target_pairs={{0,12},{4,0},{8,4},{12,8},{1,13},{5,1},{9,5},{13,9},{2,14},{6,2},{... | collective-permute-start | bytes 1032200 | tf_op jit(solution)/shard_map/ppermute | solution.py:405
  (320 other events, 2766.4 us)
Sparse Core Ops, SparseCore 0:
  17.2 77.1 all-gather.4
  97.3 118.3 all-gather.6

commit v4 on v3

--- a/solution.py
+++ b/solution.py
@@ -28,6 +28,7 @@
 DECAY_STEP = 0.005
 MASKED = -1000000000.0
 PERIOD = 896
+KEYS = 256
 MIB = 1024 * 1024
 BF = jnp.bfloat16
 F32 = jnp.float32
@@ -259,7 +260,7 @@
     )(where, queries, kv)
 
 
-def attend_back_kernel(causal, where_ref, q_ref, g_ref, kv_ref, dq_ref, dkv_ref, pos_ref):
+def attend_back_kernel(causal, where_ref, q_ref, g_ref, kv_ref, dq_ref, dkv_ref, pos_ref, s_ref, dp_ref):
     count = q_ref.shape[0]
     length = kv_ref.shape[0]
     blocks = length // count
@@ -276,30 +277,56 @@
     for p in range(3):
         lanes = slice(p * LANES, (p + 1) * LANES)
         values = slice(INNER + p * LANES, INNER + (p + 1) * LANES)
-        allowed = pos_ref[...] <= last
         queries = q_ref[:, lanes] * scale
         grads = g_ref[:, lanes]
-        d_query, d_key, d_value = [], None, None
+        d_query = []
         for h in range(2):
             own_q = jnp.where(head_lanes(queries.shape, h), queries, jnp.zeros_like(queries))
             own_g = jnp.where(head_lanes(grads.shape, h), grads, jnp.zeros_like(grads))
-            scores = dot_nt(kv_ref[:, lanes], own_q)
-            scores = jnp.where(allowed, scores, MASKED)
-            raised = jnp.exp(scores - jnp.max(scores, axis=0, keepdims=True))
-            probs = raised * (1.0 / jnp.sum(raised, axis=0, keepdims=True))
-            d_probs = dot_nt(kv_ref[:, values], own_g)
-            inner = jnp.sum(probs * d_probs, axis=0, keepdims=True)
-            d_scores = (probs * (d_probs - inner)).astype(BF)
-            d_query.append(dot_tn(d_scores, kv_ref[:, lanes]) * scale)
-            key_part = dot_nn(d_scores, own_q)
-            value_part = dot_nn(probs.astype(BF), own_g)
-            d_key = key_part if h == 0 else d_key + key_part
-            d_value = value_part if h == 0 else d_value + value_part
+
+            def rows(i):
+                return pl.ds(pl.multiple_of(i * KEYS, KEYS), KEYS)
+
+            def score_pass(i, peak):
+                at = rows(i)
+                scores = dot_nt(kv_ref[at, lanes], own_q)
+                scores = jnp.where(pos_ref[at, :] <= last, scores, MASKED)
+                s_ref[at, :] = scores
+                return jnp.maximum(peak, jnp.max(scores, axis=0, keepdims=True))
+
+            def sum_pass(i, sums):
+                at = rows(i)
+                raised = jnp.exp(s_ref[at, :] - peak)
+                d_probs = dot_nt(kv_ref[at, values], own_g)
+                s_ref[at, :] = raised
+                dp_ref[at, :] = d_probs
+                return (
+                    sums[0] + jnp.sum(raised, axis=0, keepdims=True),
+                    sums[1] + jnp.sum(raised * d_probs, axis=0, keepdims=True),
+                )
+
+            def grad_pass(i, total):
+                at = rows(i)
+                probs = s_ref[at, :] * share
+                d_scores = (probs * (dp_ref[at, :] - inner)).astype(BF)
+                key_part = dot_nn(d_scores, own_q).astype(BF)
+                value_part = dot_nn(probs.astype(BF), own_g).astype(BF)
+                dkv_ref[at, lanes] = key_part if h == 0 else dkv_ref[at, lanes] + key_part
+                dkv_ref[at, values] = value_part if h == 0 else dkv_ref[at, values] + value_part
+                return total + dot_tn(d_scores, kv_ref[at, lanes])
+
+            steps = length // KEYS
+            none = jnp.zeros((1, count), F32)
+            peak = lax.fori_loop(0, steps, score_pass, none + MASKED, unroll=True)
+            total, weighted = lax.fori_loop(0, steps, sum_pass, (none, none), unroll=True)
+            share = 1.0 / total
+            inner = weighted * share
+            d_query.append(
+                lax.fori_loop(0, steps, grad_pass, jnp.zeros((count, LANES), F32), unroll=True) * scale
+            )
         dq_ref[:, lanes] = jnp.where(
             head_lanes(d_query[0].shape, 0), d_query[0], d_query[1]
         ).astype(BF)
-        dkv_ref[:, lanes] = d_key.astype(BF)
-        dkv_ref[:, values] = d_value.astype(BF)
 
 
 def attend_back(where, queries, grads, kv, causal):
@@ -314,7 +341,11 @@
         ),
         in_specs=[pl.BlockSpec(memory_space=pltpu.SMEM)] + [vmem] * 3,
         out_specs=(vmem,) * 2,
-        scratch_shapes=[pltpu.VMEM((length, count), jnp.int32)],
+        scratch_shapes=[
+            pltpu.VMEM((length, count), jnp.int32),
+            pltpu.VMEM((length, count), F32),
+            pltpu.VMEM((length, count), F32),
+        ],
         compiler_params=pltpu.CompilerParams(vmem_limit_bytes=8 * MIB + 8192 * length),
         cost_estimate=pl.CostEstimate(
             flops=10 * count * length * INNER * 2,

time: 853 us -> 844 us (0.989)
  Pallas kernels: 73.3 us -> 64.3 us
    pallas_call x3, Pallas kernels: 31.6 us -> 22.6 us  [attend_back(): pl.pallas_call(functools.partial(attend_back_kernel, causal), out_shape=(...]
  transfers between devices with their start and end apart: 111 -> 111, of which waited for: 63 -> 63; matrix products, arithmetic and copies ran while one was open for 17% -> 17% of each run, Pallas kernels for 5% -> 4%
where the time goes in v4:
time: 844 us; the launch traced here: 834 us
  waiting for transfers between devices  428 us (51%)
  starting transfers between devices  117 us (14%)
  matrix products  90.4 us (11%)
  Pallas kernels  64.3 us (8%)
  other arithmetic  57.9 us (7%)
  local copies, waits for them, and re-layouts  48.7 us (6%)
  between operations  28 us (3%)
    ppermute x36, waiting for transfers between devices, ring(): return lax.ppermute(value, 'z', [(i, (i + step) % n) for i in range(n)])  207 us
    ppermute x46, waiting for transfers between devices, swap_by_core(): return lax.ppermute(value, ('c', 'z', 'y', 'x'), pairs)  142 us
    all_gather x2, waiting for transfers between devices, gather_tiles(): full = lax.all_gather(tiles[:, None], everywhere, axis=1, tiled=True)  52.5 us
    ppermute x46, starting transfers between devices, swap_by_core(): return lax.ppermute(value, ('c', 'z', 'y', 'x'), pairs)  51.4 us
    ppermute x36, starting transfers between devices, ring(): return lax.ppermute(value, 'z', [(i, (i + step) % n) for i in range(n)])  49 us
    dot_general x32, matrix products, dot_nt(): lax.dot_general(a, b, (((1,), (1,)), ((), ())), preferred_element_type=F32)  36.8 us
    dot_general x48, matrix products, dot_nn(): lax.dot_general(a, b, (((1,), (0,)), ((), ())), preferred_element_type=F32)  35.7 us
    ppermute x24, waiting for transfers between devices, swap(): return lax.ppermute(value, bit, [(0, 1), (1, 0)])  23.2 us
  transfers between devices with their start and end apart: 111, of which 63 were waited for; matrix products, arithmetic and copies ran while one was open for 17% of the time, Pallas kernels for 4%

profile of v4, /device:TPU:0, one launch (start us, length us, event | category | flops | bytes accessed | tf_op | source)
XLA Modules:
  0.0 834.3 jit_solution(14951309102658387151)
XLA Ops:
  27.9 5.5 collective-permute-start.20
  41.8 52.5 %all-gather.5.cloned.1.call-done = bf16[5,768,768]{2,1,0:T(8,128)(2,1)} async-done(((bf16[5,24,768]{2,1,0:T(8,128)(2,1)}), bf16[5,768,768]{2,1,0:T(8,128)(2,1)}) %all-gather.5.cloned.1.call-update) | async-done | bytes 5898256 | tf_op jit(solution)/shard_map/all_gather | solution.py:600
  104.3 8.4 %collective-permute-done.4 = bf16[128,768]{1,0:T(8,128)(2,1)S(1)} collective-permute-done((bf16[128,768]{1,0:T(8,128)(2,1)S(1)}, bf16[128,768]{1,0:T(8,128)(2,1)S(1)}, u32[]{:S(2)}, u32[]{:S(2)}) %collective-permute-start.4) | collective-permute-done | bytes 196640 | tf_op jit(solution)/shard_map/ppermute | solution.py:432
  116.5 10.6 %collective-permute-done.6 = bf16[112,1536]{1,0:T(8,128)(2,1)S(1)} collective-permute-done((bf16[112,1536]{1,0:T(8,128)(2,1)S(1)}, bf16[112,1536]{1,0:T(8,128)(2,1)S(1)}, u32[]{:S(2)}, u32[]{:S(2)}) %collective-permute-start.6) | collective-permute-done | bytes 344096 | tf_op jit(solution)/shard_map/ppermute | solution.py:436
  127.2 6.4 collective-permute-done.7
  136.3 18.7 %collective-permute-done.9 = bf16[112,1536]{1,0:T(8,128)(2,1)S(1)} collective-permute-done((bf16[112,1536]{1,0:T(8,128)(2,1)S(1)}, bf16[112,1536]{1,0:T(8,128)(2,1)S(1)}, u32[]{:S(2)}, u32[]{:S(2)}) %collective-permute-start.9) | collective-permute-done | bytes 344096 | tf_op jit(solution)/shard_map/ppermute | solution.py:436
  155.0 11.9 %collective-permute-done.10 = bf16[112,1536]{1,0:T(8,128)(2,1)S(1)} collective-permute-done((bf16[112,1536]{1,0:T(8,128)(2,1)S(1)}, bf16[112,1536]{1,0:T(8,128)(2,1)S(1)}, u32[]{:S(2)}, u32[]{:S(2)}) %collective-permute-start.10) | collective-permute-done | bytes 344096 | tf_op jit(solution)/shard_map/ppermute | solution.py:436
  177.1 4.9 attend.3
  185.5 15.8 %collective-permute-done.13 = bf16[112,1536]{1,0:T(8,128)(2,1)S(1)} collective-permute-done((bf16[112,1536]{1,0:T(8,128)(2,1)S(1)}, bf16[112,1536]{1,0:T(8,128)(2,1)S(1)}, u32[]{:S(2)}, u32[]{:S(2)}) %collective-permute-start.13) | collective-permute-done | bytes 344096 | tf_op jit(solution)/shard_map/ppermute | solution.py:436
  204.0 13.6 %collective-permute-done.15 = bf16[112,1536]{1,0:T(8,128)(2,1)S(1)} collective-permute-done((bf16[112,1536]{1,0:T(8,128)(2,1)S(1)}, bf16[112,1536]{1,0:T(8,128)(2,1)S(1)}, u32[]{:S(2)}, u32[]{:S(2)}) %collective-permute-start.15) | collective-permute-done | bytes 344096 | tf_op jit(solution)/shard_map/ppermute | solution.py:436
  241.9 11.5 %collective-permute-done.21 = bf16[112,1536]{1,0:T(8,128)(2,1)} collective-permute-done((bf16[112,1536]{1,0:T(8,128)(2,1)S(1)}, bf16[112,1536]{1,0:T(8,128)(2,1)}, u32[]{:S(2)}, u32[]{:S(2)}) %collective-permute-start.21) | collective-permute-done | bytes 344096 | tf_op jit(solution)/shard_map/ppermute | solution.py:436
  255.5 5.0 collective-permute-done.23
  263.2 6.9 fusion.212
  272.0 6.5 collective-permute-done.24
  279.8 6.5 collective-permute-done.25
  289.4 5.7 collective-permute-done.30
  296.5 5.2 collective-permute-done.27
  315.0 11.6 %collective-permute-done.34 = bf16[112,1536]{1,0:T(8,128)(2,1)S(1)} collective-permute-done((bf16[112,1536]{1,0:T(8,128)(2,1)}, bf16[112,1536]{1,0:T(8,128)(2,1)S(1)}, u32[]{:S(2)}, u32[]{:S(2)}) %collective-permute-start.34) | collective-permute-done | bytes 344096 | tf_op jit(solution)/shard_map/ppermute | solution.py:436
  329.7 5.0 attend.4
  337.1 4.9 attend.5
  344.8 12.5 %collective-permute-done.37 = bf16[112,1536]{1,0:T(8,128)(2,1)S(1)} collective-permute-done((bf16[112,1536]{1,0:T(8,128)(2,1)S(1)}, bf16[112,1536]{1,0:T(8,128)(2,1)S(1)}, u32[]{:S(2)}, u32[]{:S(2)}) %collective-permute-start.37) | collective-permute-done | bytes 344096 | tf_op jit(solution)/shard_map/ppermute | solution.py:436
  358.4 11.4 %collective-permute-done.39 = bf16[112,1536]{1,0:T(8,128)(2,1)S(1)} collective-permute-done((bf16[112,1536]{1,0:T(8,128)(2,1)S(1)}, bf16[112,1536]{1,0:T(8,128)(2,1)S(1)}, u32[]{:S(2)}, u32[]{:S(2)}) %collective-permute-start.39) | collective-permute-done | bytes 344096 | tf_op jit(solution)/shard_map/ppermute | solution.py:436
  388.7 11.4 %collective-permute-done.43 = bf16[256,1536]{1,0:T(8,128)(2,1)S(1)} collective-permute-done((bf16[256,1536]{1,0:T(8,128)(2,1)S(1)}, bf16[256,1536]{1,0:T(8,128)(2,1)S(1)}, u32[]{:S(2)}, u32[]{:S(2)}) %collective-permute-start.43) | collective-permute-done | bytes 786464 | tf_op jit(solution)/shard_map/ppermute | solution.py:432
  418.0 6.5 collective-permute-done.45
  425.3 11.4 %collective-permute-done.46 = bf16[256,1536]{1,0:T(8,128)(2,1)S(1)} collective-permute-done((bf16[256,1536]{1,0:T(8,128)(2,1)S(1)}, bf16[256,1536]{1,0:T(8,128)(2,1)S(1)}, u32[]{:S(2)}, u32[]{:S(2)}) %collective-permute-start.46) | collective-permute-done | bytes 786464 | tf_op jit(solution)/shard_map/ppermute | solution.py:432
  442.7 5.3 multiply_convert_fusion.1
  467.7 6.2 collective-permute-done.49
  475.7 8.9 %collective-permute-done.52 = bf16[112,1536]{1,0:T(8,128)(2,1)S(1)} collective-permute-done((bf16[112,1536]{1,0:T(8,128)(2,1)S(1)}, bf16[112,1536]{1,0:T(8,128)(2,1)S(1)}, u32[]{:S(2)}, u32[]{:S(2)}) %collective-permute-start.52) | collective-permute-done | bytes 344096 | tf_op jit(solution)/shard_map/ppermute | solution.py:436
  487.3 7.4 attend_back.3
  497.8 7.7 attend_back.4
  525.4 8.2 collective-permute-done.76
  547.2 6.0 collective-permute-done.78
  558.2 5.5 collective-permute-start.65
  580.3 5.5 multiply_convert_fusion
  592.0 5.1 collective-permute-start.70
  601.7 7.0 collective-permute-done.74
  625.7 11.1 %collective-permute-done.71 = bf16[112,1536]{1,0:T(8,128)(2,1)S(1)} collective-permute-done((bf16[112,1536]{1,0:T(8,128)(2,1)S(1)}, bf16[112,1536]{1,0:T(8,128)(2,1)S(1)}, u32[]{:S(2)}, u32[]{:S(2)}) %collective-permute-start.71) | collective-permute-done | bytes 344096 | tf_op jit(solution)/shard_map/ppermute | solution.py:436
  647.6 7.4 attend_back.5
  665.6 11.4 %collective-permute-done.87 = bf16[112,1536]{1,0:T(8,128)(2,1)S(1)} collective-permute-done((bf16[112,1536]{1,0:T(8,128)(2,1)S(1)}, bf16[112,1536]{1,0:T(8,128)(2,1)S(1)}, u32[]{:S(2)}, u32[]{:S(2)}) %collective-permute-start.87) | collective-permute-done | bytes 344096 | tf_op jit(solution)/shard_map/ppermute | solution.py:436
  677.0 6.0 collective-permute-done.88
  689.5 7.4 collective-permute-done.91
  697.4 5.4 collective-permute-done.92
  707.9 9.3 %collective-permute-done.100 = bf16[4,48,768]{2,1,0:T(8,128)(2,1)S(1)} collective-permute-done((bf16[4,48,768]{2,1,0:T(8,128)(2,1)S(1)}, bf16[4,48,768]{2,1,0:T(8,128)(2,1)S(1)}, u32[]{:S(2)}, u32[]{:S(2)}) %collective-permute-start.100) | collective-permute-done | bytes 294944 | tf_op jit(solution)/shard_map/ppermute | solution.py:432
  733.9 10.4 %collective-permute-done.95 = bf16[112,1536]{1,0:T(8,128)(2,1)S(1)} collective-permute-done((bf16[112,1536]{1,0:T(8,128)(2,1)S(1)}, bf16[112,1536]{1,0:T(8,128)(2,1)S(1)}, u32[]{:S(2)}, u32[]{:S(2)}) %collective-permute-start.95) | collective-permute-done | bytes 344096 | tf_op jit(solution)/shard_map/ppermute | solution.py:436
  744.4 6.4 collective-permute-done.96
  753.1 9.7 %collective-permute-done.97 = bf16[5,96,768]{2,1,0:T(8,128)(2,1)S(1)} collective-permute-done((bf16[5,96,768]{2,1,0:T(8,128)(2,1)S(1)}, bf16[5,96,768]{2,1,0:T(8,128)(2,1)S(1)}, u32[]{:S(2)}, u32[]{:S(2)}) %collective-permute-start.97) | collective-permute-done | bytes 737312 | tf_op jit(solution)/shard_map/ppermute | solution.py:432
  768.9 5.5 collective-permute-done.98
  809.0 16.8 %finish.1 = (f32[6,1288,128]{2,1,0:T(8,128)}, f32[6,1288,128]{2,1,0:T(8,128)}, f32[6,1288,128]{2,1,0:T(8,128)}, f32[12,24,736]{2,1,0:T(8,128)}, f32[12,24,736]{2...) custom-call(f32[2]{0:T(128)} %pad_maximum_fusion.47.scal_ref, ...), custom_call_target="tpu_custom_call" | custom-call | tf_op jit(solution)/shard_map/finish/pallas_call | solution.py:187
  (1054 shorter events, 356.1 us)
Async XLA Ops:
  7.2 87.2 %all-gather.5.cloned.1.call-start = ((), (), s32[]{:S(2)}) async-start(), calls=%async_computation | async-start | bytes 6082560 | tf_op jit(solution)/shard_map/all_gather | solution.py:600
  17.1 246.2 %all-gather.7.cloned.1.call-start = ((), (), s32[]{:S(2)}) async-start(), calls=%async_computation.1 | async-start | bytes 10948608 | tf_op jit(solution)/shard_map/all_gather | solution.py:600
  39.0 60.4 %collective-permute-start.2 = (bf16[112,1536]{1,0:T(8,128)(2,1)S(1)}, bf16[112,1536]{1,0:T(8,128)(2,1)S(1)}, u32[]{:S(2)}, u32[]{:S(2)}) collective-permute-start(bf16[112,1536]{1,0:T(8,128)(2,1)S(1)} %get-tuple-element.303), channel_id=1, source_target_pairs={{0,4},{4,8},{8,12},{12,0},{1,5},{5,9},{9,13},{13,1},{2,6},{6,10},{... | collective-permute-start | bytes 1032200 | tf_op jit(solution)/shard_map/ppermute | solution.py:436
  40.5 58.9 %collective-permute-start.3 = (bf16[112,1536]{1,0:T(8,128)(2,1)S(1)}, bf16[112,1536]{1,0:T(8,128)(2,1)S(1)}, u32[]{:S(2)}, u32[]{:S(2)}) collective-permute-start(bf16[112,1536]{1,0:T(8,128)(2,1)S(1)} %get-tuple-element.304), channel_id=1, source_target_pairs={{0,4},{4,8},{8,12},{12,0},{1,5},{5,9},{9,13},{13,1},{2,6},{6,10},{... | collective-permute-start | bytes 1032200 | tf_op jit(solution)/shard_map/ppermute | solution.py:436
  112.7 20.8 %collective-permute-start.5 = (bf16[256,768]{1,0:T(8,128)(2,1)S(1)}, bf16[256,768]{1,0:T(8,128)(2,1)S(1)}, u32[]{:S(2)}, u32[]{:S(2)}) collective-permute-start(bf16[256,768]{1,0:T(8,128)(2,1)S(1)} %pad_maximum_fusion.35), channel_id=1, source_target_pairs={{0,1},{1,0},{2,3},{3,2},{4,5},{5,4},{6,7},{7,6},{8,9},{9,8},{10,11... | collective-permute-start | bytes 1179656 | tf_op jit(solution)/shard_map/ppermute | solution.py:432
  116.5 17.0 %collective-permute-start.7 = (bf16[112,1536]{1,0:T(8,128)(2,1)S(1)}, bf16[112,1536]{1,0:T(8,128)(2,1)S(1)}, u32[]{:S(2)}, u32[]{:S(2)}) collective-permute-start(bf16[112,1536]{1,0:T(8,128)(2,1)S(1)} %copy-done.212), channel_id=1, source_target_pairs={{0,4},{4,8},{8,12},{12,0},{1,5},{5,9},{9,13},{13,1},{2,6},{6,10},{... | collective-permute-start | bytes 1032200 | tf_op jit(solution)/shard_map/ppermute | solution.py:436
  133.6 34.0 %collective-permute-start.8 = (bf16[512,768]{1,0:T(8,128)(2,1)S(1)}, bf16[512,768]{1,0:T(8,128)(2,1)S(1)}, u32[]{:S(2)}, u32[]{:S(2)}) collective-permute-start(bf16[512,768]{1,0:T(8,128)(2,1)S(1)} %pad_maximum_fusion.22), channel_id=1, source_target_pairs={{0,2},{1,3},{2,0},{3,1},{4,6},{5,7},{6,4},{7,5},{8,10},{9,11},{10,... | collective-permute-start | bytes 2359304 | tf_op jit(solution)/shard_map/ppermute | solution.py:432
  134.8 20.2 %collective-permute-start.9 = (bf16[112,1536]{1,0:T(8,128)(2,1)S(1)}, bf16[112,1536]{1,0:T(8,128)(2,1)S(1)}, u32[]{:S(2)}, u32[]{:S(2)}) collective-permute-start(bf16[112,1536]{1,0:T(8,128)(2,1)S(1)} %copy-done.216), channel_id=1, source_target_pairs={{0,4},{4,8},{8,12},{12,0},{1,5},{5,9},{9,13},{13,1},{2,6},{6,10},{... | collective-permute-start | bytes 1032200 | tf_op jit(solution)/shard_map/ppermute | solution.py:436
  135.0 31.9 %collective-permute-start.10 = (bf16[112,1536]{1,0:T(8,128)(2,1)S(1)}, bf16[112,1536]{1,0:T(8,128)(2,1)S(1)}, u32[]{:S(2)}, u32[]{:S(2)}) collective-permute-start(bf16[112,1536]{1,0:T(8,128)(2,1)S(1)} %collective-permute-done.7), channel_id=1, source_target_pairs={{0,4},{4,8},{8,12},{12,0},{1,5},{5,9},{9,13},{13,1},{2,6},{6,10},{... | collective-permute-start | bytes 1032200 | tf_op jit(solution)/shard_map/ppermute | solution.py:436
  184.3 17.1 %collective-permute-start.12 = (bf16[128,1536]{1,0:T(8,128)(2,1)S(1)}, bf16[128,1536]{1,0:T(8,128)(2,1)S(1)}, u32[]{:S(2)}, u32[]{:S(2)}) collective-permute-start(bf16[128,1536]{1,0:T(8,128)(2,1)S(1)} %multiply_convert_fusion.9), channel_id=1, source_target_pairs={{0,1},{1,0},{2,3},{3,2},{4,5},{5,4},{6,7},{7,6},{8,9},{9,8},{10,11... | collective-permute-start | bytes 1179656 | tf_op jit(solution)/shard_map/ppermute | solution.py:432
  185.5 15.8 %collective-permute-start.13 = (bf16[112,1536]{1,0:T(8,128)(2,1)S(1)}, bf16[112,1536]{1,0:T(8,128)(2,1)S(1)}, u32[]{:S(2)}, u32[]{:S(2)}) collective-permute-start(bf16[112,1536]{1,0:T(8,128)(2,1)S(1)} %copy-done.229), channel_id=1, source_target_pairs={{0,4},{4,8},{8,12},{12,0},{1,5},{5,9},{9,13},{13,1},{2,6},{6,10},{... | collective-permute-start | bytes 1032200 | tf_op jit(solution)/shard_map/ppermute | solution.py:436
  201.4 16.1 %collective-permute-start.14 = (bf16[256,1536]{1,0:T(8,128)(2,1)S(1)}, bf16[256,1536]{1,0:T(8,128)(2,1)S(1)}, u32[]{:S(2)}, u32[]{:S(2)}) collective-permute-start(bf16[256,1536]{1,0:T(8,128)(2,1)S(1)} %pad_maximum_fusion.23), channel_id=1, source_target_pairs={{0,2},{1,3},{2,0},{3,1},{4,6},{5,7},{6,4},{7,5},{8,10},{9,11},{10,... | collective-permute-start | bytes 2359304 | tf_op jit(solution)/shard_map/ppermute | solution.py:432
  203.2 14.3 %collective-permute-start.15 = (bf16[112,1536]{1,0:T(8,128)(2,1)S(1)}, bf16[112,1536]{1,0:T(8,128)(2,1)S(1)}, u32[]{:S(2)}, u32[]{:S(2)}) collective-permute-start(bf16[112,1536]{1,0:T(8,128)(2,1)S(1)} %copy-done.226), channel_id=1, source_target_pairs={{0,4},{4,8},{8,12},{12,0},{1,5},{5,9},{9,13},{13,1},{2,6},{6,10},{... | collective-permute-start | bytes 1032200 | tf_op jit(solution)/shard_map/ppermute | solution.py:436
  238.2 15.1 %collective-permute-start.19 = (bf16[256,1536]{1,0:T(8,128)(2,1)S(1)}, bf16[256,1536]{1,0:T(8,128)(2,1)S(1)}, u32[]{:S(2)}, u32[]{:S(2)}) collective-permute-start(bf16[256,1536]{1,0:T(8,128)(2,1)S(1)} %slice.1647), channel_id=1, source_target_pairs={{0,2},{1,3},{2,0},{3,1},{4,6},{5,7},{6,4},{7,5},{8,10},{9,11},{10,... | collective-permute-start | bytes 2359304 | tf_op jit(solution)/shard_map/ppermute | solution.py:432
  240.5 20.0 %collective-permute-start.23 = (bf16[112,1536]{1,0:T(8,128)(2,1)S(1)}, bf16[112,1536]{1,0:T(8,128)(2,1)}, u32[]{:S(2)}, u32[]{:S(2)}) collective-permute-start(bf16[112,1536]{1,0:T(8,128)(2,1)S(1)} %get-tuple-element.301), channel_id=1, source_target_pairs={{0,4},{4,8},{8,12},{12,0},{1,5},{5,9},{9,13},{13,1},{2,6},{6,10},{... | collective-permute-start | bytes 1032200 | tf_op jit(solution)/shard_map/ppermute | solution.py:436
  255.5 24.3 %collective-permute-start.26 = (bf16[112,1536]{1,0:T(8,128)(2,1)}, bf16[112,1536]{1,0:T(8,128)(2,1)}, u32[]{:S(2)}, u32[]{:S(2)}) collective-permute-start(bf16[112,1536]{1,0:T(8,128)(2,1)} %collective-permute-done.21), channel_id=1, source_target_pairs={{0,4},{4,8},{8,12},{12,0},{1,5},{5,9},{9,13},{13,1},{2,6},{6,10},{... | collective-permute-start | bytes 1032200 | tf_op jit(solution)/shard_map/ppermute | solution.py:436
  261.5 34.9 %collective-permute-start.28 = (bf16[112,1536]{1,0:T(8,128)(2,1)}, bf16[112,1536]{1,0:T(8,128)(2,1)}, u32[]{:S(2)}, u32[]{:S(2)}) collective-permute-start(bf16[112,1536]{1,0:T(8,128)(2,1)} %collective-permute-done.23), channel_id=1, source_target_pairs={{0,4},{4,8},{8,12},{12,0},{1,5},{5,9},{9,13},{13,1},{2,6},{6,10},{... | collective-permute-start | bytes 1032200 | tf_op jit(solution)/shard_map/ppermute | solution.py:436
  286.4 15.2 %collective-permute-start.27 = (bf16[512,768]{1,0:T(8,128)(2,1)S(1)}, bf16[512,768]{1,0:T(8,128)(2,1)S(1)}, u32[]{:S(2)}, u32[]{:S(2)}) collective-permute-start(bf16[512,768]{1,0:T(8,128)(2,1)S(1)} %pad_maximum_fusion.25), channel_id=1, source_target_pairs={{0,2},{1,3},{2,0},{3,1},{4,6},{5,7},{6,4},{7,5},{8,10},{9,11},{10,... | collective-permute-start | bytes 2359304 | tf_op jit(solution)/shard_map/ppermute | solution.py:432
  303.1 25.1 %collective-permute-start.29 = (bf16[1024,768]{1,0:T(8,128)(2,1)}, bf16[1024,768]{1,0:T(8,128)(2,1)}, u32[]{:S(2)}, u32[]{:S(2)}) collective-permute-start(bf16[1024,768]{1,0:T(8,128)(2,1)} %pad_maximum_fusion.10), channel_id=1, source_target_pairs={{0,16},{16,0},{1,17},{17,1},{2,18},{18,2},{3,19},{19,3},{4,20},{20... | collective-permute-start | bytes 4718600 | tf_op jit(solution)/shard_map/ppermute | solution.py:424
  310.6 16.1 %collective-permute-start.33 = (bf16[512,768]{1,0:T(8,128)(2,1)S(1)}, bf16[512,768]{1,0:T(8,128)(2,1)S(1)}, u32[]{:S(2)}, u32[]{:S(2)}) collective-permute-start(bf16[512,768]{1,0:T(8,128)(2,1)S(1)} %pad_maximum_fusion.26), channel_id=1, source_target_pairs={{0,2},{1,3},{2,0},{3,1},{4,6},{5,7},{6,4},{7,5},{8,10},{9,11},{10,... | collective-permute-start | bytes 2359304 | tf_op jit(solution)/shard_map/ppermute | solution.py:432
  466.3 68.4 %collective-permute-start.58 = (bf16[112,1536]{1,0:T(8,128)(2,1)S(1)}, bf16[112,1536]{1,0:T(8,128)(2,1)S(1)}, u32[]{:S(2)}, u32[]{:S(2)}) collective-permute-start(bf16[112,1536]{1,0:T(8,128)(2,1)S(1)} %slice.1168), channel_id=1, source_target_pairs={{0,12},{4,0},{8,4},{12,8},{1,13},{5,1},{9,5},{13,9},{2,14},{6,2},{... | collective-permute-start | bytes 1032200 | tf_op jit(solution)/shard_map/ppermute | solution.py:436
  466.3 18.3 %collective-permute-start.52 = (bf16[112,1536]{1,0:T(8,128)(2,1)S(1)}, bf16[112,1536]{1,0:T(8,128)(2,1)S(1)}, u32[]{:S(2)}, u32[]{:S(2)}) collective-permute-start(bf16[112,1536]{1,0:T(8,128)(2,1)S(1)} %slice.1159), channel_id=1, source_target_pairs={{0,12},{4,0},{8,4},{12,8},{1,13},{5,1},{9,5},{13,9},{2,14},{6,2},{... | collective-permute-start | bytes 1032200 | tf_op jit(solution)/shard_map/ppermute | solution.py:436
  475.7 36.5 %collective-permute-start.55 = (bf16[112,1536]{1,0:T(8,128)(2,1)S(1)}, bf16[112,1536]{1,0:T(8,128)(2,1)S(1)}, u32[]{:S(2)}, u32[]{:S(2)}) collective-permute-start(bf16[112,1536]{1,0:T(8,128)(2,1)S(1)} %add_convert_fusion.13), channel_id=1, source_target_pairs={{0,12},{4,0},{8,4},{12,8},{1,13},{5,1},{9,5},{13,9},{2,14},{6,2},{... | collective-permute-start | bytes 1032200 | tf_op jit(solution)/shard_map/ppermute | solution.py:436
  511.3 22.4 %collective-permute-start.76 = (bf16[512,768]{1,0:T(8,128)(2,1)S(1)}, bf16[512,768]{1,0:T(8,128)(2,1)S(1)}, u32[]{:S(2)}, u32[]{:S(2)}) collective-permute-start(bf16[512,768]{1,0:T(8,128)(2,1)S(1)} %slice.1642), channel_id=1, source_target_pairs={{0,2},{1,3},{2,0},{3,1},{4,6},{5,7},{6,4},{7,5},{8,10},{9,11},{10,... | collective-permute-start | bytes 2359304 | tf_op jit(solution)/shard_map/ppermute | solution.py:432
  521.1 13.5 %collective-permute-start.59 = (bf16[112,1536]{1,0:T(8,128)(2,1)S(1)}, bf16[112,1536]{1,0:T(8,128)(2,1)S(1)}, u32[]{:S(2)}, u32[]{:S(2)}) collective-permute-start(bf16[112,1536]{1,0:T(8,128)(2,1)S(1)} %add_convert_fusion.11), channel_id=1, source_target_pairs={{0,12},{4,0},{8,4},{12,8},{1,13},{5,1},{9,5},{13,9},{2,14},{6,2},{... | collective-permute-start | bytes 1032200 | tf_op jit(solution)/shard_map/ppermute | solution.py:436
  522.9 33.6 %collective-permute-start.62 = (bf16[112,1536]{1,0:T(8,128)(2,1)S(1)}, bf16[112,1536]{1,0:T(8,128)(2,1)S(1)}, u32[]{:S(2)}, u32[]{:S(2)}) collective-permute-start(bf16[112,1536]{1,0:T(8,128)(2,1)S(1)} %add_convert_fusion.10), channel_id=1, source_target_pairs={{0,12},{4,0},{8,4},{12,8},{1,13},{5,1},{9,5},{13,9},{2,14},{6,2},{... | collective-permute-start | bytes 1032200 | tf_op jit(solution)/shard_map/ppermute | solution.py:436
  535.3 21.2 %collective-permute-start.63 = (bf16[112,1536]{1,0:T(8,128)(2,1)S(1)}, bf16[112,1536]{1,0:T(8,128)(2,1)S(1)}, u32[]{:S(2)}, u32[]{:S(2)}) collective-permute-start(bf16[112,1536]{1,0:T(8,128)(2,1)S(1)} %add_convert_fusion.9), channel_id=1, source_target_pairs={{0,12},{4,0},{8,4},{12,8},{1,13},{5,1},{9,5},{13,9},{2,14},{6,2},{... | collective-permute-start | bytes 1032200 | tf_op jit(solution)/shard_map/ppermute | solution.py:436
  554.6 20.6 %collective-permute-start.79 = (bf16[4,384,768]{2,1,0:T(8,128)(2,1)S(1)}, bf16[4,384,768]{2,1,0:T(8,128)(2,1)S(1)}, u32[]{:S(2)}, u32[]{:S(2)}) collective-permute-start(bf16[4,384,768]{2,1,0:T(8,128)(2,1)S(1)} %convolution_convert_fusion.12), channel_id=1, source_target_pairs={{0,16},{16,0},{1,17},{17,1},{2,18},{18,2},{3,19},{19,3},{4,20},{20... | collective-permute-start | bytes 7077896 | tf_op jit(solution)/shard_map/ppermute | solution.py:424
  555.6 22.1 %collective-permute-start.67 = (bf16[5,384,768]{2,1,0:T(8,128)(2,1)S(1)}, bf16[5,384,768]{2,1,0:T(8,128)(2,1)S(1)}, u32[]{:S(2)}, u32[]{:S(2)}) collective-permute-start(bf16[5,384,768]{2,1,0:T(8,128)(2,1)S(1)} %convolution_convert_fusion.11), channel_id=1, source_target_pairs={{0,16},{16,0},{1,17},{17,1},{2,18},{18,2},{3,19},{19,3},{4,20},{20... | collective-permute-start | bytes 8847368 | tf_op jit(solution)/shard_map/ppermute | solution.py:424
  576.6 44.3 %collective-permute-start.81 = (bf16[4,192,768]{2,1,0:T(8,128)(2,1)S(1)}, bf16[4,192,768]{2,1,0:T(8,128)(2,1)S(1)}, u32[]{:S(2)}, u32[]{:S(2)}) collective-permute-start(bf16[4,192,768]{2,1,0:T(8,128)(2,1)S(1)} %slice.1640), channel_id=1, source_target_pairs={{0,1},{1,0},{2,3},{3,2},{4,5},{5,4},{6,7},{7,6},{8,9},{9,8},{10,11... | collective-permute-start | bytes 3538952 | tf_op jit(solution)/shard_map/ppermute | solution.py:432
  578.9 29.8 %collective-permute-start.74 = (bf16[5,192,768]{2,1,0:T(8,128)(2,1)S(1)}, bf16[5,192,768]{2,1,0:T(8,128)(2,1)S(1)}, u32[]{:S(2)}, u32[]{:S(2)}) collective-permute-start(bf16[5,192,768]{2,1,0:T(8,128)(2,1)S(1)} %slice.1639), channel_id=1, source_target_pairs={{0,1},{1,0},{2,3},{3,2},{4,5},{5,4},{6,7},{7,6},{8,9},{9,8},{10,11... | collective-permute-start | bytes 4423688 | tf_op jit(solution)/shard_map/ppermute | solution.py:432
  590.0 20.6 %collective-permute-start.68 = (bf16[512,1536]{1,0:T(8,128)(2,1)}, bf16[512,1536]{1,0:T(8,128)(2,1)S(1)}, u32[]{:S(2)}, u32[]{:S(2)}) collective-permute-start(bf16[512,1536]{1,0:T(8,128)(2,1)} %fusion.1), channel_id=1, source_target_pairs={{0,16},{16,0},{1,17},{17,1},{2,18},{18,2},{3,19},{19,3},{4,20},{20... | collective-permute-start | bytes 4718600 | tf_op jit(solution)/shard_map/ppermute | solution.py:424
  592.0 31.7 %collective-permute-start.70 = (bf16[112,1536]{1,0:T(8,128)(2,1)S(1)}, bf16[112,1536]{1,0:T(8,128)(2,1)S(1)}, u32[]{:S(2)}, u32[]{:S(2)}) collective-permute-start(bf16[112,1536]{1,0:T(8,128)(2,1)S(1)} %slice.1183), channel_id=1, source_target_pairs={{0,12},{4,0},{8,4},{12,8},{1,13},{5,1},{9,5},{13,9},{2,14},{6,2},{... | collective-permute-start | bytes 1032200 | tf_op jit(solution)/shard_map/ppermute | solution.py:436
  613.7 23.1 %collective-permute-start.69 = (bf16[256,1536]{1,0:T(8,128)(2,1)S(1)}, bf16[256,1536]{1,0:T(8,128)(2,1)S(1)}, u32[]{:S(2)}, u32[]{:S(2)}) collective-permute-start(bf16[256,1536]{1,0:T(8,128)(2,1)S(1)} %slice.1643), channel_id=1, source_target_pairs={{0,2},{1,3},{2,0},{3,1},{4,6},{5,7},{6,4},{7,5},{8,10},{9,11},{10,... | collective-permute-start | bytes 2359304 | tf_op jit(solution)/shard_map/ppermute | solution.py:432
  616.2 26.4 %collective-permute-start.73 = (bf16[112,1536]{1,0:T(8,128)(2,1)S(1)}, bf16[112,1536]{1,0:T(8,128)(2,1)S(1)}, u32[]{:S(2)}, u32[]{:S(2)}) collective-permute-start(bf16[112,1536]{1,0:T(8,128)(2,1)S(1)} %slice.1188), channel_id=1, source_target_pairs={{0,12},{4,0},{8,4},{12,8},{1,13},{5,1},{9,5},{13,9},{2,14},{6,2},{... | collective-permute-start | bytes 1032200 | tf_op jit(solution)/shard_map/ppermute | solution.py:436
  620.9 15.9 %collective-permute-start.71 = (bf16[112,1536]{1,0:T(8,128)(2,1)S(1)}, bf16[112,1536]{1,0:T(8,128)(2,1)S(1)}, u32[]{:S(2)}, u32[]{:S(2)}) collective-permute-start(bf16[112,1536]{1,0:T(8,128)(2,1)S(1)} %slice.1184), channel_id=1, source_target_pairs={{0,12},{4,0},{8,4},{12,8},{1,13},{5,1},{9,5},{13,9},{2,14},{6,2},{... | collective-permute-start | bytes 1032200 | tf_op jit(solution)/shard_map/ppermute | solution.py:436
  621.5 16.9 %collective-permute-start.83 = (bf16[4,96,768]{2,1,0:T(8,128)(2,1)S(1)}, bf16[4,96,768]{2,1,0:T(8,128)(2,1)S(1)}, u32[]{:S(2)}, u32[]{:S(2)}) collective-permute-start(bf16[4,96,768]{2,1,0:T(8,128)(2,1)S(1)} %slice.1650), channel_id=1, source_target_pairs={{0,2},{1,3},{2,0},{3,1},{4,6},{5,7},{6,4},{7,5},{8,10},{9,11},{10,... | collective-permute-start | bytes 1769480 | tf_op jit(solution)/shard_map/ppermute | solution.py:432
  623.7 18.9 %collective-permute-start.82 = (bf16[5,48,768]{2,1,0:T(8,128)(2,1)S(1)}, bf16[5,48,768]{2,1,0:T(8,128)(2,1)S(1)}, u32[]{:S(2)}, u32[]{:S(2)}) collective-permute-start(bf16[5,48,768]{2,1,0:T(8,128)(2,1)S(1)} %slice.1655), channel_id=1, source_target_pairs={{0,4},{1,5},{2,6},{3,7},{4,0},{5,1},{6,2},{7,3},{8,12},{9,13},{10,... | collective-permute-start | bytes 1105928 | tf_op jit(solution)/shard_map/ppermute | solution.py:432
  656.8 32.7 %collective-permute-start.90 = (bf16[112,1536]{1,0:T(8,128)(2,1)S(1)}, bf16[112,1536]{1,0:T(8,128)(2,1)S(1)}, u32[]{:S(2)}, u32[]{:S(2)}) collective-permute-start(bf16[112,1536]{1,0:T(8,128)(2,1)S(1)} %add_convert_fusion.5), channel_id=1, source_target_pairs={{0,12},{4,0},{8,4},{12,8},{1,13},{5,1},{9,5},{13,9},{2,14},{6,2},{... | collective-permute-start | bytes 1032200 | tf_op jit(solution)/shard_map/ppermute | solution.py:436
  661.2 15.8 %collective-permute-start.87 = (bf16[112,1536]{1,0:T(8,128)(2,1)S(1)}, bf16[112,1536]{1,0:T(8,128)(2,1)S(1)}, u32[]{:S(2)}, u32[]{:S(2)}) collective-permute-start(bf16[112,1536]{1,0:T(8,128)(2,1)S(1)} %add_convert_fusion.7), channel_id=1, source_target_pairs={{0,12},{4,0},{8,4},{12,8},{1,13},{5,1},{9,5},{13,9},{2,14},{6,2},{... | collective-permute-start | bytes 1032200 | tf_op jit(solution)/shard_map/ppermute | solution.py:436
  661.7 21.3 %collective-permute-start.86 = (bf16[512,768]{1,0:T(8,128)(2,1)S(1)}, bf16[512,768]{1,0:T(8,128)(2,1)S(1)}, u32[]{:S(2)}, u32[]{:S(2)}) collective-permute-start(bf16[512,768]{1,0:T(8,128)(2,1)S(1)} %slice.1641), channel_id=1, source_target_pairs={{0,2},{1,3},{2,0},{3,1},{4,6},{5,7},{6,4},{7,5},{8,10},{9,11},{10,... | collective-permute-start | bytes 2359304 | tf_op jit(solution)/shard_map/ppermute | solution.py:432
  663.8 19.3 %collective-permute-start.88 = (bf16[112,1536]{1,0:T(8,128)(2,1)S(1)}, bf16[112,1536]{1,0:T(8,128)(2,1)S(1)}, u32[]{:S(2)}, u32[]{:S(2)}) collective-permute-start(bf16[112,1536]{1,0:T(8,128)(2,1)S(1)} %add_convert_fusion.6), channel_id=1, source_target_pairs={{0,12},{4,0},{8,4},{12,8},{1,13},{5,1},{9,5},{13,9},{2,14},{6,2},{... | collective-permute-start | bytes 1032200 | tf_op jit(solution)/shard_map/ppermute | solution.py:436
  683.2 13.6 %collective-permute-start.89 = (bf16[256,768]{1,0:T(8,128)(2,1)S(1)}, bf16[256,768]{1,0:T(8,128)(2,1)S(1)}, u32[]{:S(2)}, u32[]{:S(2)}) collective-permute-start(bf16[256,768]{1,0:T(8,128)(2,1)S(1)} %slice.1651), channel_id=1, source_target_pairs={{0,1},{1,0},{2,3},{3,2},{4,5},{5,4},{6,7},{7,6},{8,9},{9,8},{10,11... | collective-permute-start | bytes 1179656 | tf_op jit(solution)/shard_map/ppermute | solution.py:432
  707.6 13.6 %collective-permute-start.93 = (bf16[5,384,768]{2,1,0:T(8,128)(2,1)S(1)}, bf16[5,384,768]{2,1,0:T(8,128)(2,1)S(1)}, u32[]{:S(2)}, u32[]{:S(2)}) collective-permute-start(bf16[5,384,768]{2,1,0:T(8,128)(2,1)S(1)} %convolution_convert_fusion.10), channel_id=1, source_target_pairs={{0,16},{16,0},{1,17},{17,1},{2,18},{18,2},{3,19},{19,3},{4,20},{20... | collective-permute-start | bytes 8847368 | tf_op jit(solution)/shard_map/ppermute | solution.py:424
  722.4 28.4 %collective-permute-start.94 = (bf16[5,192,768]{2,1,0:T(8,128)(2,1)S(1)}, bf16[5,192,768]{2,1,0:T(8,128)(2,1)S(1)}, u32[]{:S(2)}, u32[]{:S(2)}) collective-permute-start(bf16[5,192,768]{2,1,0:T(8,128)(2,1)S(1)} %slice.1638), channel_id=1, source_target_pairs={{0,1},{1,0},{2,3},{3,2},{4,5},{5,4},{6,7},{7,6},{8,9},{9,8},{10,11... | collective-permute-start | bytes 4423688 | tf_op jit(solution)/shard_map/ppermute | solution.py:432
  728.9 38.6 %collective-permute-start.102 = (bf16[5,24,768]{2,1,0:T(8,128)(2,1)S(1)}, bf16[5,24,768]{2,1,0:T(8,128)(2,1)S(1)}, u32[]{:S(2)}, u32[]{:S(2)}) collective-permute-start(bf16[5,24,768]{2,1,0:T(8,128)(2,1)S(1)} %slice.1660), channel_id=1, source_target_pairs={{0,8},{1,9},{2,10},{3,11},{4,12},{5,13},{6,14},{7,15},{8,0},{9,1},... | collective-permute-start | bytes 552968 | tf_op jit(solution)/shard_map/ppermute | solution.py:432
  729.1 15.3 %collective-permute-start.95 = (bf16[112,1536]{1,0:T(8,128)(2,1)S(1)}, bf16[112,1536]{1,0:T(8,128)(2,1)S(1)}, u32[]{:S(2)}, u32[]{:S(2)}) collective-permute-start(bf16[112,1536]{1,0:T(8,128)(2,1)S(1)} %add_convert_fusion.3), channel_id=1, source_target_pairs={{0,12},{4,0},{8,4},{12,8},{1,13},{5,1},{9,5},{13,9},{2,14},{6,2},{... | collective-permute-start | bytes 1032200 | tf_op jit(solution)/shard_map/ppermute | solution.py:436
  732.7 18.1 %collective-permute-start.96 = (bf16[112,1536]{1,0:T(8,128)(2,1)S(1)}, bf16[112,1536]{1,0:T(8,128)(2,1)S(1)}, u32[]{:S(2)}, u32[]{:S(2)}) collective-permute-start(bf16[112,1536]{1,0:T(8,128)(2,1)S(1)} %add_convert_fusion.2), channel_id=1, source_target_pairs={{0,12},{4,0},{8,4},{12,8},{1,13},{5,1},{9,5},{13,9},{2,14},{6,2},{... | collective-permute-start | bytes 1032200 | tf_op jit(solution)/shard_map/ppermute | solution.py:436
  (320 other events, 2751.9 us)
Sparse Core Ops, SparseCore 0:
  17.2 77.1 all-gather.4
  97.3 118.3 all-gather.6
